TPU v7x, 32 devices: a whole 2x2x4 slice. The times are simulated.
32 devices in a mesh: ctx: 8 (over z, y), fsdp: 4 (over x, core).
Axes of the slice: x: 2, y: 2, z: 4, core: 2. Of those that a mesh axis runs over, the one named last changes fastest.
Arguments:
- inputs: bfloat16 [8, 2048, 768], P('fsdp', 'ctx'), may hold values from -6 to 6
- earlier: bfloat16 [4, 8, 2048, 768], P(None, 'fsdp', 'ctx'), may hold values from -6 to 6
- input_proj: bfloat16 [768, 2304], P('fsdp'), may hold values from -0.21875 to 0.21875
- output_proj: bfloat16 [768, 768], P('fsdp'), may hold values from -6 to 6
- up_proj: bfloat16 [768, 3072], P('fsdp'), may hold values from -0.21875 to 0.21875
- down_proj: bfloat16 [3072, 768], P('fsdp'), may hold values from -0.109375 to 0.109375
- norm1_gain: float32 [768], P('fsdp'), may hold values from 0.5 to 1.5
- norm1_bias: float32 [768], P('fsdp'), may hold values from -1.75 to 1.75
- norm2_gain: float32 [768], P('fsdp'), may hold values from 0.5 to 1.5
- norm2_bias: float32 [768], P('fsdp'), may hold values from -1.75 to 1.75
- mixing: float32 [5], replicated, may hold values from 0.3 to 1
- block_order: int32 [2, 8], replicated, may hold values from 0 to 7, each once within a row
- grad_next: bfloat16 [8, 2048, 768], P('fsdp', 'ctx'), may hold values from -6 to 6
Outputs:
- next_input: bfloat16 [8, 2048, 768], P('fsdp', 'ctx')
- grad_input: bfloat16 [8, 2048, 768], P('fsdp', 'ctx')
- grad_earlier: bfloat16 [4, 8, 2048, 768], P(None, 'fsdp', 'ctx')
- grad_input_proj: float32 [768, 2304], P('fsdp')
- grad_output_proj: float32 [768, 768], P('fsdp')
- grad_up_proj: float32 [768, 3072], P('fsdp')
- grad_down_proj: float32 [3072, 768], P('fsdp')
- grad_norm1_gain: float32 [768], P('fsdp')
- grad_norm1_bias: float32 [768], P('fsdp')
- grad_norm2_gain: float32 [768], P('fsdp')
- grad_norm2_bias: float32 [768], P('fsdp')
- grad_mixing: float32 [5], replicated
Inputs may be any that keep to these rules, and one draw needn't show every extreme that they name: `block_order`: each row is an ordering of the 8 blocks of a sequence: entry c names the block held at index c of ctx, each block once.
All inputs are finite; a program needn't handle non-finite values.
Results may differ from a plain program's by a relative error of at most 0.034.
Values may be sent and summed in bfloat16 or wider, within the bound.
No kernel may reach another device: no remote copies, remote signals or barrier semaphores. Data moves between devices by JAX's collectives and lax.ppermute only.
A program may use at most 256 MiB of HBM per device.

v0:
```python
import math

import jax
import jax.numpy as jnp
from jax import lax
from jax.sharding import PartitionSpec as P

HEADS = 12


def passed_along(value, axis, steps):
    count = lax.axis_size(axis)
    pairs = [(source, (source + steps) % count) for source in range(count)]
    return lax.ppermute(value, axis, pairs)


def norm_parts(values, gain, bias):
    mean_value = jnp.mean(values, axis=-1, keepdims=True)
    centered = values - mean_value
    inv_std = lax.rsqrt(jnp.mean(centered * centered, axis=-1, keepdims=True) + 1e-05)
    normed = centered * inv_std
    return (normed * gain + bias, normed, inv_std)


def norm_back(grad_out, normed, inv_std, gain):
    scaled = grad_out * gain
    mean_one = jnp.mean(scaled, axis=-1, keepdims=True)
    mean_two = jnp.mean(scaled * normed, axis=-1, keepdims=True)
    return inv_std * (scaled - mean_one - normed * mean_two)


def rotary_tables(block_id, block_rows, head_dim):
    half_dim = head_dim // 2
    positions = (block_id * block_rows + lax.iota(jnp.int32, block_rows)).astype(jnp.float32)
    freqs = jnp.exp(lax.iota(jnp.float32, half_dim) * (-2.0 * math.log(10000.0) / head_dim))
    angle = positions[:, None] * freqs[None, :]
    return (jnp.cos(angle)[:, None, :], jnp.sin(angle)[:, None, :])


def rotate(values, cosine, sine_table):
    half_dim = values.shape[-1] // 2
    first_half = values[..., :half_dim]
    second_half = values[..., half_dim:]
    return jnp.concatenate(
        [
            first_half * cosine - second_half * sine_table,
            second_half * cosine + first_half * sine_table,
        ],
        axis=-1,
    )


def unrotate(grads, cosine, sine_table):
    half_dim = grads.shape[-1] // 2
    first_half = grads[..., :half_dim]
    second_half = grads[..., half_dim:]
    return jnp.concatenate(
        [
            first_half * cosine + second_half * sine_table,
            second_half * cosine - first_half * sine_table,
        ],
        axis=-1,
    )


def head_view(values, head_count):
    return values.reshape(values.shape[0], head_count, values.shape[1] // head_count)


def forward_visit(state, local_query, block_keys, block_values, head_count, score_scale):
    run_max, run_sum, accum = state
    query_heads = head_view(local_query, head_count)
    key_heads = head_view(block_keys, head_count)
    value_heads = head_view(block_values, head_count)
    scores = (
        jnp.einsum("qhe,khe->hqk", query_heads, key_heads, preferred_element_type=jnp.float32)
        * score_scale
    )
    new_max = jnp.maximum(run_max, jnp.max(scores, axis=-1))
    weights = jnp.exp(scores - new_max[:, :, None])
    factor = jnp.exp(run_max - new_max)
    new_sum = run_sum * factor + jnp.sum(weights, axis=-1)
    update = jnp.einsum(
        "hqk,khe->qhe",
        weights.astype(jnp.bfloat16),
        value_heads,
        preferred_element_type=jnp.float32,
    )
    return (new_max, new_sum, accum * jnp.transpose(factor)[:, :, None] + update)


def backward_pair(
    query_rows, key_rows, value_rows, grad_rows, log_total, row_delta, head_count, score_scale
):
    query_heads = head_view(query_rows, head_count)
    key_heads = head_view(key_rows, head_count)
    value_heads = head_view(value_rows, head_count)
    grad_heads = head_view(grad_rows, head_count)
    scores = (
        jnp.einsum("qhe,khe->hqk", query_heads, key_heads, preferred_element_type=jnp.float32)
        * score_scale
    )
    probs = jnp.exp(scores - log_total[:, :, None])
    grad_probs = jnp.einsum(
        "qhe,khe->hqk", grad_heads, value_heads, preferred_element_type=jnp.float32
    )
    grad_scores = (probs * (grad_probs - row_delta[:, :, None])).astype(jnp.bfloat16)
    grad_query = (
        jnp.einsum("hqk,khe->qhe", grad_scores, key_heads, preferred_element_type=jnp.float32)
        * score_scale
    )
    grad_keys = (
        jnp.einsum("hqk,qhe->khe", grad_scores, query_heads, preferred_element_type=jnp.float32)
        * score_scale
    )
    grad_values = jnp.einsum(
        "hqk,qhe->khe", probs.astype(jnp.bfloat16), grad_heads, preferred_element_type=jnp.float32
    )
    return (
        grad_query.reshape(query_rows.shape[0], -1),
        grad_keys.reshape(key_rows.shape[0], -1),
        grad_values.reshape(key_rows.shape[0], -1),
    )


def body(
    inputs,
    earlier,
    input_proj,
    output_proj,
    up_proj,
    down_proj,
    norm1_gain,
    norm1_bias,
    norm2_gain,
    norm2_bias,
    mixing,
    block_order,
    grad_next,
):
    head_count = HEADS
    batch_count = inputs.shape[0]
    block_rows = inputs.shape[1]
    model_width = inputs.shape[2]
    head_dim = model_width // head_count
    score_scale = head_dim ** (-0.5)
    stream_count = earlier.shape[0]
    cycle_size = lax.axis_size("ctx")
    cycle_place = lax.axis_index("ctx")
    norm_stack = jnp.stack([norm1_gain, norm1_bias, norm2_gain, norm2_bias])
    full_in, full_out, full_up, full_down, full_norms = (
        lax.all_gather(input_proj, "fsdp", axis=0, tiled=True),
        lax.all_gather(output_proj, "fsdp", axis=0, tiled=True),
        lax.all_gather(up_proj, "fsdp", axis=0, tiled=True),
        lax.all_gather(down_proj, "fsdp", axis=0, tiled=True),
        lax.all_gather(norm_stack.astype(jnp.bfloat16), "fsdp", axis=1, tiled=True).astype(
            norm_stack.dtype
        ),
    )
    gain_one = full_norms[0]
    bias_one = full_norms[1]
    gain_two = full_norms[2]
    bias_two = full_norms[3]
    next_list = []
    grad_in_list = []
    earlier_list = []
    totals = None
    for batch in range(batch_count):
        block_input = inputs[batch].astype(jnp.float32)
        order_row = block_order[batch]
        own_block = order_row[cycle_place]
        cosine, sine_table = rotary_tables(own_block, block_rows, head_dim)
        normed_in, normed_one, inv_one = norm_parts(block_input, gain_one, bias_one)
        normed_in_b = normed_in.astype(jnp.bfloat16)
        projected = jnp.dot(normed_in_b, full_in, preferred_element_type=jnp.float32)
        local_query = (
            rotate(head_view(projected[:, :model_width], head_count), cosine, sine_table)
            .reshape(block_rows, model_width)
            .astype(jnp.bfloat16)
        )
        local_keys = (
            rotate(
                head_view(projected[:, model_width : 2 * model_width], head_count),
                cosine,
                sine_table,
            )
            .reshape(block_rows, model_width)
            .astype(jnp.bfloat16)
        )
        local_values = projected[:, 2 * model_width :].astype(jnp.bfloat16)
        start_state = (
            jnp.full((head_count, block_rows), -1e30, jnp.float32),
            jnp.zeros((head_count, block_rows), jnp.float32),
            jnp.zeros((block_rows, head_count, head_dim), jnp.float32),
        )
        piece_keys = lax.all_gather(local_keys, "ctx", axis=0, tiled=True)
        piece_values = lax.all_gather(local_values, "ctx", axis=0, tiled=True)
        count = piece_keys.shape[0] // block_rows

        def one_block(index, state_now):
            block_keys = lax.dynamic_slice_in_dim(piece_keys, index * block_rows, block_rows, 0)
            block_values = lax.dynamic_slice_in_dim(piece_values, index * block_rows, block_rows, 0)
            return lax.cond(
                order_row[index] <= own_block,
                lambda held: forward_visit(
                    held, local_query, block_keys, block_values, head_count, score_scale
                ),
                lambda held: held,
                state_now,
            )

        run_max, run_sum, accum = lax.fori_loop(0, count, one_block, start_state)
        log_total = run_max + jnp.log(run_sum)
        attended = accum / jnp.transpose(run_sum)[:, :, None]
        attended_b = attended.reshape(block_rows, model_width).astype(jnp.bfloat16)
        middle = block_input + jnp.dot(attended_b, full_out, preferred_element_type=jnp.float32)
        normed_mid, normed_two, inv_two = norm_parts(middle, gain_two, bias_two)
        normed_mid_b = normed_mid.astype(jnp.bfloat16)
        hidden_pre = jnp.dot(normed_mid_b, full_up, preferred_element_type=jnp.float32)
        hidden_b = jax.nn.gelu(hidden_pre).astype(jnp.bfloat16)
        result = middle + jnp.dot(hidden_b, full_down, preferred_element_type=jnp.float32)
        previous = earlier[:, batch].astype(jnp.float32)
        mixed_out = (
            jnp.sum(mixing[:stream_count, None, None] * previous, axis=0)
            + mixing[stream_count] * result
        )
        next_list.append(mixed_out.astype(jnp.bfloat16))
        grad_out = grad_next[batch].astype(jnp.float32)
        earlier_list.append(
            (mixing[:stream_count, None, None] * grad_out[None]).astype(jnp.bfloat16)
        )
        mix_grad = jnp.concatenate(
            [jnp.sum(previous * grad_out[None], axis=(1, 2)), jnp.sum(result * grad_out)[None]]
        )
        grad_result = mixing[stream_count] * grad_out
        grad_result_b = grad_result.astype(jnp.bfloat16)
        grad_down = jnp.einsum(
            "rf,rd->fd", hidden_b, grad_result_b, preferred_element_type=jnp.float32
        )
        grad_hidden = jnp.einsum(
            "rd,fd->rf", grad_result_b, full_down, preferred_element_type=jnp.float32
        )
        grad_pre = jax.vjp(jax.nn.gelu, hidden_pre)[1](grad_hidden)[0]
        grad_pre_b = grad_pre.astype(jnp.bfloat16)
        grad_up = jnp.einsum(
            "rd,rf->df", normed_mid_b, grad_pre_b, preferred_element_type=jnp.float32
        )
        grad_norm_mid = jnp.einsum(
            "rf,df->rd", grad_pre_b, full_up, preferred_element_type=jnp.float32
        )
        grad_gain_two = jnp.sum(grad_norm_mid * normed_two, axis=0)
        grad_bias_two = jnp.sum(grad_norm_mid, axis=0)
        grad_middle = grad_result + norm_back(grad_norm_mid, normed_two, inv_two, gain_two)
        grad_middle_b = grad_middle.astype(jnp.bfloat16)
        grad_out_proj = jnp.einsum(
            "rd,re->de", attended_b, grad_middle_b, preferred_element_type=jnp.float32
        )
        grad_att_b = jnp.einsum(
            "re,de->rd", grad_middle_b, full_out, preferred_element_type=jnp.float32
        ).astype(jnp.bfloat16)
        row_delta = jnp.einsum(
            "qhe,qhe->hq", head_view(grad_att_b, head_count).astype(jnp.float32), attended
        )
        zero_rows = jnp.zeros((block_rows, model_width), jnp.float32)

        def key_visit(offset, grad_query, cycle_keys, cycle_values, cycle_dk, cycle_dv):
            their_block = order_row[(cycle_place - offset) % cycle_size]

            def add_pair(held):
                part_q, part_k, part_v = backward_pair(
                    local_query,
                    cycle_keys,
                    cycle_values,
                    grad_att_b,
                    log_total,
                    row_delta,
                    head_count,
                    score_scale,
                )
                return (held[0] + part_q, held[1] + part_k, held[2] + part_v)

            return lax.cond(
                their_block <= own_block,
                add_pair,
                lambda held: held,
                (grad_query, cycle_dk, cycle_dv),
            )

        def key_turn(offset, carry):
            grad_query, cycle_keys, cycle_values, cycle_dk, cycle_dv = carry
            grad_query, cycle_dk, cycle_dv = key_visit(
                offset, grad_query, cycle_keys, cycle_values, cycle_dk, cycle_dv
            )
            cycle_keys, cycle_values = passed_along((cycle_keys, cycle_values), "ctx", 1)
            cycle_dk, cycle_dv = (
                passed_along(cycle_dk.astype(jnp.bfloat16), "ctx", 1).astype(cycle_dk.dtype),
                passed_along(cycle_dv.astype(jnp.bfloat16), "ctx", 1).astype(cycle_dv.dtype),
            )
            return (grad_query, cycle_keys, cycle_values, cycle_dk, cycle_dv)

        grad_query, cycle_keys, cycle_values, cycle_dk, cycle_dv = lax.fori_loop(
            0, cycle_size - 1, key_turn, (zero_rows, local_keys, local_values, zero_rows, zero_rows)
        )
        grad_query, cycle_dk, cycle_dv = key_visit(
            cycle_size - 1, grad_query, cycle_keys, cycle_values, cycle_dk, cycle_dv
        )
        grad_keys, grad_values = (
            passed_along(cycle_dk.astype(jnp.bfloat16), "ctx", 1).astype(cycle_dk.dtype),
            passed_along(cycle_dv.astype(jnp.bfloat16), "ctx", 1).astype(cycle_dv.dtype),
        )
        grad_query_pre = unrotate(head_view(grad_query, head_count), cosine, sine_table).reshape(
            block_rows, model_width
        )
        grad_keys_pre = unrotate(head_view(grad_keys, head_count), cosine, sine_table).reshape(
            block_rows, model_width
        )
        grad_proj_b = jnp.concatenate([grad_query_pre, grad_keys_pre, grad_values], axis=1).astype(
            jnp.bfloat16
        )
        grad_in_proj = jnp.einsum(
            "rd,rf->df", normed_in_b, grad_proj_b, preferred_element_type=jnp.float32
        )
        grad_norm_in = jnp.einsum(
            "rf,df->rd", grad_proj_b, full_in, preferred_element_type=jnp.float32
        )
        grad_gain_one = jnp.sum(grad_norm_in * normed_one, axis=0)
        grad_bias_one = jnp.sum(grad_norm_in, axis=0)
        grad_block_in = grad_middle + norm_back(grad_norm_in, normed_one, inv_one, gain_one)
        grad_in_list.append(grad_block_in.astype(jnp.bfloat16))
        norm_grads = jnp.stack([grad_gain_one, grad_bias_one, grad_gain_two, grad_bias_two])
        mix_tiled = jnp.broadcast_to(mix_grad[None, :], (lax.axis_size("fsdp"), stream_count + 1))
        grad_terms = (grad_in_proj, grad_out_proj, grad_up, grad_down, norm_grads, mix_tiled)
        shares = (
            lax.psum_scatter(
                grad_terms[0].astype(jnp.bfloat16), "fsdp", scatter_dimension=0, tiled=True
            ).astype(jnp.float32),
            lax.psum_scatter(
                grad_terms[1].astype(jnp.bfloat16), "fsdp", scatter_dimension=0, tiled=True
            ).astype(jnp.float32),
            lax.psum_scatter(
                grad_terms[2].astype(jnp.bfloat16), "fsdp", scatter_dimension=0, tiled=True
            ).astype(jnp.float32),
            lax.psum_scatter(
                grad_terms[3].astype(jnp.bfloat16), "fsdp", scatter_dimension=0, tiled=True
            ).astype(jnp.float32),
            lax.psum_scatter(
                grad_terms[4].astype(jnp.bfloat16), "fsdp", scatter_dimension=1, tiled=True
            ).astype(jnp.float32),
            lax.psum_scatter(
                grad_terms[5].astype(jnp.bfloat16), "fsdp", scatter_dimension=0, tiled=True
            ).astype(jnp.float32),
        )
        totals = (
            shares
            if totals is None
            else tuple((first + second for first, second in zip(totals, shares)))
        )
    totals = lax.psum(totals, "ctx")
    norm_total = totals[4]
    return (
        jnp.stack(next_list),
        jnp.stack(grad_in_list),
        jnp.stack(earlier_list, axis=1),
        totals[0],
        totals[1],
        totals[2],
        totals[3],
        norm_total[0],
        norm_total[1],
        norm_total[2],
        norm_total[3],
        totals[5].reshape(-1),
    )


def solution(mesh):
    placed = (
        P("fsdp", "ctx", None),
        P(None, "fsdp", "ctx", None),
        P("fsdp", None),
        P("fsdp", None),
        P("fsdp", None),
        P("fsdp", None),
        P("fsdp"),
        P("fsdp"),
        P("fsdp"),
        P("fsdp"),
        P(),
        P(),
        P("fsdp", "ctx", None),
    )
    return jax.shard_map(
        body,
        mesh=mesh,
        in_specs=placed,
        out_specs=(
            P("fsdp", "ctx", None),
            P("fsdp", "ctx", None),
            P(None, "fsdp", "ctx", None),
            P("fsdp", None),
            P("fsdp", None),
            P("fsdp", None),
            P("fsdp", None),
            P("fsdp"),
            P("fsdp"),
            P("fsdp"),
            P("fsdp"),
            P(),
        ),
        check_vma=False,
    )
```

profile of v0, /device:TPU:0, one launch (start us, length us, event | category | flops | bytes accessed | tf_op | source)
XLA Modules:
  0.0 1612.3 jit_solution(10270844397078836579)
XLA Ops:
  20.6 22.4 %all-gather.10.cloned.1.call-done = bf16[768,2304]{1,0:T(8,128)(2,1)} async-done(((bf16[192,2304]{1,0:T(8,128)(2,1)}), bf16[768,2304]{1,0:T(8,128)(2,1)}) %all-gather.10.cloned.1.call-update) | async-done | bytes 3538960 | tf_op jit(solution)/shard_map/all_gather | solution.py:152
  66.6 42.3 %all-gather.14.cloned.1.call-done = bf16[2048,768]{1,0:T(8,128)(2,1)} async-done(((bf16[256,768]{1,0:T(8,128)(2,1)}), bf16[2048,768]{1,0:T(8,128)(2,1)}) %all-gather.14.cloned.1.call-update) | async-done | bytes 3145744 | tf_op jit(solution)/shard_map/all_gather | solution.py:197
  113.5 56.2 %all-gather.24.cloned.1.call-done = bf16[2048,768]{1,0:T(8,128)(2,1)} async-done(((bf16[256,768]{1,0:T(8,128)(2,1)}), bf16[2048,768]{1,0:T(8,128)(2,1)}) %all-gather.24.cloned.1.call-update) | async-done | bytes 3145744 | tf_op jit(solution)/shard_map/all_gather | solution.py:197
  174.4 58.6 %all-gather.12.cloned.1.call-done = bf16[2048,768]{0,1:T(8,128)(2,1)} async-done(((bf16[256,768]{0,1:T(8,128)(2,1)}), bf16[2048,768]{0,1:T(8,128)(2,1)}) %all-gather.12.cloned.1.call-update) | async-done | bytes 3145744 | tf_op jit(solution)/shard_map/all_gather | solution.py:196
  233.1 39.3 %while.82 = (s32[]{:T(128)}, f32[12,256]{1,0:T(8,128)S(1)}, f32[12,256]{1,0:T(8,128)S(1)}, f32[256,12,64]{0,2,1:T(8,128)S(1)}, s32[8]{0:T(128)}, /*index=5*/s32[...) while((s32[]{:T(128)}, f32[12,256]{1,0:T(8,128)S(1)}, ...), condition=%wide.region_8.0_spmd, body=%wide.region_3.8_spmd.sunk | while | flops 208020480 | bytes 13959457 | solution.py:212
  272.5 23.9 %all-gather.22.cloned.1.call-done = bf16[2048,768]{0,1:T(8,128)(2,1)} async-done(((bf16[256,768]{0,1:T(8,128)(2,1)}), bf16[2048,768]{0,1:T(8,128)(2,1)}) %all-gather.22.cloned.1.call-update) | async-done | bytes 3145744 | tf_op jit(solution)/shard_map/all_gather | solution.py:196
  296.4 26.4 %while.83 = (s32[]{:T(128)}, f32[12,256]{1,0:T(8,128)S(1)}, f32[12,256]{1,0:T(8,128)S(1)}, f32[256,12,64]{0,2,1:T(8,128)S(1)}, s32[8]{0:T(128)}, /*index=5*/s32[...) while((s32[]{:T(128)}, f32[12,256]{1,0:T(8,128)S(1)}, ...), condition=%wide.region_19.20_spmd, body=%wide.region_14.19_spmd.sunk | while | flops 208020480 | bytes 13959457 | solution.py:212
  330.7 21.7 %all-gather.18.cloned.1.call-done = bf16[768,3072]{1,0:T(8,128)(2,1)} async-done(((bf16[192,3072]{1,0:T(8,128)(2,1)}), bf16[768,3072]{1,0:T(8,128)(2,1)}) %all-gather.18.cloned.1.call-update) | async-done | bytes 4718608 | tf_op jit(solution)/shard_map/all_gather | solution.py:154
  361.4 30.1 %all-gather.20.cloned.1.call-done = bf16[3072,768]{1,0:T(8,128)(2,1)} async-done(((bf16[768,768]{1,0:T(8,128)(2,1)}), bf16[3072,768]{1,0:T(8,128)(2,1)}) %all-gather.20.cloned.1.call-update) | async-done | bytes 4718608 | tf_op jit(solution)/shard_map/all_gather | solution.py:155
  421.9 320.3 %while.84 = (s32[]{:T(128)}, f32[256,768]{0,1:T(8,128)}, bf16[256,768]{0,1:T(8,128)(2,1)S(1)}, bf16[256,768]{0,1:T(8,128)(2,1)S(1)}, f32[256,768]{0,1:T(8,128)},...) while((s32[]{:T(128)}, f32[256,768]{0,1:T(8,128)}, ...), condition=%wide.region_27.28_spmd.clone, body=%wide.region_24.0_spmd.clone.sunk | while | flops 511770656 | bytes 48452304 | solution.py:301
  437.3 8.9 collective-permute-done.2
  463.0 7.7 collective-permute-done.1
  485.7 10.7 collective-permute-done.2
  531.1 14.6 collective-permute-done.2
  577.1 11.2 collective-permute-done.2
  623.5 12.4 collective-permute-done.2
  668.1 14.6 collective-permute-done.2
  711.6 11.2 collective-permute-done.2
  742.2 9.8 conditional.6
  756.8 8.6 collective-permute-done.8
  778.2 273.9 %while.85 = (s32[]{:T(128)}, f32[256,768]{0,1:T(8,128)S(1)}, bf16[256,768]{0,1:T(8,128)(2,1)S(1)}, bf16[256,768]{0,1:T(8,128)(2,1)S(1)}, f32[256,768]{0,1:T(8,12...) while((s32[]{:T(128)}, f32[256,768]{0,1:T(8,128)S(1)}, ...), condition=%wide.region_37.38_spmd.clone, body=%wide.region_34.0_spmd.clone.sunk | while | flops 511770656 | bytes 43733684 | solution.py:301
  788.6 13.7 collective-permute-done.6
  830.3 10.2 collective-permute-done.6
  909.3 7.9 collective-permute-done.6
  1027.3 9.8 collective-permute-done.6
  1119.7 45.7 %reduce-scatter.23.cloned.1.call-done = bf16[192,3072]{1,0:T(8,128)(2,1)} async-done(((bf16[768,3072]{1,0:T(8,128)(2,1)}), bf16[192,3072]{1,0:T(8,128)(2,1)}) %reduce-scatter.23.cloned.1.call-update) | async-done | bytes 1179664 | tf_op jit(solution)/shard_map/reduce_scatter | solution.py:340
  1165.4 50.4 %reduce-scatter.25.cloned.1.call-done = bf16[192,3072]{1,0:T(8,128)(2,1)} async-done(((bf16[768,3072]{1,0:T(8,128)(2,1)}), bf16[192,3072]{1,0:T(8,128)(2,1)}) %reduce-scatter.25.cloned.1.call-update) | async-done | bytes 1179664 | tf_op jit(solution)/shard_map/reduce_scatter | solution.py:340
  1219.2 47.0 %reduce-scatter.27.cloned.1.call-done = bf16[768,768]{1,0:T(8,128)(2,1)} async-done(((bf16[3072,768]{1,0:T(8,128)(2,1)}), bf16[768,768]{1,0:T(8,128)(2,1)}) %reduce-scatter.27.cloned.1.call-update) | async-done | bytes 1179664 | tf_op jit(solution)/shard_map/reduce_scatter | solution.py:343
  1266.2 50.4 %reduce-scatter.29.cloned.1.call-done = bf16[768,768]{1,0:T(8,128)(2,1)} async-done(((bf16[3072,768]{1,0:T(8,128)(2,1)}), bf16[768,768]{1,0:T(8,128)(2,1)}) %reduce-scatter.29.cloned.1.call-update) | async-done | bytes 1179664 | tf_op jit(solution)/shard_map/reduce_scatter | solution.py:343
  1350.2 10.6 reduce-scatter.33.cloned.1.call-done
  1361.7 23.1 %all-reduce.2 = (f32[4,192]{1,0:T(4,128)S(1)}, f32[5]{0:T(128)}) all-reduce(f32[4,192]{1,0:T(4,128)S(1)} %convert_add_fusion.4, f32[5]{0:T(128)S(1)} %fusion.126), channel_id=1, replica_groups=mesh['ctx'=8,'fsdp'=4] {'ctx'}, use_global_device_ids=true, to_apply=%region_64.65 | all-reduce | flops 773 | bytes 6184 | tf_op jit(solution)/shard_map/psum | solution.py:358
  1385.4 213.3 %all-reduce.7.cloned.1.call-done = (f32[192,2304]{1,0:T(8,128)}, f32[192,768]{1,0:T(8,128)}, f32[192,3072]{1,0:T(8,128)}, f32[768,768]{1,0:T(8,128)}) async-done(((f32[192,2304]{1,0:T(8,128)}, f32[192,768]{1,0:T(8,128)}, f32[192,3072]{1,0:T(8,128)}, f32[768,768]{1,0:T(8,128)}), (f32[192,2304]{1,0:T(8,128)}, f32[192,768]{1,0:T(8,128)}, f32[192,3072]{1,0:T(8,128)}, ...) | async-done | bytes 7077904 | tf_op jit(solution)/shard_map/psum | solution.py:358
  (857 shorter events, 780.4 us)
Async XLA Ops:
  7.2 35.9 %all-gather.10.cloned.1.call-start = ((), (), s32[]{:S(2)}) async-start(), calls=%async_computation.10 | async-start | bytes 4423680 | tf_op jit(solution)/shard_map/all_gather | solution.py:152
  7.9 100.9 %all-gather.14.cloned.1.call-start = ((), (), s32[]{:S(2)}) async-start(), calls=%async_computation.12 | async-start | bytes 3538944 | tf_op jit(solution)/shard_map/all_gather | solution.py:197
  48.7 121.1 %all-gather.24.cloned.1.call-start = ((), (), s32[]{:S(2)}) async-start(), calls=%async_computation.17 | async-start | bytes 3538944 | tf_op jit(solution)/shard_map/all_gather | solution.py:197
  54.2 178.7 %all-gather.12.cloned.1.call-start = ((), (), s32[]{:S(2)}) async-start(), calls=%async_computation.11 | async-start | bytes 3538944 | tf_op jit(solution)/shard_map/all_gather | solution.py:196
  60.4 235.9 %all-gather.22.cloned.1.call-start = ((), (), s32[]{:S(2)}) async-start(), calls=%async_computation.16 | async-start | bytes 3538944 | tf_op jit(solution)/shard_map/all_gather | solution.py:196
  63.5 259.4 %all-gather.16.cloned.1.call-start = ((), (), s32[]{:S(2)}) async-start(), calls=%async_computation.13 | async-start | bytes 1474560 | tf_op jit(solution)/shard_map/all_gather | solution.py:153
  64.1 288.3 %all-gather.18.cloned.1.call-start = ((), (), s32[]{:S(2)}) async-start(), calls=%async_computation.14 | async-start | bytes 5898240 | tf_op jit(solution)/shard_map/all_gather | solution.py:154
  64.9 326.6 %all-gather.20.cloned.1.call-start = ((), (), s32[]{:S(2)}) async-start(), calls=%async_computation.15 | async-start | bytes 5898240 | tf_op jit(solution)/shard_map/all_gather | solution.py:155
  65.6 1049.3 %reduce-scatter.19.cloned.1.call-start = ((), (), s32[]{:S(2)}) async-start(), calls=%async_computation.20 | async-start | bytes 1474560 | tf_op jit(solution)/shard_map/reduce_scatter | solution.py:337
  411.4 703.5 %reduce-scatter.21.cloned.1.call-start = ((), (), s32[]{:S(2)}) async-start(), calls=%async_computation.21 | async-start | bytes 1474560 | tf_op jit(solution)/shard_map/reduce_scatter | solution.py:337
  420.9 696.0 %reduce-scatter.15.cloned.1.call-start = ((), (), s32[]{:S(2)}) async-start(), calls=%async_computation.18 | async-start | bytes 4423680 | tf_op jit(solution)/shard_map/reduce_scatter | solution.py:334
  435.8 35.0 %collective-permute-start.1 = (bf16[256,768]{0,1:T(8,128)(2,1)S(1)}, bf16[256,768]{0,1:T(8,128)(2,1)S(1)}, u32[]{:S(2)}, u32[]{:S(2)}) collective-permute-start(bf16[256,768]{0,1:T(8,128)(2,1)S(1)} %copy.181), channel_id=1, source_target_pairs={{0,4},{4,8},{8,12},{12,16},{16,20},{20,24},{24,28},{28,0},{1,5},{5... | collective-permute-start | bytes 1179656 | tf_op jit(solution)/shard_map/while/body/eval_jaxpr/ppermute | solution.py:14
  482.7 30.5 %collective-permute-start = (bf16[256,768]{0,1:T(8,128)(2,1)S(1)}, bf16[256,768]{0,1:T(8,128)(2,1)S(1)}, u32[]{:S(2)}, u32[]{:S(2)}) collective-permute-start(bf16[256,768]{0,1:T(8,128)(2,1)S(1)} %copy.180), channel_id=1, source_target_pairs={{0,4},{4,8},{8,12},{12,16},{16,20},{20,24},{24,28},{28,0},{1,5},{5... | collective-permute-start | bytes 1179656 | tf_op jit(solution)/shard_map/while/body/eval_jaxpr/ppermute | solution.py:14
  482.8 37.3 %collective-permute-start.1 = (bf16[256,768]{0,1:T(8,128)(2,1)S(1)}, bf16[256,768]{0,1:T(8,128)(2,1)S(1)}, u32[]{:S(2)}, u32[]{:S(2)}) collective-permute-start(bf16[256,768]{0,1:T(8,128)(2,1)S(1)} %copy.181), channel_id=1, source_target_pairs={{0,4},{4,8},{8,12},{12,16},{16,20},{20,24},{24,28},{28,0},{1,5},{5... | collective-permute-start | bytes 1179656 | tf_op jit(solution)/shard_map/while/body/eval_jaxpr/ppermute | solution.py:14
  530.9 31.6 %collective-permute-start = (bf16[256,768]{0,1:T(8,128)(2,1)S(1)}, bf16[256,768]{0,1:T(8,128)(2,1)S(1)}, u32[]{:S(2)}, u32[]{:S(2)}) collective-permute-start(bf16[256,768]{0,1:T(8,128)(2,1)S(1)} %copy.180), channel_id=1, source_target_pairs={{0,4},{4,8},{8,12},{12,16},{16,20},{20,24},{24,28},{28,0},{1,5},{5... | collective-permute-start | bytes 1179656 | tf_op jit(solution)/shard_map/while/body/eval_jaxpr/ppermute | solution.py:14
  531.0 37.6 %collective-permute-start.1 = (bf16[256,768]{0,1:T(8,128)(2,1)S(1)}, bf16[256,768]{0,1:T(8,128)(2,1)S(1)}, u32[]{:S(2)}, u32[]{:S(2)}) collective-permute-start(bf16[256,768]{0,1:T(8,128)(2,1)S(1)} %copy.181), channel_id=1, source_target_pairs={{0,4},{4,8},{8,12},{12,16},{16,20},{20,24},{24,28},{28,0},{1,5},{5... | collective-permute-start | bytes 1179656 | tf_op jit(solution)/shard_map/while/body/eval_jaxpr/ppermute | solution.py:14
  577.1 33.2 %collective-permute-start.1 = (bf16[256,768]{0,1:T(8,128)(2,1)S(1)}, bf16[256,768]{0,1:T(8,128)(2,1)S(1)}, u32[]{:S(2)}, u32[]{:S(2)}) collective-permute-start(bf16[256,768]{0,1:T(8,128)(2,1)S(1)} %copy.181), channel_id=1, source_target_pairs={{0,4},{4,8},{8,12},{12,16},{16,20},{20,24},{24,28},{28,0},{1,5},{5... | collective-permute-start | bytes 1179656 | tf_op jit(solution)/shard_map/while/body/eval_jaxpr/ppermute | solution.py:14
  623.4 29.4 %collective-permute-start = (bf16[256,768]{0,1:T(8,128)(2,1)S(1)}, bf16[256,768]{0,1:T(8,128)(2,1)S(1)}, u32[]{:S(2)}, u32[]{:S(2)}) collective-permute-start(bf16[256,768]{0,1:T(8,128)(2,1)S(1)} %copy.180), channel_id=1, source_target_pairs={{0,4},{4,8},{8,12},{12,16},{16,20},{20,24},{24,28},{28,0},{1,5},{5... | collective-permute-start | bytes 1179656 | tf_op jit(solution)/shard_map/while/body/eval_jaxpr/ppermute | solution.py:14
  623.4 33.6 %collective-permute-start.1 = (bf16[256,768]{0,1:T(8,128)(2,1)S(1)}, bf16[256,768]{0,1:T(8,128)(2,1)S(1)}, u32[]{:S(2)}, u32[]{:S(2)}) collective-permute-start(bf16[256,768]{0,1:T(8,128)(2,1)S(1)} %copy.181), channel_id=1, source_target_pairs={{0,4},{4,8},{8,12},{12,16},{16,20},{20,24},{24,28},{28,0},{1,5},{5... | collective-permute-start | bytes 1179656 | tf_op jit(solution)/shard_map/while/body/eval_jaxpr/ppermute | solution.py:14
  667.9 30.9 %collective-permute-start = (bf16[256,768]{0,1:T(8,128)(2,1)S(1)}, bf16[256,768]{0,1:T(8,128)(2,1)S(1)}, u32[]{:S(2)}, u32[]{:S(2)}) collective-permute-start(bf16[256,768]{0,1:T(8,128)(2,1)S(1)} %copy.180), channel_id=1, source_target_pairs={{0,4},{4,8},{8,12},{12,16},{16,20},{20,24},{24,28},{28,0},{1,5},{5... | collective-permute-start | bytes 1179656 | tf_op jit(solution)/shard_map/while/body/eval_jaxpr/ppermute | solution.py:14
  668.0 35.0 %collective-permute-start.1 = (bf16[256,768]{0,1:T(8,128)(2,1)S(1)}, bf16[256,768]{0,1:T(8,128)(2,1)S(1)}, u32[]{:S(2)}, u32[]{:S(2)}) collective-permute-start(bf16[256,768]{0,1:T(8,128)(2,1)S(1)} %copy.181), channel_id=1, source_target_pairs={{0,4},{4,8},{8,12},{12,16},{16,20},{20,24},{24,28},{28,0},{1,5},{5... | collective-permute-start | bytes 1179656 | tf_op jit(solution)/shard_map/while/body/eval_jaxpr/ppermute | solution.py:14
  711.5 30.7 %collective-permute-start.1 = (bf16[256,768]{0,1:T(8,128)(2,1)S(1)}, bf16[256,768]{0,1:T(8,128)(2,1)S(1)}, u32[]{:S(2)}, u32[]{:S(2)}) collective-permute-start(bf16[256,768]{0,1:T(8,128)(2,1)S(1)} %copy.181), channel_id=1, source_target_pairs={{0,4},{4,8},{8,12},{12,16},{16,20},{20,24},{24,28},{28,0},{1,5},{5... | collective-permute-start | bytes 1179656 | tf_op jit(solution)/shard_map/while/body/eval_jaxpr/ppermute | solution.py:14
  773.6 343.3 %reduce-scatter.17.cloned.1.call-start = ((), (), s32[]{:S(2)}) async-start(), calls=%async_computation.19 | async-start | bytes 4423680 | tf_op jit(solution)/shard_map/reduce_scatter | solution.py:334
  788.6 31.5 %collective-permute-start.5 = (bf16[256,768]{0,1:T(8,128)(2,1)}, bf16[256,768]{0,1:T(8,128)(2,1)S(1)}, u32[]{:S(2)}, u32[]{:S(2)}) collective-permute-start(bf16[256,768]{0,1:T(8,128)(2,1)} %copy.205), channel_id=1, source_target_pairs={{0,4},{4,8},{8,12},{12,16},{16,20},{20,24},{24,28},{28,0},{1,5},{5... | collective-permute-start | bytes 1179656 | tf_op jit(solution)/shard_map/while/body/eval_jaxpr/ppermute | solution.py:14
  1022.3 29.7 %collective-permute-start.5 = (bf16[256,768]{0,1:T(8,128)(2,1)}, bf16[256,768]{0,1:T(8,128)(2,1)S(1)}, u32[]{:S(2)}, u32[]{:S(2)}) collective-permute-start(bf16[256,768]{0,1:T(8,128)(2,1)} %copy.205), channel_id=1, source_target_pairs={{0,4},{4,8},{8,12},{12,16},{16,20},{20,24},{24,28},{28,0},{1,5},{5... | collective-permute-start | bytes 1179656 | tf_op jit(solution)/shard_map/while/body/eval_jaxpr/ppermute | solution.py:14
  1076.2 89.2 %reduce-scatter.23.cloned.1.call-start = ((), (), s32[]{:S(2)}) async-start(), calls=%async_computation.22 | async-start | bytes 5898240 | tf_op jit(solution)/shard_map/reduce_scatter | solution.py:340
  1082.6 133.2 %reduce-scatter.25.cloned.1.call-start = ((), (), s32[]{:S(2)}) async-start(), calls=%async_computation.23 | async-start | bytes 5898240 | tf_op jit(solution)/shard_map/reduce_scatter | solution.py:340
  1089.1 177.1 %reduce-scatter.27.cloned.1.call-start = ((), (), s32[]{:S(2)}) async-start(), calls=%async_computation.24 | async-start | bytes 5898240 | tf_op jit(solution)/shard_map/reduce_scatter | solution.py:343
  1097.5 219.2 %reduce-scatter.29.cloned.1.call-start = ((), (), s32[]{:S(2)}) async-start(), calls=%async_computation.25 | async-start | bytes 5898240 | tf_op jit(solution)/shard_map/reduce_scatter | solution.py:343
  1104.5 244.9 %reduce-scatter.31.cloned.1.call-start = ((), (), s32[]{:S(2)}) async-start(), calls=%async_computation.26 | async-start | bytes 245760
  1113.7 247.2 %reduce-scatter.33.cloned.1.call-start = ((), (), s32[]{:S(2)}) async-start(), calls=%async_computation.27 | async-start | bytes 245760
  1114.6 484.1 %all-reduce.7.cloned.1.call-start = ((), (), s32[]{:S(2)}) async-start(), calls=%async_computation.28 | async-start | bytes 14155776 | tf_op jit(solution)/shard_map/psum | solution.py:358
  (187 other events, 1958.5 us)
Sparse Core Ops, SparseCore 0:
  9.5 33.4 all-gather.9
  48.8 60.0 all-gather.13
  111.0 58.6 all-gather.23
  171.6 61.3 all-gather.11
  235.5 60.8 all-gather.21
  297.7 15.6 all-gather.15
  314.9 37.4 all-gather.17
  354.0 37.4 all-gather.19
  411.5 25.5 reduce-scatter.18
  440.1 25.6 reduce-scatter.20
  773.7 36.3 reduce-scatter.14
  1076.4 38.5 reduce-scatter.16
  1117.5 47.9 reduce-scatter.22
  1167.8 47.9 reduce-scatter.24
  1218.2 47.9 reduce-scatter.26
  1268.6 47.9 reduce-scatter.28
  1318.9 19.7 reduce-scatter.30
  1341.0 19.7 reduce-scatter.32
  1365.8 232.8 all-reduce.6
where the time goes:
time: 1620 us; the launch traced here: 1610 us
  waiting for transfers between devices  1070 us (66%)
  matrix products  135 us (8%)
  other arithmetic  124 us (8%)
  local copies, waits for them, and re-layouts  107 us (7%)
  starting transfers between devices  80.6 us (5%)
  loops' own time  40.1 us (2%)
  blocking collectives  35.1 us (2%)
  between operations  20 us (1%)
    ppermute x60, waiting for transfers between devices, passed_along(): return lax.ppermute(value, axis, pairs)  396 us
    psum x1, waiting for transfers between devices, body(): totals = lax.psum(totals, 'ctx')  213 us
    all_gather x2, waiting for transfers between devices, body(): piece_values = lax.all_gather(local_values, 'ctx', axis=0, tiled=True)  98.5 us
    reduce_scatter x2, waiting for transfers between devices, body(): lax.psum_scatter(grad_terms[3].astype(jnp.bfloat16), 'fsdp', scatter_dime...  97.4 us
    reduce_scatter x2, waiting for transfers between devices, body(): lax.psum_scatter(grad_terms[2].astype(jnp.bfloat16), 'fsdp', scatter_dime...  96.1 us
    all_gather x2, waiting for transfers between devices, body(): piece_keys = lax.all_gather(local_keys, 'ctx', axis=0, tiled=True)  82.5 us
    ppermute x60, starting transfers between devices, passed_along(): return lax.ppermute(value, axis, pairs)  79.2 us
  transfers between devices with their start and end apart: 79, of which 73 were waited for; matrix products, arithmetic and copies ran while one was open for 20% of the time, Pallas kernels for 0%

commit v1 on v0

--- a/solution.py
+++ b/solution.py
@@ -1,8 +1,11 @@
+import functools
 import math
 
 import jax
 import jax.numpy as jnp
 from jax import lax
+from jax.experimental import pallas as pl
+from jax.experimental.pallas import tpu as pltpu
 from jax.sharding import PartitionSpec as P
 
 HEADS = 12
@@ -373,6 +376,832 @@
     )
 
 
+F32 = jnp.float32
+BF16 = jnp.bfloat16
+LOG2E = math.log2(math.e)
+GELU_C = math.sqrt(2.0 / math.pi)
+GELU_A = 0.044715
+ANY = pl.ANY
+VMEM = pltpu.VMEM
+SMEM = pltpu.SMEM
+MIB = 1 << 20
+
+
+def mm(left, right, left_dim, right_dim):
+    return lax.dot_general(
+        left, right, (((left_dim,), (right_dim,)), ((), ())), preferred_element_type=F32
+    )
+
+
+def spec(space):
+    return pl.BlockSpec(memory_space=space)
+
+
+def shape_of(dims, kind):
+    return jax.ShapeDtypeStruct(dims, kind)
+
+
+def run_kernel(kernel, name, operands, spaces, outs, scratch, flops, limit=56):
+    moved = sum(o.size * o.dtype.itemsize for o in operands) + sum(
+        math.prod(o.shape) * jnp.dtype(o.dtype).itemsize for o in outs
+    )
+    return pl.pallas_call(
+        kernel,
+        name=name,
+        in_specs=[spec(s) for s in spaces],
+        out_specs=[spec(VMEM) for _ in outs],
+        out_shape=outs,
+        scratch_shapes=scratch,
+        compiler_params=pltpu.CompilerParams(vmem_limit_bytes=limit * MIB),
+        cost_estimate=pl.CostEstimate(
+            flops=int(flops), bytes_accessed=int(moved), transcendentals=0
+        ),
+    )(*operands)
+
+
+def block_index(scalars, order):
+    place = scalars[1]
+    return lax.bitwise_xor(place, jnp.int32((0, 2, 1, 3)[order]))
+
+
+def early_kernel(mix, earlier, grad, out_grad, out_prev, out_mix):
+    streams = earlier.shape[0]
+    rows = grad.shape[0]
+    step = 128
+
+    out_mix[...] = jnp.zeros_like(out_mix)
+
+    def one(index, carry):
+        here = pl.ds(pl.multiple_of(index * step, step), step)
+        g = grad[here, :].astype(F32)
+        total = None
+        for k in range(streams):
+            e = earlier[k, here, :].astype(F32)
+            out_grad[k, here, :] = (mix[k] * g).astype(BF16)
+            out_mix[k : k + 1, :] += jnp.sum(e * g, axis=0, keepdims=True)
+            total = mix[k] * e if total is None else total + mix[k] * e
+        out_prev[here, :] = total
+        return carry
+
+    lax.fori_loop(0, rows // step, one, 0)
+
+
+def qkv_kernel(hps, batches, has_x, *refs):
+    if has_x:
+        scalars, x, norms, cosine, sine, w0, w1, w2, w3 = refs[:9]
+        outs = refs[9:-3]
+        n1t, weight, pairs = refs[-3:]
+        v = x[...].astype(F32)
+        center = v - jnp.mean(v, axis=-1, keepdims=True)
+        inv = lax.rsqrt(jnp.mean(center * center, axis=-1, keepdims=True) + 1e-05)
+        n1 = center * inv * norms[0:1, :] + norms[1:2, :]
+        n1t[...] = n1.astype(BF16).T
+    else:
+        scalars, n1t, cosine, sine, w0, w1, w2, w3 = refs[:8]
+        outs = refs[8:-2]
+        weight, pairs = refs[-2:]
+    rows = w0.shape[0]
+    for order, piece in enumerate((w0, w1, w2, w3)):
+        start = pl.multiple_of(block_index(scalars, order) * rows, rows)
+        weight[pl.ds(start, rows), :] = piece[...]
+    width = weight.shape[1] // 3
+    size = width // hps
+    half = size // 2
+    tokens = n1t.shape[1] // batches
+    for part in range(3):
+        cols = mm(weight[:, part * width : (part + 1) * width], n1t[...], 0, 0)
+        for head in range(hps):
+            for batch in range(batches):
+                lanes = slice(batch * tokens, (batch + 1) * tokens)
+                top = cols[head * size : head * size + half, lanes]
+                low = cols[head * size + half : (head + 1) * size, lanes]
+                if part < 2:
+                    c = cosine[batch]
+                    s = sine[batch]
+                    top, low = top * c - low * s, low * c + top * s
+                slot = batch * hps + head
+                pairs[slot, part * size : part * size + half, :] = top.astype(BF16)
+                pairs[slot, part * size + half : (part + 1) * size, :] = low.astype(BF16)
+    for delta, out in enumerate(outs):
+        out[...] = pairs[lax.bitwise_xor(scalars[0], jnp.int32(delta))]
+
+
+def attend_kernel(count, scale, ids, *refs):
+    ins = refs[:count]
+    outs = refs[count : 2 * count]
+    ot, lse, qt, kk, vt, scores, top, total, acc = refs[2 * count :]
+    size = qt.shape[1]
+    factor = scale * LOG2E
+    for d in range(count):
+        slot = ids[d]
+        qt[slot] = ins[d][0:size, :]
+        kk[slot] = ins[d][size : 2 * size, :].T
+        vt[slot] = ins[d][2 * size :, :]
+    acc[...] = jnp.zeros_like(acc)
+    total[...] = jnp.zeros_like(total)
+    top[...] = jnp.full_like(top, -1e30)
+    scores[0] = mm(kk[0], qt[0], 1, 0) * factor
+
+    def step(index, carry):
+        i, j = carry
+        last = j == i
+        next_i = jnp.where(last, i + 1, i)
+        next_j = jnp.where(last, 0, j + 1)
+        ahead = jnp.minimum(next_i, count - 1)
+        scores[(index + 1) % 2] = mm(kk[next_j], qt[ahead], 1, 0) * factor
+        s = scores[index % 2]
+        old = jnp.where(j == 0, -1e30, top[...])
+        new = jnp.maximum(old, jnp.max(s, axis=0, keepdims=True))
+        shrink = jnp.exp2(old - new)
+        p = jnp.exp2(s - new)
+        run = total[...] * shrink + jnp.sum(p, axis=0, keepdims=True)
+        out = acc[...] * shrink + mm(vt[j], p.astype(BF16), 1, 0)
+        top[...] = new
+        total[...] = run
+        acc[...] = out
+
+        @pl.when(last)
+        def _():
+            ot[i] = out / run
+            lse[i] = new + jnp.log2(run)
+
+        return (next_i, next_j)
+
+    lax.fori_loop(0, count * (count + 1) // 2, step, (jnp.int32(0), jnp.int32(0)))
+    for d in range(count):
+        outs[d][...] = ot[ids[d]].astype(BF16)
+
+
+def attend_back_kernel(count, scale, ids, *refs):
+    ins = refs[:count]
+    grads = refs[count : 2 * count]
+    ot, lse = refs[2 * count : 2 * count + 2]
+    outs = refs[2 * count + 2 : 3 * count + 2]
+    qt, qq, kt, kk, vv, gt, gg, delta, scores, gains, dq, dk, dv = refs[3 * count + 2 :]
+    size = qt.shape[1]
+    factor = scale * LOG2E
+    for d in range(count):
+        slot = ids[d]
+        block = ins[d][...]
+        q = block[0:size]
+        k = block[size : 2 * size]
+        qt[slot] = q
+        kt[slot] = k
+        qq[slot] = q.T
+        kk[slot] = k.T
+        vv[slot] = block[2 * size :].T
+        g = grads[d][...]
+        gt[slot] = g
+        gg[slot] = g.T
+        delta[slot] = jnp.sum(g.astype(F32) * ot[slot], axis=0, keepdims=True)
+    dq[...] = jnp.zeros_like(dq)
+    dk[...] = jnp.zeros_like(dk)
+    dv[...] = jnp.zeros_like(dv)
+    scores[0] = mm(kk[0], qt[0], 1, 0)
+    gains[0] = mm(vv[0], gt[0], 1, 0)
+
+    def step(index, carry):
+        i, j = carry
+        last = j == i
+        next_i = jnp.where(last, i + 1, i)
+        next_j = jnp.where(last, 0, j + 1)
+        ahead = jnp.minimum(next_i, count - 1)
+        later = (index + 1) % 2
+        scores[later] = mm(kk[next_j], qt[ahead], 1, 0)
+        gains[later] = mm(vv[next_j], gt[ahead], 1, 0)
+        now = index % 2
+        p = jnp.exp2(scores[now] * factor - lse[i])
+        ds = (p * (gains[now] - delta[i])).astype(BF16)
+        dq[i] += mm(kt[j], ds, 1, 0)
+        dk[j] += mm(ds, qq[i], 1, 0)
+        dv[j] += mm(p.astype(BF16), gg[i], 1, 0)
+        return (next_i, next_j)
+
+    lax.fori_loop(0, count * (count + 1) // 2, step, (jnp.int32(0), jnp.int32(0)))
+    for d in range(count):
+        slot = ids[d]
+        outs[d][0:size, :] = (dq[slot] * scale).astype(BF16)
+        outs[d][size : 2 * size, :] = (dk[slot] * scale).T.astype(BF16)
+        outs[d][2 * size :, :] = dv[slot].T.astype(BF16)
+
+
+def gather_rows(scalars, pieces, target, sems, base):
+    copies = []
+    rows = pieces[0].shape[0]
+    for order, piece in enumerate(pieces):
+        start = pl.multiple_of(block_index(scalars, order) * rows, rows)
+        copy = pltpu.make_async_copy(piece, target.at[pl.ds(start, rows), :], sems.at[base + order])
+        copy.start()
+        copies.append(copy)
+    return copies
+
+
+def mlp_kernel(count, stages, hps, batches, scalars, mix, x, grad, norms, *refs):
+    heads = refs[: count * stages]
+    refs = refs[count * stages :]
+    w_out, w_up, w_down = refs[0:4], refs[4:8], refs[8:12]
+    hidden, dhidden, n2_out, mid_out, dmid_out, dmid_low, ot, norm_grads = refs[12:20]
+    head_grads = refs[20 : 20 + count * stages]
+    out_scr, up_scr, down_scr, dn2, got, sems = refs[20 + count * stages :]
+    copies_out = gather_rows(scalars, w_out, out_scr, sems, 0)
+    copies_up = gather_rows(scalars, w_up, up_scr, sems, 4)
+    copies_down = gather_rows(scalars, w_down, down_scr, sems, 8)
+    me = scalars[0]
+    for stage in range(stages):
+        for d in range(count):
+            slot = lax.bitwise_xor(me, jnp.int32(d))
+            batch = lax.div(slot, jnp.int32(hps))
+            head = stage * hps + lax.rem(slot, jnp.int32(hps))
+            ot[batch, head] = heads[stage * count + d][...]
+    for copy in copies_out:
+        copy.wait()
+    tokens = x.shape[0] // batches
+    width = x.shape[1]
+    for batch in range(batches):
+        rows = slice(batch * tokens, (batch + 1) * tokens)
+        attended = ot[batch].reshape(width, tokens)
+        middle = x[rows, :].astype(F32) + mm(attended, out_scr[...], 0, 0)
+        mid_out[rows, :] = middle
+        center = middle - jnp.mean(middle, axis=-1, keepdims=True)
+        inv = lax.rsqrt(jnp.mean(center * center, axis=-1, keepdims=True) + 1e-05)
+        n2_out[rows, :] = (center * inv * norms[2:3, :] + norms[3:4, :]).astype(BF16)
+    for copy in copies_up + copies_down:
+        copy.wait()
+    dn2[...] = jnp.zeros_like(dn2)
+    dy = (mix[mix.shape[0] - 1] * grad[...].astype(F32)).astype(BF16)
+    step = 512 if up_scr.shape[1] % 512 == 0 else 128
+
+    def one(index, carry):
+        here = pl.ds(pl.multiple_of(index * step, step), step)
+        up = up_scr[:, here]
+        u = mm(n2_out[...], up, 1, 0)
+        da = mm(dy, down_scr[here, :], 1, 1)
+        square = u * u
+        bend = jnp.tanh(u * (GELU_C + (GELU_C * GELU_A) * square))
+        gate = 0.5 + 0.5 * bend
+        hidden[:, here] = (u * gate).astype(BF16)
+        slope = gate + (0.5 * u) * (1.0 - bend * bend) * (
+            GELU_C + (3.0 * GELU_C * GELU_A) * square
+        )
+        du = (da * slope).astype(BF16)
+        dhidden[:, here] = du
+        dn2[...] += mm(du, up, 1, 1)
+        return carry
+
+    lax.fori_loop(0, up_scr.shape[1] // step, one, 0)
+    gain_sum = None
+    for batch in range(batches):
+        rows = slice(batch * tokens, (batch + 1) * tokens)
+        middle = mid_out[rows, :]
+        center = middle - jnp.mean(middle, axis=-1, keepdims=True)
+        inv = lax.rsqrt(jnp.mean(center * center, axis=-1, keepdims=True) + 1e-05)
+        z = center * inv
+        dn = dn2[rows, :]
+        part_gain = jnp.sum(dn * z, axis=0, keepdims=True)
+        part_bias = jnp.sum(dn, axis=0, keepdims=True)
+        gain_sum = part_gain if gain_sum is None else gain_sum + part_gain
+        bias_sum = part_bias if batch == 0 else bias_sum + part_bias
+        h = dn * norms[2:3, :]
+        back = inv * (
+            h - jnp.mean(h, axis=-1, keepdims=True) - z * jnp.mean(h * z, axis=-1, keepdims=True)
+        )
+        dmid = mix[mix.shape[0] - 1] * grad[rows, :].astype(F32) + back
+        dmid_out[rows, :] = dmid
+        low = dmid.astype(BF16)
+        dmid_low[rows, :] = low
+        got[batch] = mm(out_scr[...], low, 1, 1).astype(BF16).reshape(got.shape[1:])
+    norm_grads[...] = jnp.zeros_like(norm_grads)
+    norm_grads[0:1, :] = gain_sum
+    norm_grads[1:2, :] = bias_sum
+    for stage in range(stages):
+        for d in range(count):
+            slot = lax.bitwise_xor(me, jnp.int32(d))
+            batch = lax.div(slot, jnp.int32(hps))
+            head = stage * hps + lax.rem(slot, jnp.int32(hps))
+            head_grads[stage * count + d][...] = got[batch, head]
+
+
+def result_kernel(scalars, mix, hidden, mid, prev, grad, w0, w1, w2, w3, out, out_mix, acc):
+    acc[...] = mid[...]
+    rows = w0.shape[0]
+    for order, piece in enumerate((w0, w1, w2, w3)):
+        start = pl.multiple_of(block_index(scalars, order) * rows, rows)
+        acc[...] += mm(hidden[:, pl.ds(start, rows)], piece[...], 1, 0)
+    y = acc[...]
+    out[...] = (prev[...] + mix[mix.shape[0] - 1] * y).astype(BF16)
+    out_mix[...] = jnp.zeros_like(out_mix)
+    out_mix[0:1, :] = jnp.sum(grad[...].astype(F32) * y, axis=0, keepdims=True)
+
+
+def put_pieces(me, value, outs, order, count, lanes):
+    keep, send = outs
+    target = (keep, keep, send, send)[order]
+    rows = value.shape[0] // count
+    low = value.astype(BF16)
+    for sub in range(count):
+        slot = lax.bitwise_xor(me, jnp.int32(sub))
+        target[order % 2, slot, :, lanes] = low[sub * rows : (sub + 1) * rows, :]
+
+
+def down_grad_kernel(count, scalars, mix, hidden, grad, keep, send):
+    dy = (mix[mix.shape[0] - 1] * grad[...].astype(F32)).astype(BF16)
+    rows = keep.shape[1] * keep.shape[2]
+    for order in range(4):
+        start = pl.multiple_of(block_index(scalars, order) * rows, rows)
+        value = mm(hidden[:, pl.ds(start, rows)], dy, 0, 0)
+        put_pieces(scalars[0], value, (keep, send), order, count, slice(None))
+
+
+def up_out_grad_kernel(count, scalars, n2, dhidden, ot, dmid, keep, send, left, left_out):
+    batches = ot.shape[0]
+    width = n2.shape[1]
+    tokens = ot.shape[3]
+    rows = width // 4
+    flipped = n2[...].T
+    for order in range(4):
+        here = pl.ds(pl.multiple_of(block_index(scalars, order) * rows, rows), rows)
+        left_out[order * rows : (order + 1) * rows, :] = jnp.zeros(
+            (rows, left_out.shape[1]), BF16
+        )
+    left_out[...] = flipped
+    for order in range(4):
+        here = pl.ds(pl.multiple_of(block_index(scalars, order) * rows, rows), rows)
+        left[order * rows : (order + 1) * rows, :] = left_out[here, :]
+    inner = dhidden.shape[1]
+    step = 768 if inner % 768 == 0 else 256
+
+    def one(index, carry):
+        start = pl.multiple_of(index * step, step)
+        value = mm(left[...], dhidden[:, pl.ds(start, step)], 1, 0)
+        for order in range(4):
+            put_pieces(
+                scalars[0],
+                value[order * rows : (order + 1) * rows, :],
+                (keep, send),
+                order,
+                count,
+                pl.ds(start, step),
+            )
+        return carry
+
+    lax.fori_loop(0, inner // step, one, 0)
+    for batch in range(batches):
+        left_out[:, batch * tokens : (batch + 1) * tokens] = ot[batch].reshape(width, tokens)
+    for order in range(4):
+        here = pl.ds(pl.multiple_of(block_index(scalars, order) * rows, rows), rows)
+        left[order * rows : (order + 1) * rows, :] = left_out[here, :]
+    value = mm(left[...], dmid[...], 1, 0)
+    for order in range(4):
+        put_pieces(
+            scalars[0],
+            value[order * rows : (order + 1) * rows, :],
+            (keep, send),
+            order,
+            count,
+            slice(inner, inner + value.shape[1]),
+        )
+
+
+def in_grad_kernel(count, hps, scalars, cosine, sine, n1t, *refs):
+    grads = refs[:count]
+    dt, keep, send, left = refs[count:]
+    batches = dt.shape[0]
+    size = dt.shape[3]
+    half = size // 2
+    tokens = dt.shape[4]
+    me = scalars[0]
+    for d in range(count):
+        slot = lax.bitwise_xor(me, jnp.int32(d))
+        batch = lax.div(slot, jnp.int32(hps))
+        head = lax.rem(slot, jnp.int32(hps))
+        c = cosine[batch]
+        s = sine[batch]
+        for part in range(2):
+            top = grads[d][part * size : part * size + half, :].astype(F32)
+            low = grads[d][part * size + half : (part + 1) * size, :].astype(F32)
+            dt[batch, part, head, 0:half, :] = (top * c + low * s).astype(BF16)
+            dt[batch, part, head, half:size, :] = (low * c - top * s).astype(BF16)
+        dt[batch, 2, head] = grads[d][2 * size :, :]
+    width = n1t.shape[0]
+    rows = width // 4
+    for order in range(4):
+        here = pl.ds(pl.multiple_of(block_index(scalars, order) * rows, rows), rows)
+        left[order * rows : (order + 1) * rows, :] = n1t[here, :]
+    cols = 3 * hps * size
+    value = None
+    for batch in range(batches):
+        term = mm(
+            left[:, batch * tokens : (batch + 1) * tokens], dt[batch].reshape(cols, tokens), 1, 1
+        )
+        value = term if value is None else value + term
+    for order in range(4):
+        put_pieces(
+            me, value[order * rows : (order + 1) * rows, :], (keep, send), order, count, slice(None)
+        )
+
+
+def input_grad_kernel(stages, scalars, x, norms, dmid, *refs):
+    dts = refs[:stages]
+    pieces = refs[stages : stages + 4 * stages]
+    out, norm_grads, weights, sems = refs[5 * stages :]
+    copies = []
+    for stage in range(stages):
+        copies.append(
+            gather_rows(
+                scalars,
+                pieces[4 * stage : 4 * stage + 4],
+                weights.at[stage],
+                sems,
+                4 * stage,
+            )
+        )
+    for group in copies:
+        for copy in group:
+            copy.wait()
+    batches = dts[0].shape[0]
+    tokens = dts[0].shape[4]
+    cols = weights.shape[2]
+    gain_sum = bias_sum = None
+    for batch in range(batches):
+        rows = slice(batch * tokens, (batch + 1) * tokens)
+        dnt = None
+        for stage in range(stages):
+            term = mm(weights[stage], dts[stage][batch].reshape(cols, tokens), 1, 0)
+            dnt = term if dnt is None else dnt + term
+        dn = dnt.T
+        v = x[rows, :].astype(F32)
+        center = v - jnp.mean(v, axis=-1, keepdims=True)
+        inv = lax.rsqrt(jnp.mean(center * center, axis=-1, keepdims=True) + 1e-05)
+        z = center * inv
+        part_gain = jnp.sum(dn * z, axis=0, keepdims=True)
+        part_bias = jnp.sum(dn, axis=0, keepdims=True)
+        gain_sum = part_gain if batch == 0 else gain_sum + part_gain
+        bias_sum = part_bias if batch == 0 else bias_sum + part_bias
+        h = dn * norms[0:1, :]
+        back = inv * (
+            h - jnp.mean(h, axis=-1, keepdims=True) - z * jnp.mean(h * z, axis=-1, keepdims=True)
+        )
+        out[rows, :] = (dmid[rows, :] + back).astype(BF16)
+    norm_grads[...] = jnp.zeros_like(norm_grads)
+    norm_grads[0:1, :] = gain_sum
+    norm_grads[1:2, :] = bias_sum
+
+
+def place_kernel(count, groups, scalars, *refs):
+    pieces = refs[: count * len(groups)]
+    outs = refs[count * len(groups) :]
+    for g, moves in enumerate(groups):
+        for d in range(count):
+            slot = lax.bitwise_xor(scalars[0], jnp.int32(d))
+            piece = pieces[g * count + d]
+            for out, begin, wide, to in moves:
+                outs[out][slot, :, to : to + wide] = piece[:, begin : begin + wide].astype(F32)
+
+
+def exchange(value, axis, bit):
+    size = lax.axis_size(axis)
+    return lax.ppermute(value, axis, [(i, i ^ bit) for i in range(size)])
+
+
+def added(left, right):
+    return (left.astype(F32) + right.astype(F32)).astype(BF16)
+
+
+def reduce_blocks(keep, send):
+    got = exchange(send, "fsdp", 1)
+    passed = added(keep[1], got[1])
+    own = added(keep[0], got[0])
+    own = added(own, exchange(passed, "fsdp", 2))
+    bit = 1
+    while bit < lax.axis_size("ctx"):
+        pairs = own.reshape(own.shape[0] // 2, 2, *own.shape[1:])
+        own = added(pairs[:, 0], exchange(pairs[:, 1], "ctx", bit))
+        bit *= 2
+    return own[0]
+
+
+def gather_blocks(own):
+    count = lax.axis_size("ctx")
+    held = {0: own}
+    bit = count // 2
+    while bit:
+        for index in list(held):
+            held[index ^ bit] = exchange(held[index], "ctx", bit)
+        bit //= 2
+    return [held[index] for index in range(count)]
+
+
+def gathered(shard):
+    other_chip = exchange(shard, "fsdp", 2)
+    return [shard, other_chip, exchange(shard, "fsdp", 1), exchange(other_chip, "fsdp", 1)]
+
+
+def head_body(
+    inputs,
+    earlier,
+    input_proj,
+    output_proj,
+    up_proj,
+    down_proj,
+    norm1_gain,
+    norm1_bias,
+    norm2_gain,
+    norm2_bias,
+    mixing,
+    block_order,
+    grad_next,
+):
+    batches, tokens, width = inputs.shape
+    rows = batches * tokens
+    heads = HEADS
+    size = width // heads
+    scale = size ** (-0.5)
+    streams = earlier.shape[0]
+    count = lax.axis_size("ctx")
+    hps = count // batches
+    stages = heads // hps
+    inner = down_proj.shape[0] * 4
+    me = lax.axis_index("ctx").astype(jnp.int32)
+    place = lax.axis_index("fsdp").astype(jnp.int32)
+    scalars = jnp.stack([me, place])
+    own_batch = me // hps
+    ids = block_order[own_batch][me ^ jnp.arange(count, dtype=jnp.int32)].astype(jnp.int32)
+    x = inputs.reshape(rows, width)
+    grad = grad_next.reshape(rows, width)
+
+    norm_stack = jnp.stack([norm1_gain, norm1_bias, norm2_gain, norm2_bias])
+    norms = lax.all_gather(norm_stack, "fsdp", axis=1, tiled=True)
+    chunks = input_proj.reshape(width // 4, 3, stages, hps * size)
+    w_in = [gathered(chunks[:, :, s].reshape(width // 4, 3 * hps * size)) for s in range(stages)]
+    w_out = gathered(output_proj)
+    w_up = gathered(up_proj)
+    w_down = gathered(down_proj)
+
+    half = size // 2
+    own_blocks = block_order[:, me]
+    positions = (own_blocks[:, None] * tokens + lax.iota(jnp.int32, tokens)[None]).astype(F32)
+    freqs = jnp.exp(lax.iota(F32, half) * (-2.0 * math.log(10000.0) / size))
+    angle = freqs[None, :, None] * positions[:, None, :]
+    cosine = jnp.cos(angle)
+    sine = jnp.sin(angle)
+
+    grad_earlier, prev, mix_early = run_kernel(
+        early_kernel,
+        "early",
+        [mixing, earlier.reshape(streams, rows, width), grad],
+        [SMEM, VMEM, VMEM],
+        [
+            shape_of((streams, rows, width), BF16),
+            shape_of((rows, width), F32),
+            shape_of((8, width), F32),
+        ],
+        [],
+        6 * streams * rows * width,
+    )
+
+    pair_shape = shape_of((3 * size, tokens), BF16)
+    held = []
+    n1t = None
+    for s in range(stages):
+        first = s == 0
+        operands = [scalars] + ([x, norms] if first else [n1t]) + [cosine, sine] + w_in[s]
+        outs = [pair_shape] * count + ([shape_of((width, rows), BF16)] if first else [])
+        result = run_kernel(
+            functools.partial(qkv_kernel, hps, batches, first),
+            "qkv",
+            operands,
+            [SMEM] + [VMEM] * (len(operands) - 1),
+            outs,
+            [
+                pltpu.VMEM((width, 3 * hps * size), BF16),
+                pltpu.VMEM((count, 3 * size, tokens), BF16),
+            ],
+            2 * rows * width * 3 * hps * size,
+        )
+        if first:
+            n1t = result[count]
+        sent = result[:count]
+        held.append([sent[0]] + [exchange(sent[d], "ctx", d) for d in range(1, count)])
+
+    tiles = count * (count + 1) // 2
+    one = tokens * tokens * size * 2
+    head_shape = shape_of((size, tokens), BF16)
+    attended = []
+    saved = []
+    for s in range(stages):
+        result = run_kernel(
+            functools.partial(attend_kernel, count, scale),
+            "attend",
+            [ids] + held[s],
+            [SMEM] + [VMEM] * count,
+            [head_shape] * count
+            + [shape_of((count, size, tokens), F32), shape_of((count, 1, tokens), F32)],
+            [
+                pltpu.VMEM((count, size, tokens), BF16),
+                pltpu.VMEM((count, tokens, size), BF16),
+                pltpu.VMEM((count, size, tokens), BF16),
+                pltpu.VMEM((2, tokens, tokens), F32),
+                pltpu.VMEM((1, tokens), F32),
+                pltpu.VMEM((1, tokens), F32),
+                pltpu.VMEM((size, tokens), F32),
+            ],
+            4 * 2 * one * tiles,
+        )
+        saved.append(result[count:])
+        attended += [result[0]] + [exchange(result[d], "ctx", d) for d in range(1, count)]
+
+    mlp_operands = [scalars, mixing, x, grad, norms] + attended + w_out + w_up + w_down
+    result = run_kernel(
+        functools.partial(mlp_kernel, count, stages, hps, batches),
+        "mlp",
+        mlp_operands,
+        [SMEM, SMEM, VMEM, VMEM, VMEM] + [VMEM] * (count * stages) + [ANY] * 12,
+        [
+            shape_of((rows, inner), BF16),
+            shape_of((rows, inner), BF16),
+            shape_of((rows, width), BF16),
+            shape_of((rows, width), F32),
+            shape_of((rows, width), F32),
+            shape_of((rows, width), BF16),
+            shape_of((batches, heads, size, tokens), BF16),
+            shape_of((8, width), F32),
+        ]
+        + [head_shape] * (count * stages),
+        [
+            pltpu.VMEM((width, width), BF16),
+            pltpu.VMEM((width, inner), BF16),
+            pltpu.VMEM((inner, width), BF16),
+            pltpu.VMEM((rows, width), F32),
+            pltpu.VMEM((batches, heads, size, tokens), BF16),
+            pltpu.SemaphoreType.DMA((12,)),
+        ],
+        6 * rows * width * inner,
+    )
+    hidden, dhidden, n2, mid, dmid, dmid_low, ot, norm2_grads = result[:8]
+    head_grads = result[8:]
+    sent_grads = []
+    for s in range(stages):
+        mine = head_grads[s * count : (s + 1) * count]
+        sent_grads.append([mine[0]] + [exchange(mine[d], "ctx", d) for d in range(1, count)])
+
+    sub = inner // 4 // count
+    down_keep, down_send = run_kernel(
+        functools.partial(down_grad_kernel, count),
+        "down_grad",
+        [scalars, mixing, hidden, grad],
+        [SMEM, SMEM, VMEM, VMEM],
+        [shape_of((2, count, sub, width), BF16)] * 2,
+        [],
+        2 * rows * width * inner,
+    )
+    down_pieces = gather_blocks(reduce_blocks(down_keep, down_send))
+    thin = width // 4 // count
+    up_keep, up_send = run_kernel(
+        functools.partial(up_out_grad_kernel, count),
+        "up_out_grad",
+        [scalars, n2, dhidden, ot, dmid_low],
+        [SMEM] + [VMEM] * 4,
+        [shape_of((2, count, thin, inner + width), BF16)] * 2,
+        [pltpu.VMEM((width, rows), BF16), pltpu.VMEM((width, rows), BF16)],
+        2 * rows * width * (inner + width),
+    )
+    up_pieces = gather_blocks(reduce_blocks(up_keep, up_send))
+
+    next_input, mix_last = run_kernel(
+        result_kernel,
+        "result",
+        [scalars, mixing, hidden, mid, prev, grad] + w_down,
+        [SMEM, SMEM] + [VMEM] * 8,
+        [shape_of((rows, width), BF16), shape_of((8, width), F32)],
+        [pltpu.VMEM((rows, width), F32)],
+        2 * rows * width * inner,
+    )
+
+    dts = []
+    in_pieces = []
+    cols = 3 * hps * size
+    for s in range(stages):
+        back = run_kernel(
+            functools.partial(attend_back_kernel, count, scale),
+            "attend_back",
+            [ids] + held[s] + sent_grads[s] + list(saved[s]),
+            [SMEM] + [VMEM] * (2 * count + 2),
+            [pair_shape] * count,
+            [
+                pltpu.VMEM((count, size, tokens), BF16),
+                pltpu.VMEM((count, tokens, size), BF16),
+                pltpu.VMEM((count, size, tokens), BF16),
+                pltpu.VMEM((count, tokens, size), BF16),
+                pltpu.VMEM((count, tokens, size), BF16),
+                pltpu.VMEM((count, size, tokens), BF16),
+                pltpu.VMEM((count, tokens, size), BF16),
+                pltpu.VMEM((count, 1, tokens), F32),
+                pltpu.VMEM((2, tokens, tokens), F32),
+                pltpu.VMEM((2, tokens, tokens), F32),
+                pltpu.VMEM((count, size, tokens), F32),
+                pltpu.VMEM((count, tokens, size), F32),
+                pltpu.VMEM((count, tokens, size), F32),
+            ],
+            4 * 5 * one * tiles,
+        )
+        arrived = [back[0]] + [exchange(back[d], "ctx", d) for d in range(1, count)]
+        dt, keep, send = run_kernel(
+            functools.partial(in_grad_kernel, count, hps),
+            "in_grad",
+            [scalars, cosine, sine, n1t] + arrived,
+            [SMEM] + [VMEM] * (3 + count),
+            [shape_of((batches, 3, hps, size, tokens), BF16)]
+            + [shape_of((2, count, thin, cols), BF16)] * 2,
+            [pltpu.VMEM((width, rows), BF16)],
+            2 * rows * width * cols,
+        )
+        dts.append(dt)
+        in_pieces += gather_blocks(reduce_blocks(keep, send))
+
+    flat_in = [piece for pieces in w_in for piece in pieces]
+    grad_input, norm1_grads = run_kernel(
+        functools.partial(input_grad_kernel, stages),
+        "input_grad",
+        [scalars, x, norms, dmid] + dts + flat_in,
+        [SMEM] + [VMEM] * (3 + stages) + [ANY] * (4 * stages),
+        [shape_of((rows, width), BF16), shape_of((8, width), F32)],
+        [pltpu.VMEM((stages, width, cols), BF16), pltpu.SemaphoreType.DMA((4 * stages,))],
+        2 * rows * width * 3 * width,
+    )
+
+    small = jnp.concatenate(
+        [norm1_grads[:2], norm2_grads[:2], mix_early[:streams], mix_last[:1]], axis=0
+    )
+    for axis in ("fsdp", "ctx"):
+        bit = 1
+        while bit < lax.axis_size(axis):
+            small = small + exchange(small, axis, bit)
+            bit *= 2
+    norm_total = lax.dynamic_slice_in_dim(small[:4], place * (width // 4), width // 4, 1)
+    mix_total = jnp.sum(small[4:], axis=1)
+
+    (grad_down,) = run_kernel(
+        functools.partial(place_kernel, count, (((0, 0, width, 0),),)),
+        "place_down",
+        [scalars] + down_pieces,
+        [SMEM] + [VMEM] * count,
+        [shape_of((count, sub, width), F32)],
+        [],
+        0,
+    )
+    grad_up, grad_out = run_kernel(
+        functools.partial(place_kernel, count, (((0, 0, inner, 0), (1, inner, width, 0)),)),
+        "place_up",
+        [scalars] + up_pieces,
+        [SMEM] + [VMEM] * count,
+        [shape_of((count, thin, inner), F32), shape_of((count, thin, width), F32)],
+        [],
+        0,
+    )
+    wide = hps * size
+    groups = tuple(
+        tuple((0, part * wide, wide, part * width + s * wide) for part in range(3))
+        for s in range(stages)
+    )
+    (grad_in,) = run_kernel(
+        functools.partial(place_kernel, count, groups),
+        "place_in",
+        [scalars] + in_pieces,
+        [SMEM] + [VMEM] * (count * stages),
+        [shape_of((count, thin, 3 * width), F32)],
+        [],
+        0,
+    )
+    return (
+        next_input.reshape(batches, tokens, width),
+        grad_input.reshape(batches, tokens, width),
+        grad_earlier.reshape(streams, batches, tokens, width),
+        grad_in.reshape(width // 4, 3 * width),
+        grad_out.reshape(width // 4, width),
+        grad_up.reshape(width // 4, inner),
+        grad_down.reshape(inner // 4, width),
+        norm_total[0],
+        norm_total[1],
+        norm_total[2],
+        norm_total[3],
+        mix_total,
+    )
+
+
+def heads_fit(batches):
+    count = lax.axis_size("ctx")
+    return (
+        lax.axis_size("fsdp") == 4
+        and count & (count - 1) == 0
+        and count % batches == 0
+        and HEADS % max(count // batches, 1) == 0
+    )
+
+
+def either_body(inputs, *rest):
+    return (head_body if heads_fit(inputs.shape[0]) else body)(inputs, *rest)
+
+
 def solution(mesh):
     placed = (
         P("fsdp", "ctx", None),
@@ -390,7 +1219,7 @@
         P("fsdp", "ctx", None),
     )
     return jax.shard_map(
-        body,
+        either_body,
         mesh=mesh,
         in_specs=placed,
         out_specs=(

time: 1620 us -> 756 us (0.47)
  waiting for transfers between devices: 1070 us -> 257 us
  Pallas kernels: 0 us -> 212 us
  matrix products: 135 us -> 0 us
  starting transfers between devices: 80.6 us -> 202 us
  other arithmetic: 124 us -> 5.57 us
  local copies, waits for them, and re-layouts: 107 us -> 20.9 us
  loops' own time: 40.1 us -> 0 us
  between operations: 20 us -> 2.73 us
    all_gather x8 -> x0, waiting for transfers between devices: 255 us -> none  [the longest x2 98.5 us: body(): piece_values = lax.all_gather(local_values, 'ctx', axis=0, tiled=True)]
    psum x1 -> x0, waiting for transfers between devices: 213 us -> none  [body(): totals = lax.psum(totals, 'ctx')]
    pallas_call x0 -> x21, Pallas kernels: none -> 212 us  [run_kernel(): pl.pallas_call(kernel, name=name, in_specs=[spec(s) for s in spaces], out...]
    reduce_scatter x8 -> x0, waiting for transfers between devices: 194 us -> none  [the longest x2 97.4 us: body(): lax.psum_scatter(grad_terms[3].astype(jnp.bfloat16), 'fsdp', scatter_dime...]
    ppermute x60 -> x167, waiting for transfers between devices: 396 us -> 257 us  [exchange(): return lax.ppermute(value, axis, [(i, i ^ bit) for i in range(size)])]
    dot_general x80 -> x0, matrix products: 135 us -> none  [the longest x2 14.2 us: body(): jnp.einsum('rf,rd->fd', hidden_b, grad_result_b, preferred_element_type=j...]
    ppermute x60 -> x167, starting transfers between devices: 79.2 us -> 202 us  [exchange(): return lax.ppermute(value, axis, [(i, i ^ bit) for i in range(size)])]
    convert_element_type x66 -> x16, other arithmetic: 58.7 us -> 2.74 us  [the longest x15 2.66 us: added(): return (left.astype(F32) + right.astype(F32)).astype(BF16)]
  transfers between devices with their start and end apart: 79 -> 167, of which waited for: 73 -> 53; matrix products, arithmetic and copies ran while one was open for 20% -> 1% of each run, Pallas kernels for 0% -> 24%
where the time goes in v1:
time: 756 us; the launch traced here: 750 us
  waiting for transfers between devices  257 us (34%)
  Pallas kernels  212 us (28%)
  starting transfers between devices  202 us (27%)
  blocking collectives  50.1 us (7%)
  local copies, waits for them, and re-layouts  20.9 us (3%)
    ppermute x167, waiting for transfers between devices, exchange(): return lax.ppermute(value, axis, [(i, i ^ bit) for i in range(size)])  257 us
    pallas_call x21, Pallas kernels, run_kernel(): pl.pallas_call(kernel, name=name, in_specs=[spec(s) for s in spaces], out...  212 us
    ppermute x167, starting transfers between devices, exchange(): return lax.ppermute(value, axis, [(i, i ^ bit) for i in range(size)])  202 us
    all_gather x1, blocking collectives, head_body(): norms = lax.all_gather(norm_stack, 'fsdp', axis=1, tiled=True)  50.1 us
  transfers between devices with their start and end apart: 167, of which 53 were waited for; matrix products, arithmetic and copies ran while one was open for 1% of the time, Pallas kernels for 24%

profile of v1, /device:TPU:0, one launch (start us, length us, event | category | flops | bytes accessed | tf_op | source)
XLA Modules:
  0.0 750.3 jit_solution(244295857808726660)
XLA Ops:
  12.9 5.2 collective-permute-done.refs_6_.refs_4_
  37.7 50.1 %all-gather = f32[4,192,4]{1,2,0:T(4,128)S(1)} all-gather(f32[1,192,4]{1,2,0:T(4,128)S(1)} %maximum_bitcast_fusion), channel_id=1, replica_groups=mesh['ctx'=8,'fsdp'=4] {'fsdp'}, dimensions={0}, use_global_device_ids=true | all-gather | bytes 15360 | tf_op jit(solution)/shard_map/all_gather | solution.py:933
  131.3 6.1 collective-permute-done.23.refs_4_
  165.1 17.1 %attend.5 = (bf16[64,256]{1,0:T(8,128)(2,1)}, bf16[64,256]{1,0:T(8,128)(2,1)}, bf16[64,256]{1,0:T(8,128)(2,1)}, bf16[64,256]{1,0:T(8,128)(2,1)}, bf16[64,256]{1,...) custom-call(s32[8]{0:T(128)} %gather_fusion, ...), custom_call_target="tpu_custom_call" | custom-call | flops 2415919104 | bytes 1581088 | tf_op jit(solution)/shard_map/attend/pallas_call | solution.py:408
  202.1 6.2 collective-permute-done.48.refs_21_
  208.4 5.9 collective-permute-done.49.refs_22_
  216.1 16.9 %attend.4 = (bf16[64,256]{1,0:T(8,128)(2,1)}, bf16[64,256]{1,0:T(8,128)(2,1)}, bf16[64,256]{1,0:T(8,128)(2,1)}, bf16[64,256]{1,0:T(8,128)(2,1)}, bf16[64,256]{1,...) custom-call(s32[8]{0:T(128)} %gather_fusion, ...), custom_call_target="tpu_custom_call" | custom-call | flops 2415919104 | bytes 1581088 | tf_op jit(solution)/shard_map/attend/pallas_call | solution.py:408
  241.5 5.1 collective-permute-done.29.refs_11_
  266.9 16.9 %attend.3 = (bf16[64,256]{1,0:T(8,128)(2,1)}, bf16[64,256]{1,0:T(8,128)(2,1)}, bf16[64,256]{1,0:T(8,128)(2,1)}, bf16[64,256]{1,0:T(8,128)(2,1)}, bf16[64,256]{1,...) custom-call(s32[8]{0:T(128)} %gather_fusion, ...), custom_call_target="tpu_custom_call" | custom-call | flops 2415919104 | bytes 1581088 | tf_op jit(solution)/shard_map/attend/pallas_call | solution.py:408
  297.5 5.1 collective-permute-done.13.refs_4_
  302.6 5.9 collective-permute-done.14.refs_5_
  308.6 5.9 collective-permute-done.15.refs_6_
  315.8 5.5 collective-permute-done.16.refs_7_
  323.5 19.1 %mlp.1 = (bf16[512,3072]{1,0:T(8,128)(2,1)}, bf16[512,3072]{1,0:T(8,128)(2,1)}, bf16[512,768]{1,0:T(8,128)(2,1)}, f32[512,768]{1,0:T(8,128)}, f32[512,768]{1,0:T...) custom-call(s32[2]{0:T(128)} %pad_add_fusion.refs_0_.scalars, ...), custom_call_target="tpu_custom_call" | custom-call | flops 7247757312 | bytes 25595932 | tf_op jit(solution)/shard_map/mlp/pallas_call | solution.py:408
  361.7 24.5 %attend_back.5 = (bf16[192,256]{1,0:T(8,128)(2,1)}, bf16[192,256]{1,0:T(8,128)(2,1)}, bf16[192,256]{1,0:T(8,128)(2,1)}, bf16[192,256]{1,0:T(8,128)(2,1)}, bf16[1...) custom-call(s32[8]{0:T(128)} %gather_fusion, ...), custom_call_target="tpu_custom_call" | custom-call | flops 6039797760 | bytes 2367520 | tf_op jit(solution)/shard_map/attend_back/pallas_call | solution.py:408
  403.0 5.4 early.1
  416.6 24.5 %attend_back.4 = (bf16[192,256]{1,0:T(8,128)(2,1)}, bf16[192,256]{1,0:T(8,128)(2,1)}, bf16[192,256]{1,0:T(8,128)(2,1)}, bf16[192,256]{1,0:T(8,128)(2,1)}, bf16[1...) custom-call(s32[8]{0:T(128)} %gather_fusion, ...), custom_call_target="tpu_custom_call" | custom-call | flops 6039797760 | bytes 2367520 | tf_op jit(solution)/shard_map/attend_back/pallas_call | solution.py:408
  447.7 24.9 %attend_back.3 = (bf16[192,256]{1,0:T(8,128)(2,1)}, bf16[192,256]{1,0:T(8,128)(2,1)}, bf16[192,256]{1,0:T(8,128)(2,1)}, bf16[192,256]{1,0:T(8,128)(2,1)}, bf16[1...) custom-call(s32[8]{0:T(128)} %gather_fusion, ...), custom_call_target="tpu_custom_call" | custom-call | flops 6039797760 | bytes 2367520 | tf_op jit(solution)/shard_map/attend_back/pallas_call | solution.py:408
  480.3 8.2 %result.1 = (bf16[512,768]{1,0:T(8,128)(2,1)}, f32[8,768]{1,0:T(8,128)}) custom-call(s32[2]{0:T(128)} %pad_add_fusion.refs_0_.scalars, f32[5]{0:T(128)} %mix.7, bf16[512,3072]{1,0:T(8,128)(2,1)} %get-tuple-element.194.hidden, f32[512,768]{1,0:T(8,128)} %get-tuple-element.195.mid, f32[512,768]{1,0:T(8,128)} %get-tuple-element.196.prev, ...), custom_call_target="tpu_custom_call" | custom-call | flops 2415919104 | bytes 12607516 | tf_op jit(solution)/shard_map/result/pallas_call | solution.py:408
  512.9 8.3 %input_grad.1 = (bf16[512,768]{1,0:T(8,128)(2,1)}, f32[8,768]{1,0:T(8,128)}) custom-call(s32[2]{0:T(128)} %pad_add_fusion.refs_0_.scalars, bf16[512,768]{1,0:T(8,128)(2,1)} %bitcast.285, f32[4,768]{1,0:T(4,128)} %bitcast.294, f32[512,768]{1,0:T(8,128)} %get-tuple-element.198.dmid, bf16[2,3,4,64,256]{4,3,2,1,0:T(8,128)(2,1)} %get-tuple-element.217.refs_0_, ...), custom_call_target="tpu_custom_call" | custom-call | flops 1811939328 | bytes 9080840 | tf_op jit(solution)/shard_map/input_grad/pallas_call | solution.py:408
  527.8 6.3 down_grad.1
  534.7 9.6 %up_out_grad.1 = (bf16[2,8,24,3840]{3,2,1,0:T(8,128)(2,1)}, bf16[2,8,24,3840]{3,2,1,0:T(8,128)(2,1)}) custom-call(s32[2]{0:T(128)} %pad_add_fusion.refs_0_.scalars, bf16[512,768]{1,0:T(8,128)(2,1)} %get-tuple-element.264.n2, bf16[512,3072]{1,0:T(8,128)(2,1)} %get-tuple-element.265.dhidden, bf16[2,12,64,256]{3,2,1,0:T(8,128)(2,1)} %get-tuple-element.266.ot, ...), custom_call_target="tpu_custom_call" | custom-call | flops 3019898880 | bytes 11403272 | tf_op jit(solution)/shard_map/up_out_grad/pallas_call | solution.py:408
  550.5 7.6 %collective-permute-done.127 = bf16[8,24,768]{2,1,0:T(8,128)(2,1)S(1)} collective-permute-done((bf16[8,24,768]{2,1,0:T(8,128)(2,1)S(1)}, bf16[8,24,768]{2,1,0:T(8,128)(2,1)S(1)}, u32[]{:S(2)}, u32[]{:S(2)}) %collective-permute-start.127) | collective-permute-done | bytes 294944 | tf_op jit(solution)/shard_map/ppermute | solution.py:863
  558.7 5.8 collective-permute-done.115
  564.9 5.1 collective-permute-done.103
  587.8 24.1 %collective-permute-done.151 = bf16[8,96,768]{2,1,0:T(8,128)(2,1)S(1)} collective-permute-done((bf16[8,96,768]{2,1,0:T(8,128)(2,1)S(1)}, bf16[8,96,768]{2,1,0:T(8,128)(2,1)S(1)}, u32[]{:S(2)}, u32[]{:S(2)}) %collective-permute-start.151) | collective-permute-done | bytes 1179680 | tf_op jit(solution)/shard_map/ppermute | solution.py:863
  614.5 24.4 %collective-permute-done.139 = bf16[8,24,3840]{2,1,0:T(8,128)(2,1)S(1)} collective-permute-done((bf16[8,24,3840]{2,1,0:T(8,128)(2,1)S(1)}, bf16[8,24,3840]{2,1,0:T(8,128)(2,1)S(1)}, u32[]{:S(2)}, u32[]{:S(2)}) %collective-permute-start.139) | collective-permute-done | bytes 1474592 | tf_op jit(solution)/shard_map/ppermute | solution.py:863
  643.8 11.3 %collective-permute-done.152 = bf16[4,96,768]{2,1,0:T(8,128)(2,1)S(1)} collective-permute-done((bf16[4,96,768]{2,1,0:T(8,128)(2,1)S(1)}, bf16[4,96,768]{2,1,0:T(8,128)(2,1)S(1)}, u32[]{:S(2)}, u32[]{:S(2)}) %collective-permute-start.152) | collective-permute-done | bytes 589856 | tf_op jit(solution)/shard_map/ppermute | solution.py:863
  655.8 9.7 %collective-permute-done.140 = bf16[4,24,3840]{2,1,0:T(8,128)(2,1)S(1)} collective-permute-done((bf16[4,24,3840]{2,1,0:T(8,128)(2,1)S(1)}, bf16[4,24,3840]{2,1,0:T(8,128)(2,1)S(1)}, u32[]{:S(2)}, u32[]{:S(2)}) %collective-permute-start.140) | collective-permute-done | bytes 737312 | tf_op jit(solution)/shard_map/ppermute | solution.py:863
  667.8 5.2 collective-permute-done.153
  673.4 5.2 collective-permute-done.141
  692.3 5.2 collective-permute-done.142
  (692 shorter events, 361.4 us)
Async XLA Ops:
  25.1 139.5 %collective-permute-start.57 = (bf16[768,768]{1,0:T(8,128)(2,1)S(1)}, bf16[768,768]{1,0:T(8,128)(2,1)S(1)}, u32[]{:S(2)}, u32[]{:S(2)}) collective-permute-start(bf16[768,768]{1,0:T(8,128)(2,1)S(1)} %copy-done.2), channel_id=1, source_target_pairs={{0,2},{1,3},{2,0},{3,1},{4,6},{5,7},{6,4},{7,5},{8,10},{9,11},{10,... | collective-permute-start | bytes 3538952 | tf_op jit(solution)/shard_map/ppermute | solution.py:863
  30.8 133.9 %collective-permute-start.54 = (bf16[192,3072]{1,0:T(8,128)(2,1)}, bf16[192,3072]{1,0:T(8,128)(2,1)}, u32[]{:S(2)}, u32[]{:S(2)}) collective-permute-start(bf16[192,3072]{1,0:T(8,128)(2,1)} %refs_28_.1), channel_id=1, source_target_pairs={{0,2},{1,3},{2,0},{3,1},{4,6},{5,7},{6,4},{7,5},{8,10},{9,11},{10,... | collective-permute-start | bytes 3538952 | tf_op jit(solution)/shard_map/ppermute | solution.py:863
  33.5 54.9 %collective-permute-start.36 = (bf16[192,768]{1,0:T(8,128)(2,1)}, bf16[192,768]{1,0:T(8,128)(2,1)}, u32[]{:S(2)}, u32[]{:S(2)}) collective-permute-start(bf16[192,768]{1,0:T(8,128)(2,1)} %copy-done.16), channel_id=1, source_target_pairs={{0,1},{1,0},{2,3},{3,2},{4,5},{5,4},{6,7},{7,6},{8,9},{9,8},{10,11... | collective-permute-start | bytes 884744 | tf_op jit(solution)/shard_map/ppermute | solution.py:863
  37.1 59.8 %collective-permute-start.52 = (bf16[192,768]{1,0:T(8,128)(2,1)}, bf16[192,768]{1,0:T(8,128)(2,1)}, u32[]{:S(2)}, u32[]{:S(2)}) collective-permute-start(bf16[192,768]{1,0:T(8,128)(2,1)} %refs_24_.1), channel_id=1, source_target_pairs={{0,1},{1,0},{2,3},{3,2},{4,5},{5,4},{6,7},{7,6},{8,9},{9,8},{10,11... | collective-permute-start | bytes 884744 | tf_op jit(solution)/shard_map/ppermute | solution.py:863
  37.1 61.7 %collective-permute-start.19 = (bf16[192,768]{1,0:T(8,128)(2,1)}, bf16[192,768]{1,0:T(8,128)(2,1)}, u32[]{:S(2)}, u32[]{:S(2)}) collective-permute-start(bf16[192,768]{1,0:T(8,128)(2,1)} %collective-permute-done.17.refs_5_.refs_8_), channel_id=1, source_target_pairs={{0,1},{1,0},{2,3},{3,2},{4,5},{5,4},{6,7},{7,6},{8,9},{9,8},{10,11... | collective-permute-start | bytes 884744 | tf_op jit(solution)/shard_map/ppermute | solution.py:863
  159.4 161.9 %collective-permute-start.58 = (bf16[768,768]{1,0:T(8,128)(2,1)S(1)}, bf16[768,768]{1,0:T(8,128)(2,1)S(1)}, u32[]{:S(2)}, u32[]{:S(2)}) collective-permute-start(bf16[768,768]{1,0:T(8,128)(2,1)S(1)} %copy-done.2), channel_id=1, source_target_pairs={{0,1},{1,0},{2,3},{3,2},{4,5},{5,4},{6,7},{7,6},{8,9},{9,8},{10,11... | collective-permute-start | bytes 3538952 | tf_op jit(solution)/shard_map/ppermute | solution.py:863
  162.4 158.9 %collective-permute-start.55 = (bf16[192,3072]{1,0:T(8,128)(2,1)S(1)}, bf16[192,3072]{1,0:T(8,128)(2,1)S(1)}, u32[]{:S(2)}, u32[]{:S(2)}) collective-permute-start(bf16[192,3072]{1,0:T(8,128)(2,1)S(1)} %copy-done.62), channel_id=1, source_target_pairs={{0,1},{1,0},{2,3},{3,2},{4,5},{5,4},{6,7},{7,6},{8,9},{9,8},{10,11... | collective-permute-start | bytes 3538952 | tf_op jit(solution)/shard_map/ppermute | solution.py:863
  164.6 156.8 %collective-permute-start.59 = (bf16[768,768]{1,0:T(8,128)(2,1)S(1)}, bf16[768,768]{1,0:T(8,128)(2,1)S(1)}, u32[]{:S(2)}, u32[]{:S(2)}) collective-permute-start(bf16[768,768]{1,0:T(8,128)(2,1)S(1)} %collective-permute-done.57.refs_33_.w1), channel_id=1, source_target_pairs={{0,1},{1,0},{2,3},{3,2},{4,5},{5,4},{6,7},{7,6},{8,9},{9,8},{10,11... | collective-permute-start | bytes 3538952 | tf_op jit(solution)/shard_map/ppermute | solution.py:863
  164.7 156.6 %collective-permute-start.56 = (bf16[192,3072]{1,0:T(8,128)(2,1)}, bf16[192,3072]{1,0:T(8,128)(2,1)S(1)}, u32[]{:S(2)}, u32[]{:S(2)}) collective-permute-start(bf16[192,3072]{1,0:T(8,128)(2,1)} %collective-permute-done.54.refs_29_), channel_id=1, source_target_pairs={{0,1},{1,0},{2,3},{3,2},{4,5},{5,4},{6,7},{7,6},{8,9},{9,8},{10,11... | collective-permute-start | bytes 3538952 | tf_op jit(solution)/shard_map/ppermute | solution.py:863
  354.1 32.1 %collective-permute-start.75 = (bf16[64,256]{1,0:T(8,128)(2,1)}, bf16[64,256]{1,0:T(8,128)(2,1)S(1)}, u32[]{:S(2)}, u32[]{:S(2)}) collective-permute-start(bf16[64,256]{1,0:T(8,128)(2,1)} %get-tuple-element.220), channel_id=1, source_target_pairs={{0,8},{4,12},{8,0},{12,4},{16,24},{20,28},{24,16},{28,20},{1,9},{5... | collective-permute-start | bytes 98312 | tf_op jit(solution)/shard_map/ppermute | solution.py:863
  354.1 34.4 %collective-permute-start.76 = (bf16[64,256]{1,0:T(8,128)(2,1)}, bf16[64,256]{1,0:T(8,128)(2,1)S(1)}, u32[]{:S(2)}, u32[]{:S(2)}) collective-permute-start(bf16[64,256]{1,0:T(8,128)(2,1)} %get-tuple-element.221), channel_id=1, source_target_pairs={{0,12},{4,8},{8,4},{12,0},{16,28},{20,24},{24,20},{28,16},{1,13},{... | collective-permute-start | bytes 98312 | tf_op jit(solution)/shard_map/ppermute | solution.py:863
  357.3 32.5 %collective-permute-start.77 = (bf16[64,256]{1,0:T(8,128)(2,1)}, bf16[64,256]{1,0:T(8,128)(2,1)S(1)}, u32[]{:S(2)}, u32[]{:S(2)}) collective-permute-start(bf16[64,256]{1,0:T(8,128)(2,1)} %get-tuple-element.222), channel_id=1, source_target_pairs={{0,16},{4,20},{8,24},{12,28},{16,0},{20,4},{24,8},{28,12},{1,17},{... | collective-permute-start | bytes 98312 | tf_op jit(solution)/shard_map/ppermute | solution.py:863
  357.3 34.3 %collective-permute-start.78 = (bf16[64,256]{1,0:T(8,128)(2,1)}, bf16[64,256]{1,0:T(8,128)(2,1)S(1)}, u32[]{:S(2)}, u32[]{:S(2)}) collective-permute-start(bf16[64,256]{1,0:T(8,128)(2,1)} %get-tuple-element.223), channel_id=1, source_target_pairs={{0,20},{4,16},{8,28},{12,24},{16,4},{20,0},{24,12},{28,8},{1,21},{... | collective-permute-start | bytes 98312 | tf_op jit(solution)/shard_map/ppermute | solution.py:863
  360.0 31.8 %collective-permute-start.79 = (bf16[64,256]{1,0:T(8,128)(2,1)}, bf16[64,256]{1,0:T(8,128)(2,1)S(1)}, u32[]{:S(2)}, u32[]{:S(2)}) collective-permute-start(bf16[64,256]{1,0:T(8,128)(2,1)} %get-tuple-element.224), channel_id=1, source_target_pairs={{0,24},{4,28},{8,16},{12,20},{16,8},{20,12},{24,0},{28,4},{1,25},{... | collective-permute-start | bytes 98312 | tf_op jit(solution)/shard_map/ppermute | solution.py:863
  409.2 31.9 %collective-permute-start.101 = (bf16[192,256]{1,0:T(8,128)(2,1)S(1)}, bf16[192,256]{1,0:T(8,128)(2,1)S(1)}, u32[]{:S(2)}, u32[]{:S(2)}) collective-permute-start(bf16[192,256]{1,0:T(8,128)(2,1)S(1)} %copy-done.85), channel_id=1, source_target_pairs={{0,28},{4,24},{8,20},{12,16},{16,12},{20,8},{24,4},{28,0},{1,29},{... | collective-permute-start | bytes 294920 | tf_op jit(solution)/shard_map/ppermute | solution.py:863
  411.1 32.5 %collective-permute-start.95 = (bf16[192,256]{1,0:T(8,128)(2,1)S(1)}, bf16[192,256]{1,0:T(8,128)(2,1)S(1)}, u32[]{:S(2)}, u32[]{:S(2)}) collective-permute-start(bf16[192,256]{1,0:T(8,128)(2,1)S(1)} %copy-done.84), channel_id=1, source_target_pairs={{0,4},{4,0},{8,12},{12,8},{16,20},{20,16},{24,28},{28,24},{1,5},{5... | collective-permute-start | bytes 294920 | tf_op jit(solution)/shard_map/ppermute | solution.py:863
  413.0 31.0 %collective-permute-start.96 = (bf16[192,256]{1,0:T(8,128)(2,1)S(1)}, bf16[192,256]{1,0:T(8,128)(2,1)S(1)}, u32[]{:S(2)}, u32[]{:S(2)}) collective-permute-start(bf16[192,256]{1,0:T(8,128)(2,1)S(1)} %copy-done.83), channel_id=1, source_target_pairs={{0,8},{4,12},{8,0},{12,4},{16,24},{20,28},{24,16},{28,20},{1,9},{5... | collective-permute-start | bytes 294920 | tf_op jit(solution)/shard_map/ppermute | solution.py:863
  413.1 31.7 %collective-permute-start.97 = (bf16[192,256]{1,0:T(8,128)(2,1)S(1)}, bf16[192,256]{1,0:T(8,128)(2,1)S(1)}, u32[]{:S(2)}, u32[]{:S(2)}) collective-permute-start(bf16[192,256]{1,0:T(8,128)(2,1)S(1)} %copy-done.82), channel_id=1, source_target_pairs={{0,12},{4,8},{8,4},{12,0},{16,28},{20,24},{24,20},{28,16},{1,13},{... | collective-permute-start | bytes 294920 | tf_op jit(solution)/shard_map/ppermute | solution.py:863
  414.8 32.3 %collective-permute-start.98 = (bf16[192,256]{1,0:T(8,128)(2,1)S(1)}, bf16[192,256]{1,0:T(8,128)(2,1)S(1)}, u32[]{:S(2)}, u32[]{:S(2)}) collective-permute-start(bf16[192,256]{1,0:T(8,128)(2,1)S(1)} %copy-done.81), channel_id=1, source_target_pairs={{0,16},{4,20},{8,24},{12,28},{16,0},{20,4},{24,8},{28,12},{1,17},{... | collective-permute-start | bytes 294920 | tf_op jit(solution)/shard_map/ppermute | solution.py:863
  441.2 31.5 %collective-permute-start.99 = (bf16[192,256]{1,0:T(8,128)(2,1)S(1)}, bf16[192,256]{1,0:T(8,128)(2,1)S(1)}, u32[]{:S(2)}, u32[]{:S(2)}) collective-permute-start(bf16[192,256]{1,0:T(8,128)(2,1)S(1)} %copy-done.75), channel_id=1, source_target_pairs={{0,20},{4,16},{8,28},{12,24},{16,4},{20,0},{24,12},{28,8},{1,21},{... | collective-permute-start | bytes 294920 | tf_op jit(solution)/shard_map/ppermute | solution.py:863
  443.6 31.2 %collective-permute-start.81 = (bf16[192,256]{1,0:T(8,128)(2,1)}, bf16[192,256]{1,0:T(8,128)(2,1)S(1)}, u32[]{:S(2)}, u32[]{:S(2)}) collective-permute-start(bf16[192,256]{1,0:T(8,128)(2,1)} %get-tuple-element.229), channel_id=1, source_target_pairs={{0,4},{4,0},{8,12},{12,8},{16,20},{20,16},{24,28},{28,24},{1,5},{5... | collective-permute-start | bytes 294920 | tf_op jit(solution)/shard_map/ppermute | solution.py:863
  443.9 34.1 %collective-permute-start.82 = (bf16[192,256]{1,0:T(8,128)(2,1)}, bf16[192,256]{1,0:T(8,128)(2,1)S(1)}, u32[]{:S(2)}, u32[]{:S(2)}) collective-permute-start(bf16[192,256]{1,0:T(8,128)(2,1)} %get-tuple-element.230), channel_id=1, source_target_pairs={{0,8},{4,12},{8,0},{12,4},{16,24},{20,28},{24,16},{28,20},{1,9},{5... | collective-permute-start | bytes 294920 | tf_op jit(solution)/shard_map/ppermute | solution.py:863
  444.8 35.2 %collective-permute-start.83 = (bf16[192,256]{1,0:T(8,128)(2,1)}, bf16[192,256]{1,0:T(8,128)(2,1)S(1)}, u32[]{:S(2)}, u32[]{:S(2)}) collective-permute-start(bf16[192,256]{1,0:T(8,128)(2,1)} %get-tuple-element.231), channel_id=1, source_target_pairs={{0,12},{4,8},{8,4},{12,0},{16,28},{20,24},{24,20},{28,16},{1,13},{... | collective-permute-start | bytes 294920 | tf_op jit(solution)/shard_map/ppermute | solution.py:863
  447.1 33.1 %collective-permute-start.84 = (bf16[192,256]{1,0:T(8,128)(2,1)}, bf16[192,256]{1,0:T(8,128)(2,1)S(1)}, u32[]{:S(2)}, u32[]{:S(2)}) collective-permute-start(bf16[192,256]{1,0:T(8,128)(2,1)} %get-tuple-element.232), channel_id=1, source_target_pairs={{0,16},{4,20},{8,24},{12,28},{16,0},{20,4},{24,8},{28,12},{1,17},{... | collective-permute-start | bytes 294920 | tf_op jit(solution)/shard_map/ppermute | solution.py:863
  534.1 47.7 %collective-permute-start.150 = (bf16[2,8,96,768]{3,2,1,0:T(8,128)(2,1)}, bf16[2,8,96,768]{3,2,1,0:T(8,128)(2,1)S(1)}, u32[]{:S(2)}, u32[]{:S(2)}) collective-permute-start(bf16[2,8,96,768]{3,2,1,0:T(8,128)(2,1)} %get-tuple-element.273), channel_id=1, source_target_pairs={{0,1},{1,0},{2,3},{3,2},{4,5},{5,4},{6,7},{7,6},{8,9},{9,8},{10,11... | collective-permute-start | bytes 7077896 | tf_op jit(solution)/shard_map/ppermute | solution.py:863
  544.3 38.7 %collective-permute-start.138 = (bf16[2,8,24,3840]{3,2,1,0:T(8,128)(2,1)}, bf16[2,8,24,3840]{3,2,1,0:T(8,128)(2,1)S(1)}, u32[]{:S(2)}, u32[]{:S(2)}) collective-permute-start(bf16[2,8,24,3840]{3,2,1,0:T(8,128)(2,1)} %get-tuple-element.269), channel_id=1, source_target_pairs={{0,1},{1,0},{2,3},{3,2},{4,5},{5,4},{6,7},{7,6},{8,9},{9,8},{10,11... | collective-permute-start | bytes 8847368 | tf_op jit(solution)/shard_map/ppermute | solution.py:863
  544.4 136.2 %collective-permute-start.166 = (f32[9,768]{1,0:T(8,128)S(1)}, f32[9,768]{1,0:T(8,128)S(1)}, u32[]{:S(2)}, u32[]{:S(2)}) collective-permute-start(f32[9,768]{1,0:T(8,128)S(1)} %add.194), channel_id=1, source_target_pairs={{0,16},{4,20},{8,24},{12,28},{16,0},{20,4},{24,8},{28,12},{1,17},{... | collective-permute-start | bytes 82952 | tf_op jit(solution)/shard_map/ppermute | solution.py:863
  581.8 58.2 %collective-permute-start.130 = (bf16[1,24,768]{2,1,0:T(8,128)(2,1)S(1)}, bf16[1,24,768]{2,1,0:T(8,128)(2,1)S(1)}, u32[]{:S(2)}, u32[]{:S(2)}) collective-permute-start(bf16[1,24,768]{2,1,0:T(8,128)(2,1)S(1)} %slice_bitcast_fusion.24), channel_id=1, source_target_pairs={{0,16},{4,20},{8,24},{12,28},{16,0},{20,4},{24,8},{28,12},{1,17},{... | collective-permute-start | bytes 110600 | tf_op jit(solution)/shard_map/ppermute | solution.py:863
  585.3 53.6 %collective-permute-start.139 = (bf16[8,24,3840]{2,1,0:T(8,128)(2,1)S(1)}, bf16[8,24,3840]{2,1,0:T(8,128)(2,1)S(1)}, u32[]{:S(2)}, u32[]{:S(2)}) collective-permute-start(bf16[8,24,3840]{2,1,0:T(8,128)(2,1)S(1)} %fusion.3), channel_id=1, source_target_pairs={{0,2},{1,3},{2,0},{3,1},{4,6},{5,7},{6,4},{7,5},{8,10},{9,11},{10,... | collective-permute-start | bytes 4423688 | tf_op jit(solution)/shard_map/ppermute | solution.py:863
  586.9 54.8 %collective-permute-start.118 = (bf16[1,24,768]{2,1,0:T(8,128)(2,1)S(1)}, bf16[1,24,768]{2,1,0:T(8,128)(2,1)S(1)}, u32[]{:S(2)}, u32[]{:S(2)}) collective-permute-start(bf16[1,24,768]{2,1,0:T(8,128)(2,1)S(1)} %slice_bitcast_fusion.26), channel_id=1, source_target_pairs={{0,16},{4,20},{8,24},{12,28},{16,0},{20,4},{24,8},{28,12},{1,17},{... | collective-permute-start | bytes 110600 | tf_op jit(solution)/shard_map/ppermute | solution.py:863
  611.9 54.2 %collective-permute-start.106 = (bf16[1,24,768]{2,1,0:T(8,128)(2,1)S(1)}, bf16[1,24,768]{2,1,0:T(8,128)(2,1)S(1)}, u32[]{:S(2)}, u32[]{:S(2)}) collective-permute-start(bf16[1,24,768]{2,1,0:T(8,128)(2,1)S(1)} %slice_bitcast_fusion.28), channel_id=1, source_target_pairs={{0,16},{4,20},{8,24},{12,28},{16,0},{20,4},{24,8},{28,12},{1,17},{... | collective-permute-start | bytes 110600 | tf_op jit(solution)/shard_map/ppermute | solution.py:863
  641.7 39.2 %collective-permute-start.134 = (bf16[24,768]{1,0:T(8,128)(2,1)S(1)}, bf16[24,768]{1,0:T(8,128)(2,1)S(1)}, u32[]{:S(2)}, u32[]{:S(2)}) collective-permute-start(bf16[24,768]{1,0:T(8,128)(2,1)S(1)} %fusion.39.refs_16_), channel_id=1, source_target_pairs={{0,16},{4,20},{8,24},{12,28},{16,0},{20,4},{24,8},{28,12},{1,17},{... | collective-permute-start | bytes 110600 | tf_op jit(solution)/shard_map/ppermute | solution.py:863
  (284 other events, 4645.6 us)

commit v2 on v1

--- a/solution.py
+++ b/solution.py
@@ -446,11 +446,21 @@
     lax.fori_loop(0, rows // step, one, 0)
 
 
-def qkv_kernel(hps, batches, has_x, *refs):
+def full_rows(pieces, first, last):
+    total = None
+    for piece in pieces:
+        term = piece[first:last, :].astype(F32)
+        total = term if total is None else total + term
+    return total
+
+
+def qkv_kernel(hps, batches, has_x, offset, *refs):
     if has_x:
-        scalars, x, norms, cosine, sine, w0, w1, w2, w3 = refs[:9]
-        outs = refs[9:-3]
-        n1t, weight, pairs = refs[-3:]
+        scalars, x, cosine, sine, w0, w1, w2, w3 = refs[:8]
+        out, n1t, norms, weight = refs[8:]
+        rows = n1t.shape[0] // 4
+        parts = full_rows((w0, w1, w2, w3), rows, rows + 16)
+        norms[...] = parts[0:8, :] + parts[8:16, :]
         v = x[...].astype(F32)
         center = v - jnp.mean(v, axis=-1, keepdims=True)
         inv = lax.rsqrt(jnp.mean(center * center, axis=-1, keepdims=True) + 1e-05)
@@ -458,12 +468,11 @@
         n1t[...] = n1.astype(BF16).T
     else:
         scalars, n1t, cosine, sine, w0, w1, w2, w3 = refs[:8]
-        outs = refs[8:-2]
-        weight, pairs = refs[-2:]
-    rows = w0.shape[0]
+        out, weight = refs[8:]
+        rows = n1t.shape[0] // 4
     for order, piece in enumerate((w0, w1, w2, w3)):
         start = pl.multiple_of(block_index(scalars, order) * rows, rows)
-        weight[pl.ds(start, rows), :] = piece[...]
+        weight[pl.ds(start, rows), :] = piece[offset : offset + rows, :]
     width = weight.shape[1] // 3
     size = width // hps
     half = size // 2
@@ -480,69 +489,70 @@
                     s = sine[batch]
                     top, low = top * c - low * s, low * c + top * s
                 slot = batch * hps + head
-                pairs[slot, part * size : part * size + half, :] = top.astype(BF16)
-                pairs[slot, part * size + half : (part + 1) * size, :] = low.astype(BF16)
-    for delta, out in enumerate(outs):
-        out[...] = pairs[lax.bitwise_xor(scalars[0], jnp.int32(delta))]
-
-
-def attend_kernel(count, scale, ids, *refs):
-    ins = refs[:count]
-    outs = refs[count : 2 * count]
-    ot, lse, qt, kk, vt, scores, top, total, acc = refs[2 * count :]
+                out[slot, part * size : part * size + half, :] = top.astype(BF16)
+                out[slot, part * size + half : (part + 1) * size, :] = low.astype(BF16)
+
+
+def stream_tile(count, stream, step):
+    long = count - stream
+    late = step >= long
+    query = jnp.where(late, stream, count - 1 - stream)
+    return query, jnp.where(late, step - long, step)
+
+
+def attend_kernel(count, scale, ids, ins, outs, ot, lse, qt, kk, vt, scores, *states):
+    streams = count // 2
+    tops, totals, accs = states[:streams], states[streams : 2 * streams], states[2 * streams :]
     size = qt.shape[1]
     factor = scale * LOG2E
     for d in range(count):
         slot = ids[d]
-        qt[slot] = ins[d][0:size, :]
-        kk[slot] = ins[d][size : 2 * size, :].T
-        vt[slot] = ins[d][2 * size :, :]
-    acc[...] = jnp.zeros_like(acc)
-    total[...] = jnp.zeros_like(total)
-    top[...] = jnp.full_like(top, -1e30)
-    scores[0] = mm(kk[0], qt[0], 1, 0) * factor
+        qt[slot] = ins[d, 0:size, :]
+        kk[slot] = ins[d, size : 2 * size, :].T
+        vt[slot] = ins[d, 2 * size :, :]
+    for r in range(streams):
+        tops[r][...] = jnp.full_like(tops[r], -1e30)
+        totals[r][...] = jnp.zeros_like(totals[r])
+        accs[r][...] = jnp.zeros_like(accs[r])
+        scores[0, r] = mm(kk[0], qt[count - 1 - r], 1, 0)
 
     def step(index, carry):
-        i, j = carry
-        last = j == i
-        next_i = jnp.where(last, i + 1, i)
-        next_j = jnp.where(last, 0, j + 1)
-        ahead = jnp.minimum(next_i, count - 1)
-        scores[(index + 1) % 2] = mm(kk[next_j], qt[ahead], 1, 0) * factor
-        s = scores[index % 2]
-        old = jnp.where(j == 0, -1e30, top[...])
-        new = jnp.maximum(old, jnp.max(s, axis=0, keepdims=True))
-        shrink = jnp.exp2(old - new)
-        p = jnp.exp2(s - new)
-        run = total[...] * shrink + jnp.sum(p, axis=0, keepdims=True)
-        out = acc[...] * shrink + mm(vt[j], p.astype(BF16), 1, 0)
-        top[...] = new
-        total[...] = run
-        acc[...] = out
-
-        @pl.when(last)
-        def _():
-            ot[i] = out / run
-            lse[i] = new + jnp.log2(run)
-
-        return (next_i, next_j)
-
-    lax.fori_loop(0, count * (count + 1) // 2, step, (jnp.int32(0), jnp.int32(0)))
+        for r in range(streams):
+            i, j = stream_tile(count, r, jnp.minimum(index + 1, count))
+            scores[(index + 1) % 2, r] = mm(kk[j], qt[i], 1, 0)
+        for r in range(streams):
+            i, j = stream_tile(count, r, index)
+            half = jnp.where(index >= count - r, 1, 0)
+            s = scores[index % 2, r]
+            old = tops[r][half]
+            new = jnp.maximum(old, jnp.max(s, axis=0, keepdims=True) * factor)
+            shrink = jnp.exp2(old - new)
+            p = jnp.exp2(s * factor - new)
+            totals[r][half] = totals[r][half] * shrink + jnp.sum(p, axis=0, keepdims=True)
+            accs[r][half] = accs[r][half] * shrink + mm(vt[j], p.astype(BF16), 1, 0)
+            tops[r][half] = new
+        return carry
+
+    lax.fori_loop(0, count + 1, step, 0)
+    for r in range(streams):
+        for half, i in enumerate((count - 1 - r, r)):
+            run = totals[r][half]
+            ot[i] = accs[r][half] / run
+            lse[i] = tops[r][half] + jnp.log2(run)
     for d in range(count):
-        outs[d][...] = ot[ids[d]].astype(BF16)
-
-
-def attend_back_kernel(count, scale, ids, *refs):
-    ins = refs[:count]
-    grads = refs[count : 2 * count]
-    ot, lse = refs[2 * count : 2 * count + 2]
-    outs = refs[2 * count + 2 : 3 * count + 2]
-    qt, qq, kt, kk, vv, gt, gg, delta, scores, gains, dq, dk, dv = refs[3 * count + 2 :]
+        outs[d] = ot[ids[d]].astype(BF16)
+
+
+def attend_back_kernel(
+    count, scale, ids, ins, grads, ot, lse, outs, qt, qq, kt, kk, vv, gt, gg, delta, scores, gains, *sums
+):
+    streams = count // 2
+    dqs, dks, dvs = sums[:streams], sums[streams : 2 * streams], sums[2 * streams :]
     size = qt.shape[1]
     factor = scale * LOG2E
     for d in range(count):
         slot = ids[d]
-        block = ins[d][...]
+        block = ins[d]
         q = block[0:size]
         k = block[size : 2 * size]
         qt[slot] = q
@@ -550,73 +560,87 @@
         qq[slot] = q.T
         kk[slot] = k.T
         vv[slot] = block[2 * size :].T
-        g = grads[d][...]
+        g = grads[d]
         gt[slot] = g
         gg[slot] = g.T
         delta[slot] = jnp.sum(g.astype(F32) * ot[slot], axis=0, keepdims=True)
-    dq[...] = jnp.zeros_like(dq)
-    dk[...] = jnp.zeros_like(dk)
-    dv[...] = jnp.zeros_like(dv)
-    scores[0] = mm(kk[0], qt[0], 1, 0)
-    gains[0] = mm(vv[0], gt[0], 1, 0)
+    for r in range(streams):
+        dqs[r][...] = jnp.zeros_like(dqs[r])
+        dks[r][...] = jnp.zeros_like(dks[r])
+        dvs[r][...] = jnp.zeros_like(dvs[r])
+        scores[0, r] = mm(kk[0], qt[count - 1 - r], 1, 0)
+        gains[0, r] = mm(vv[0], gt[count - 1 - r], 1, 0)
 
     def step(index, carry):
-        i, j = carry
-        last = j == i
-        next_i = jnp.where(last, i + 1, i)
-        next_j = jnp.where(last, 0, j + 1)
-        ahead = jnp.minimum(next_i, count - 1)
-        later = (index + 1) % 2
-        scores[later] = mm(kk[next_j], qt[ahead], 1, 0)
-        gains[later] = mm(vv[next_j], gt[ahead], 1, 0)
-        now = index % 2
-        p = jnp.exp2(scores[now] * factor - lse[i])
-        ds = (p * (gains[now] - delta[i])).astype(BF16)
-        dq[i] += mm(kt[j], ds, 1, 0)
-        dk[j] += mm(ds, qq[i], 1, 0)
-        dv[j] += mm(p.astype(BF16), gg[i], 1, 0)
-        return (next_i, next_j)
-
-    lax.fori_loop(0, count * (count + 1) // 2, step, (jnp.int32(0), jnp.int32(0)))
+        for r in range(streams):
+            i, j = stream_tile(count, r, jnp.minimum(index + 1, count))
+            scores[(index + 1) % 2, r] = mm(kk[j], qt[i], 1, 0)
+            gains[(index + 1) % 2, r] = mm(vv[j], gt[i], 1, 0)
+        for r in range(streams):
+            i, j = stream_tile(count, r, index)
+            half = jnp.where(index >= count - r, 1, 0)
+            p = jnp.exp2(scores[index % 2, r] * factor - lse[i])
+            ds = (p * (gains[index % 2, r] - delta[i])).astype(BF16)
+            dqs[r][half] += mm(kt[j], ds, 1, 0)
+            dks[r][j] += mm(ds, qq[i], 1, 0)
+            dvs[r][j] += mm(p.astype(BF16), gg[i], 1, 0)
+        return carry
+
+    lax.fori_loop(0, count + 1, step, 0)
+    for r in range(streams):
+        for half, i in enumerate((count - 1 - r, r)):
+            qt[i] = (dqs[r][half] * scale).astype(BF16)
     for d in range(count):
         slot = ids[d]
-        outs[d][0:size, :] = (dq[slot] * scale).astype(BF16)
-        outs[d][size : 2 * size, :] = (dk[slot] * scale).T.astype(BF16)
-        outs[d][2 * size :, :] = dv[slot].T.astype(BF16)
-
-
-def gather_rows(scalars, pieces, target, sems, base):
+        outs[d, 0:size, :] = qt[slot]
+        dk = dks[0][slot]
+        dv = dvs[0][slot]
+        for r in range(1, streams):
+            dk = dk + dks[r][slot]
+            dv = dv + dvs[r][slot]
+        outs[d, size : 2 * size, :] = (dk * scale).astype(BF16).T
+        outs[d, 2 * size :, :] = dv.astype(BF16).T
+
+
+def gather_rows(scalars, pieces, window, target, sems, base):
     copies = []
-    rows = pieces[0].shape[0]
+    first, rows = window
     for order, piece in enumerate(pieces):
         start = pl.multiple_of(block_index(scalars, order) * rows, rows)
-        copy = pltpu.make_async_copy(piece, target.at[pl.ds(start, rows), :], sems.at[base + order])
+        copy = pltpu.make_async_copy(
+            piece.at[pl.ds(first, rows), :], target.at[pl.ds(start, rows), :], sems.at[base + order]
+        )
         copy.start()
         copies.append(copy)
     return copies
 
 
 def mlp_kernel(count, stages, hps, batches, scalars, mix, x, grad, norms, *refs):
-    heads = refs[: count * stages]
-    refs = refs[count * stages :]
-    w_out, w_up, w_down = refs[0:4], refs[4:8], refs[8:12]
-    hidden, dhidden, n2_out, mid_out, dmid_out, dmid_low, ot, norm_grads = refs[12:20]
-    head_grads = refs[20 : 20 + count * stages]
-    out_scr, up_scr, down_scr, dn2, got, sems = refs[20 + count * stages :]
-    copies_out = gather_rows(scalars, w_out, out_scr, sems, 0)
-    copies_up = gather_rows(scalars, w_up, up_scr, sems, 4)
-    copies_down = gather_rows(scalars, w_down, down_scr, sems, 8)
-    me = scalars[0]
+    heads = refs[:stages]
+    pieces = refs[stages : stages + 4]
+    refs = refs[stages + 4 :]
+    hidden, dhidden, n2_out, mid_out, dmid_out, dmid_low, ot, norm_grads = refs[:8]
+    head_grads = refs[8 : 8 + stages]
+    out_scr, up_scr, down_scr, dn2, got, sems = refs[8 + stages :]
+    width = x.shape[1]
+    share = width // 4
+    groups = up_scr.shape[1] // width
+    deep = down_scr.shape[0] // 4
+    last = (groups * share) + deep
+    copies_out = gather_rows(scalars, pieces, (last, share), out_scr, sems, 0)
+    copies_up = []
+    for group in range(groups):
+        lanes = up_scr.at[:, pl.ds(group * width, width)]
+        copies_up += gather_rows(scalars, pieces, (group * share, share), lanes, sems, 4 + 4 * group)
+    copies_down = gather_rows(
+        scalars, pieces, (groups * share, deep), down_scr, sems, 4 + 4 * groups
+    )
     for stage in range(stages):
-        for d in range(count):
-            slot = lax.bitwise_xor(me, jnp.int32(d))
-            batch = lax.div(slot, jnp.int32(hps))
-            head = stage * hps + lax.rem(slot, jnp.int32(hps))
-            ot[batch, head] = heads[stage * count + d][...]
+        for slot in range(count):
+            ot[slot // hps, stage * hps + slot % hps] = heads[stage][slot]
     for copy in copies_out:
         copy.wait()
     tokens = x.shape[0] // batches
-    width = x.shape[1]
     for batch in range(batches):
         rows = slice(batch * tokens, (batch + 1) * tokens)
         attended = ot[batch].reshape(width, tokens)
@@ -674,65 +698,60 @@
     norm_grads[0:1, :] = gain_sum
     norm_grads[1:2, :] = bias_sum
     for stage in range(stages):
-        for d in range(count):
-            slot = lax.bitwise_xor(me, jnp.int32(d))
-            batch = lax.div(slot, jnp.int32(hps))
-            head = stage * hps + lax.rem(slot, jnp.int32(hps))
-            head_grads[stage * count + d][...] = got[batch, head]
-
-
-def result_kernel(scalars, mix, hidden, mid, prev, grad, w0, w1, w2, w3, out, out_mix, acc):
+        for slot in range(count):
+            head_grads[stage][slot] = got[slot // hps, stage * hps + slot % hps]
+
+
+def result_kernel(window, scalars, mix, hidden, mid, prev, grad, w0, w1, w2, w3, out, out_mix, acc):
     acc[...] = mid[...]
-    rows = w0.shape[0]
+    first, rows = window
     for order, piece in enumerate((w0, w1, w2, w3)):
         start = pl.multiple_of(block_index(scalars, order) * rows, rows)
-        acc[...] += mm(hidden[:, pl.ds(start, rows)], piece[...], 1, 0)
+        acc[...] += mm(hidden[:, pl.ds(start, rows)], piece[first : first + rows, :], 1, 0)
     y = acc[...]
     out[...] = (prev[...] + mix[mix.shape[0] - 1] * y).astype(BF16)
     out_mix[...] = jnp.zeros_like(out_mix)
     out_mix[0:1, :] = jnp.sum(grad[...].astype(F32) * y, axis=0, keepdims=True)
 
 
-def put_pieces(me, value, outs, order, count, lanes):
-    keep, send = outs
-    target = (keep, keep, send, send)[order]
+def put_pieces(me, value, outs, order, count, first):
+    target = outs[order // 2]
     rows = value.shape[0] // count
     low = value.astype(BF16)
+    bit = lax.rem(me, jnp.int32(2))
     for sub in range(count):
-        slot = lax.bitwise_xor(me, jnp.int32(sub))
-        target[order % 2, slot, :, lanes] = low[sub * rows : (sub + 1) * rows, :]
+        side = lax.bitwise_xor(bit, jnp.int32(sub % 2))
+        target[order % 2, side, sub // 2, first : first + rows, :] = low[
+            sub * rows : (sub + 1) * rows, :
+        ]
 
 
 def down_grad_kernel(count, scalars, mix, hidden, grad, keep, send):
     dy = (mix[mix.shape[0] - 1] * grad[...].astype(F32)).astype(BF16)
-    rows = keep.shape[1] * keep.shape[2]
+    rows = count * keep.shape[3]
     for order in range(4):
         start = pl.multiple_of(block_index(scalars, order) * rows, rows)
         value = mm(hidden[:, pl.ds(start, rows)], dy, 0, 0)
-        put_pieces(scalars[0], value, (keep, send), order, count, slice(None))
-
-
-def up_out_grad_kernel(count, scalars, n2, dhidden, ot, dmid, keep, send, left, left_out):
+        put_pieces(scalars[0], value, (keep, send), order, count, 0)
+
+
+def up_out_grad_kernel(count, scalars, n2, dhidden, ot, dmid, keep, send, left, whole):
     batches = ot.shape[0]
     width = n2.shape[1]
     tokens = ot.shape[3]
     rows = width // 4
-    flipped = n2[...].T
-    for order in range(4):
-        here = pl.ds(pl.multiple_of(block_index(scalars, order) * rows, rows), rows)
-        left_out[order * rows : (order + 1) * rows, :] = jnp.zeros(
-            (rows, left_out.shape[1]), BF16
-        )
-    left_out[...] = flipped
-    for order in range(4):
-        here = pl.ds(pl.multiple_of(block_index(scalars, order) * rows, rows), rows)
-        left[order * rows : (order + 1) * rows, :] = left_out[here, :]
-    inner = dhidden.shape[1]
-    step = 768 if inner % 768 == 0 else 256
-
-    def one(index, carry):
-        start = pl.multiple_of(index * step, step)
-        value = mm(left[...], dhidden[:, pl.ds(start, step)], 1, 0)
+    thin = rows // count
+
+    def arrange():
+        for order in range(4):
+            here = pl.ds(pl.multiple_of(block_index(scalars, order) * rows, rows), rows)
+            left[order * rows : (order + 1) * rows, :] = whole[here, :]
+
+    whole[...] = n2[...].T
+    arrange()
+    groups = dhidden.shape[1] // width
+    for group in range(groups):
+        value = mm(left[...], dhidden[:, group * width : (group + 1) * width], 1, 0)
         for order in range(4):
             put_pieces(
                 scalars[0],
@@ -740,16 +759,11 @@
                 (keep, send),
                 order,
                 count,
-                pl.ds(start, step),
+                group * thin,
             )
-        return carry
-
-    lax.fori_loop(0, inner // step, one, 0)
     for batch in range(batches):
-        left_out[:, batch * tokens : (batch + 1) * tokens] = ot[batch].reshape(width, tokens)
-    for order in range(4):
-        here = pl.ds(pl.multiple_of(block_index(scalars, order) * rows, rows), rows)
-        left[order * rows : (order + 1) * rows, :] = left_out[here, :]
+        whole[:, batch * tokens : (batch + 1) * tokens] = ot[batch].reshape(width, tokens)
+    arrange()
     value = mm(left[...], dmid[...], 1, 0)
     for order in range(4):
         put_pieces(
@@ -758,32 +772,28 @@
             (keep, send),
             order,
             count,
-            slice(inner, inner + value.shape[1]),
-        )
-
-
-def in_grad_kernel(count, hps, scalars, cosine, sine, n1t, *refs):
-    grads = refs[:count]
-    dt, keep, send, left = refs[count:]
+            groups * thin,
+        )
+
+
+def in_grad_kernel(count, hps, scalars, cosine, sine, n1t, grads, dt, keep, send, left):
     batches = dt.shape[0]
     size = dt.shape[3]
     half = size // 2
     tokens = dt.shape[4]
-    me = scalars[0]
-    for d in range(count):
-        slot = lax.bitwise_xor(me, jnp.int32(d))
-        batch = lax.div(slot, jnp.int32(hps))
-        head = lax.rem(slot, jnp.int32(hps))
+    for slot in range(count):
+        batch, head = slot // hps, slot % hps
         c = cosine[batch]
         s = sine[batch]
         for part in range(2):
-            top = grads[d][part * size : part * size + half, :].astype(F32)
-            low = grads[d][part * size + half : (part + 1) * size, :].astype(F32)
+            top = grads[slot, part * size : part * size + half, :].astype(F32)
+            low = grads[slot, part * size + half : (part + 1) * size, :].astype(F32)
             dt[batch, part, head, 0:half, :] = (top * c + low * s).astype(BF16)
             dt[batch, part, head, half:size, :] = (low * c - top * s).astype(BF16)
-        dt[batch, 2, head] = grads[d][2 * size :, :]
+        dt[batch, 2, head] = grads[slot, 2 * size :, :]
     width = n1t.shape[0]
     rows = width // 4
+    thin = rows // count
     for order in range(4):
         here = pl.ds(pl.multiple_of(block_index(scalars, order) * rows, rows), rows)
         left[order * rows : (order + 1) * rows, :] = n1t[here, :]
@@ -794,30 +804,30 @@
             left[:, batch * tokens : (batch + 1) * tokens], dt[batch].reshape(cols, tokens), 1, 1
         )
         value = term if value is None else value + term
+    low = value.astype(BF16)
     for order in range(4):
-        put_pieces(
-            me, value[order * rows : (order + 1) * rows, :], (keep, send), order, count, slice(None)
-        )
-
-
-def input_grad_kernel(stages, scalars, x, norms, dmid, *refs):
+        target = (keep, send)[order // 2]
+        for sub in range(count):
+            start = order * rows + sub * thin
+            target[order % 2, sub] = low[start : start + thin, :]
+
+
+def input_grad_kernel(stages, windows, scalars, x, norms, dmid, *refs):
     dts = refs[:stages]
     pieces = refs[stages : stages + 4 * stages]
     out, norm_grads, weights, sems = refs[5 * stages :]
     copies = []
     for stage in range(stages):
-        copies.append(
-            gather_rows(
-                scalars,
-                pieces[4 * stage : 4 * stage + 4],
-                weights.at[stage],
-                sems,
-                4 * stage,
-            )
-        )
-    for group in copies:
-        for copy in group:
-            copy.wait()
+        copies += gather_rows(
+            scalars,
+            pieces[4 * stage : 4 * stage + 4],
+            windows[stage],
+            weights.at[stage],
+            sems,
+            4 * stage,
+        )
+    for copy in copies:
+        copy.wait()
     batches = dts[0].shape[0]
     tokens = dts[0].shape[4]
     cols = weights.shape[2]
@@ -847,15 +857,22 @@
     norm_grads[1:2, :] = bias_sum
 
 
-def place_kernel(count, groups, scalars, *refs):
-    pieces = refs[: count * len(groups)]
-    outs = refs[count * len(groups) :]
-    for g, moves in enumerate(groups):
-        for d in range(count):
-            slot = lax.bitwise_xor(scalars[0], jnp.int32(d))
-            piece = pieces[g * count + d]
-            for out, begin, wide, to in moves:
-                outs[out][slot, :, to : to + wide] = piece[:, begin : begin + wide].astype(F32)
+def place_split_kernel(moves, scalars, near, far, *outs):
+    bit = lax.rem(scalars[0], jnp.int32(2))
+    for side, source in enumerate((near, far)):
+        for sub in range(source.shape[0]):
+            slot = 2 * sub + lax.bitwise_xor(bit, jnp.int32(side))
+            for out, first, rows, to, wide in moves:
+                outs[out][slot, :, to : to + wide] = source[sub, first : first + rows, :].astype(F32)
+
+
+def place_in_kernel(width, wide, *refs):
+    *pieces, out = refs
+    for s, piece in enumerate(pieces):
+        for sub in range(piece.shape[0]):
+            for part in range(3):
+                to = part * width + s * wide
+                out[sub, :, to : to + wide] = piece[sub, :, part * wide : (part + 1) * wide].astype(F32)
 
 
 def exchange(value, axis, bit):
@@ -867,28 +884,54 @@
     return (left.astype(F32) + right.astype(F32)).astype(BF16)
 
 
-def reduce_blocks(keep, send):
+def swapped(value, groups=None):
+    return lax.all_to_all(value, "ctx", 0, 0, axis_index_groups=groups)
+
+
+def summed(value):
+    return jnp.sum(value.astype(F32), axis=0).astype(BF16)
+
+
+def spread(own, count, groups=None):
+    return swapped(jnp.broadcast_to(own[None], (count, *own.shape)), groups)
+
+
+def halved(keep, send):
     got = exchange(send, "fsdp", 1)
     passed = added(keep[1], got[1])
     own = added(keep[0], got[0])
-    own = added(own, exchange(passed, "fsdp", 2))
-    bit = 1
-    while bit < lax.axis_size("ctx"):
-        pairs = own.reshape(own.shape[0] // 2, 2, *own.shape[1:])
-        own = added(pairs[:, 0], exchange(pairs[:, 1], "ctx", bit))
-        bit *= 2
-    return own[0]
-
-
-def gather_blocks(own):
+    return added(own, exchange(passed, "fsdp", 2))
+
+
+def other_bits():
     count = lax.axis_size("ctx")
-    held = {0: own}
-    bit = count // 2
-    while bit:
-        for index in list(held):
-            held[index ^ bit] = exchange(held[index], "ctx", bit)
-        bit //= 2
-    return [held[index] for index in range(count)]
+    return [list(range(first, count, 2)) for first in range(2)]
+
+
+def sum_far(own):
+    groups = other_bits()
+    part = summed(swapped(own, groups))
+    near = spread(part, lax.axis_size("ctx") // 2, groups)
+    return part, near, exchange(near, "ctx", 1)
+
+
+def chip_first(keep, send):
+    own = halved(keep, send)
+    return own, added(own[0], exchange(own[1], "ctx", 1))
+
+
+def chip_last(keep, send):
+    both = added(keep, exchange(send, "fsdp", 1))
+    both = added(both[:, 0], exchange(both[:, 1], "ctx", 1))
+    return both, added(both[0], exchange(both[1], "fsdp", 2))
+
+
+def reduce_whole(keep, send):
+    return spread(summed(swapped(halved(keep, send))), lax.axis_size("ctx"))
+
+
+def after(value, *others):
+    return lax.optimization_barrier((value, *others))[0]
 
 
 def gathered(shard):
@@ -924,18 +967,31 @@
     me = lax.axis_index("ctx").astype(jnp.int32)
     place = lax.axis_index("fsdp").astype(jnp.int32)
     scalars = jnp.stack([me, place])
-    own_batch = me // hps
-    ids = block_order[own_batch][me ^ jnp.arange(count, dtype=jnp.int32)].astype(jnp.int32)
+    ids = block_order[me // hps].astype(jnp.int32)
     x = inputs.reshape(rows, width)
     grad = grad_next.reshape(rows, width)
 
+    share = width // 4
+    cols = 3 * hps * size
     norm_stack = jnp.stack([norm1_gain, norm1_bias, norm2_gain, norm2_bias])
-    norms = lax.all_gather(norm_stack, "fsdp", axis=1, tiled=True)
-    chunks = input_proj.reshape(width // 4, 3, stages, hps * size)
-    w_in = [gathered(chunks[:, :, s].reshape(width // 4, 3 * hps * size)) for s in range(stages)]
-    w_out = gathered(output_proj)
-    w_up = gathered(up_proj)
-    w_down = gathered(down_proj)
+    coarse = lax.reduce_precision(norm_stack, 8, 7)
+    norm_rows = jnp.zeros((16, width), BF16)
+    norm_rows = lax.dynamic_update_slice(norm_rows, coarse.astype(BF16), (0, place * share))
+    norm_rows = lax.dynamic_update_slice(
+        norm_rows, (norm_stack - coarse).astype(BF16), (8, place * share)
+    )
+    wide = hps * size
+    chunks = [
+        jnp.concatenate(
+            [input_proj[:, p * width + s * wide : p * width + (s + 1) * wide] for p in range(3)], 1
+        )
+        for s in range(stages)
+    ]
+    first_in = gathered(jnp.concatenate([chunks[0], jnp.pad(norm_rows, ((0, 0), (0, cols - width)))]))
+    rest_in = gathered(jnp.concatenate(chunks[1:]))
+    groups = inner // width
+    up_rows = jnp.moveaxis(up_proj.reshape(share, groups, width), 1, 0).reshape(-1, width)
+    packed = jnp.concatenate([up_rows, down_proj, output_proj])
 
     half = size // 2
     own_blocks = block_order[:, me]
@@ -959,63 +1015,63 @@
         6 * streams * rows * width,
     )
 
-    pair_shape = shape_of((3 * size, tokens), BF16)
+    pair_shape = shape_of((count, 3 * size, tokens), BF16)
+    x = after(x, mix_early)
+    weights = gathered(after(packed, rest_in[3]))
     held = []
-    n1t = None
+    n1t = norms = None
+    windows = [(0, share)] + [(share * s, share) for s in range(stages - 1)]
     for s in range(stages):
         first = s == 0
-        operands = [scalars] + ([x, norms] if first else [n1t]) + [cosine, sine] + w_in[s]
-        outs = [pair_shape] * count + ([shape_of((width, rows), BF16)] if first else [])
+        operands = [scalars] + ([x] if first else [n1t]) + [cosine, sine]
+        operands += first_in if first else rest_in
+        outs = [pair_shape]
+        if first:
+            outs += [shape_of((width, rows), BF16), shape_of((8, width), F32)]
         result = run_kernel(
-            functools.partial(qkv_kernel, hps, batches, first),
+            functools.partial(qkv_kernel, hps, batches, first, windows[s][0]),
             "qkv",
             operands,
             [SMEM] + [VMEM] * (len(operands) - 1),
             outs,
-            [
-                pltpu.VMEM((width, 3 * hps * size), BF16),
-                pltpu.VMEM((count, 3 * size, tokens), BF16),
-            ],
-            2 * rows * width * 3 * hps * size,
+            [pltpu.VMEM((width, cols), BF16)],
+            2 * rows * width * cols,
         )
         if first:
-            n1t = result[count]
-        sent = result[:count]
-        held.append([sent[0]] + [exchange(sent[d], "ctx", d) for d in range(1, count)])
+            n1t, norms = result[1:]
+        held.append(swapped(result[0]))
 
     tiles = count * (count + 1) // 2
     one = tokens * tokens * size * 2
-    head_shape = shape_of((size, tokens), BF16)
+    streams_in = count // 2
+    head_shape = shape_of((count, size, tokens), BF16)
     attended = []
     saved = []
     for s in range(stages):
         result = run_kernel(
             functools.partial(attend_kernel, count, scale),
             "attend",
-            [ids] + held[s],
-            [SMEM] + [VMEM] * count,
-            [head_shape] * count
-            + [shape_of((count, size, tokens), F32), shape_of((count, 1, tokens), F32)],
+            [after(ids, saved[-1][1]) if saved else ids, held[s]],
+            [SMEM, VMEM],
+            [head_shape, shape_of((count, size, tokens), F32), shape_of((count, 1, tokens), F32)],
             [
                 pltpu.VMEM((count, size, tokens), BF16),
                 pltpu.VMEM((count, tokens, size), BF16),
                 pltpu.VMEM((count, size, tokens), BF16),
-                pltpu.VMEM((2, tokens, tokens), F32),
-                pltpu.VMEM((1, tokens), F32),
-                pltpu.VMEM((1, tokens), F32),
-                pltpu.VMEM((size, tokens), F32),
-            ],
+                pltpu.VMEM((2, streams_in, tokens, tokens), F32),
+            ]
+            + [pltpu.VMEM((2, 1, tokens), F32)] * (2 * streams_in)
+            + [pltpu.VMEM((2, size, tokens), F32)] * streams_in,
             4 * 2 * one * tiles,
         )
-        saved.append(result[count:])
-        attended += [result[0]] + [exchange(result[d], "ctx", d) for d in range(1, count)]
-
-    mlp_operands = [scalars, mixing, x, grad, norms] + attended + w_out + w_up + w_down
+        saved.append(result[1:])
+        attended.append(swapped(result[0]))
+
     result = run_kernel(
         functools.partial(mlp_kernel, count, stages, hps, batches),
         "mlp",
-        mlp_operands,
-        [SMEM, SMEM, VMEM, VMEM, VMEM] + [VMEM] * (count * stages) + [ANY] * 12,
+        [scalars, mixing, x, grad, norms] + attended + weights,
+        [SMEM, SMEM, VMEM, VMEM, VMEM] + [VMEM] * stages + [ANY] * 4,
         [
             shape_of((rows, inner), BF16),
             shape_of((rows, inner), BF16),
@@ -1026,67 +1082,57 @@
             shape_of((batches, heads, size, tokens), BF16),
             shape_of((8, width), F32),
         ]
-        + [head_shape] * (count * stages),
+        + [head_shape] * stages,
         [
             pltpu.VMEM((width, width), BF16),
             pltpu.VMEM((width, inner), BF16),
             pltpu.VMEM((inner, width), BF16),
             pltpu.VMEM((rows, width), F32),
             pltpu.VMEM((batches, heads, size, tokens), BF16),
-            pltpu.SemaphoreType.DMA((12,)),
+            pltpu.SemaphoreType.DMA((8 + 4 * groups,)),
         ],
         6 * rows * width * inner,
     )
     hidden, dhidden, n2, mid, dmid, dmid_low, ot, norm2_grads = result[:8]
-    head_grads = result[8:]
-    sent_grads = []
-    for s in range(stages):
-        mine = head_grads[s * count : (s + 1) * count]
-        sent_grads.append([mine[0]] + [exchange(mine[d], "ctx", d) for d in range(1, count)])
+    sent_grads = [swapped(value) for value in result[8:]]
 
     sub = inner // 4 // count
-    down_keep, down_send = run_kernel(
+    thin = share // count
+    down_sums = run_kernel(
         functools.partial(down_grad_kernel, count),
         "down_grad",
         [scalars, mixing, hidden, grad],
         [SMEM, SMEM, VMEM, VMEM],
-        [shape_of((2, count, sub, width), BF16)] * 2,
+        [shape_of((2, 2, count // 2, sub, width), BF16)] * 2,
         [],
         2 * rows * width * inner,
     )
-    down_pieces = gather_blocks(reduce_blocks(down_keep, down_send))
-    thin = width // 4 // count
-    up_keep, up_send = run_kernel(
+    up_sums = run_kernel(
         functools.partial(up_out_grad_kernel, count),
         "up_out_grad",
         [scalars, n2, dhidden, ot, dmid_low],
         [SMEM] + [VMEM] * 4,
-        [shape_of((2, count, thin, inner + width), BF16)] * 2,
+        [shape_of((2, 2, count // 2, thin * (groups + 1), width), BF16)] * 2,
         [pltpu.VMEM((width, rows), BF16), pltpu.VMEM((width, rows), BF16)],
         2 * rows * width * (inner + width),
     )
-    up_pieces = gather_blocks(reduce_blocks(up_keep, up_send))
-
-    next_input, mix_last = run_kernel(
-        result_kernel,
-        "result",
-        [scalars, mixing, hidden, mid, prev, grad] + w_down,
-        [SMEM, SMEM] + [VMEM] * 8,
-        [shape_of((rows, width), BF16), shape_of((8, width), F32)],
-        [pltpu.VMEM((rows, width), F32)],
-        2 * rows * width * inner,
-    )
+    down_chip, down_own = chip_first(*down_sums)
+    up_both, up_own = chip_last(*up_sums)
+    down_part, *down_parts = sum_far(down_own)
+    up_part, *up_parts = sum_far(up_own)
+    gates = [(down_sums[0], up_sums[0]), (down_chip, up_both), (down_own, up_own)]
 
     dts = []
-    in_pieces = []
-    cols = 3 * hps * size
+    in_parts = []
     for s in range(stages):
-        back = run_kernel(
+        turn = gates[s] if s < len(gates) else gates[-1]
+        turn = turn + ((back,) if s else ())
+        (back,) = run_kernel(
             functools.partial(attend_back_kernel, count, scale),
             "attend_back",
-            [ids] + held[s] + sent_grads[s] + list(saved[s]),
-            [SMEM] + [VMEM] * (2 * count + 2),
-            [pair_shape] * count,
+            [ids, after(held[s], *turn), sent_grads[s]] + list(saved[s]),
+            [SMEM] + [VMEM] * 4,
+            [pair_shape],
             [
                 pltpu.VMEM((count, size, tokens), BF16),
                 pltpu.VMEM((count, tokens, size), BF16),
@@ -1096,33 +1142,40 @@
                 pltpu.VMEM((count, size, tokens), BF16),
                 pltpu.VMEM((count, tokens, size), BF16),
                 pltpu.VMEM((count, 1, tokens), F32),
-                pltpu.VMEM((2, tokens, tokens), F32),
-                pltpu.VMEM((2, tokens, tokens), F32),
-                pltpu.VMEM((count, size, tokens), F32),
-                pltpu.VMEM((count, tokens, size), F32),
-                pltpu.VMEM((count, tokens, size), F32),
-            ],
+                pltpu.VMEM((2, streams_in, tokens, tokens), F32),
+                pltpu.VMEM((2, streams_in, tokens, tokens), F32),
+            ]
+            + [pltpu.VMEM((2, size, tokens), F32)] * streams_in
+            + [pltpu.VMEM((count, tokens, size), F32)] * (2 * streams_in),
             4 * 5 * one * tiles,
         )
-        arrived = [back[0]] + [exchange(back[d], "ctx", d) for d in range(1, count)]
         dt, keep, send = run_kernel(
             functools.partial(in_grad_kernel, count, hps),
             "in_grad",
-            [scalars, cosine, sine, n1t] + arrived,
-            [SMEM] + [VMEM] * (3 + count),
+            [scalars, cosine, sine, n1t, swapped(back)],
+            [SMEM] + [VMEM] * 4,
             [shape_of((batches, 3, hps, size, tokens), BF16)]
             + [shape_of((2, count, thin, cols), BF16)] * 2,
             [pltpu.VMEM((width, rows), BF16)],
             2 * rows * width * cols,
         )
         dts.append(dt)
-        in_pieces += gather_blocks(reduce_blocks(keep, send))
-
-    flat_in = [piece for pieces in w_in for piece in pieces]
+        in_parts.append(reduce_whole(keep, send))
+
+    next_input, mix_last = run_kernel(
+        functools.partial(result_kernel, (groups * share, inner // 4)),
+        "result",
+        [scalars, mixing, hidden, mid, prev, after(grad, back)] + weights,
+        [SMEM, SMEM] + [VMEM] * 8,
+        [shape_of((rows, width), BF16), shape_of((8, width), F32)],
+        [pltpu.VMEM((rows, width), F32)],
+        2 * rows * width * inner,
+    )
+
     grad_input, norm1_grads = run_kernel(
-        functools.partial(input_grad_kernel, stages),
+        functools.partial(input_grad_kernel, stages, windows),
         "input_grad",
-        [scalars, x, norms, dmid] + dts + flat_in,
+        [scalars, x, norms, dmid] + dts + first_in + rest_in * (stages - 1),
         [SMEM] + [VMEM] * (3 + stages) + [ANY] * (4 * stages),
         [shape_of((rows, width), BF16), shape_of((8, width), F32)],
         [pltpu.VMEM((stages, width, cols), BF16), pltpu.SemaphoreType.DMA((4 * stages,))],
@@ -1132,42 +1185,36 @@
     small = jnp.concatenate(
         [norm1_grads[:2], norm2_grads[:2], mix_early[:streams], mix_last[:1]], axis=0
     )
-    for axis in ("fsdp", "ctx"):
-        bit = 1
-        while bit < lax.axis_size(axis):
-            small = small + exchange(small, axis, bit)
-            bit *= 2
-    norm_total = lax.dynamic_slice_in_dim(small[:4], place * (width // 4), width // 4, 1)
+    small = small + exchange(small, "fsdp", 1)
+    small = small + exchange(small, "fsdp", 2)
+    small = jnp.sum(spread(small, count), axis=0)
+    norm_total = lax.dynamic_slice_in_dim(small[:4], place * share, share, 1)
     mix_total = jnp.sum(small[4:], axis=1)
 
     (grad_down,) = run_kernel(
-        functools.partial(place_kernel, count, (((0, 0, width, 0),),)),
+        functools.partial(place_split_kernel, ((0, 0, sub, 0, width),)),
         "place_down",
-        [scalars] + down_pieces,
-        [SMEM] + [VMEM] * count,
+        [scalars, *down_parts],
+        [SMEM] + [VMEM] * 2,
         [shape_of((count, sub, width), F32)],
         [],
         0,
     )
+    moves = tuple((0, g * thin, thin, g * width, width) for g in range(groups))
     grad_up, grad_out = run_kernel(
-        functools.partial(place_kernel, count, (((0, 0, inner, 0), (1, inner, width, 0)),)),
+        functools.partial(place_split_kernel, moves + ((1, groups * thin, thin, 0, width),)),
         "place_up",
-        [scalars] + up_pieces,
-        [SMEM] + [VMEM] * count,
+        [scalars, *up_parts],
+        [SMEM] + [VMEM] * 2,
         [shape_of((count, thin, inner), F32), shape_of((count, thin, width), F32)],
         [],
         0,
     )
-    wide = hps * size
-    groups = tuple(
-        tuple((0, part * wide, wide, part * width + s * wide) for part in range(3))
-        for s in range(stages)
-    )
     (grad_in,) = run_kernel(
-        functools.partial(place_kernel, count, groups),
+        functools.partial(place_in_kernel, width, hps * size),
         "place_in",
-        [scalars] + in_pieces,
-        [SMEM] + [VMEM] * (count * stages),
+        in_parts,
+        [VMEM] * stages,
         [shape_of((count, thin, 3 * width), F32)],
         [],
         0,
@@ -1176,9 +1223,9 @@
         next_input.reshape(batches, tokens, width),
         grad_input.reshape(batches, tokens, width),
         grad_earlier.reshape(streams, batches, tokens, width),
-        grad_in.reshape(width // 4, 3 * width),
-        grad_out.reshape(width // 4, width),
-        grad_up.reshape(width // 4, inner),
+        grad_in.reshape(share, 3 * width),
+        grad_out.reshape(share, width),
+        grad_up.reshape(share, inner),
         grad_down.reshape(inner // 4, width),
         norm_total[0],
         norm_total[1],

time: 756 us -> 596 us (0.79)
  starting transfers between devices: 202 us -> 106 us
  Pallas kernels: 212 us -> 164 us
  waiting for transfers between devices: 257 us -> 213 us
  other arithmetic: 5.57 us -> 28.4 us
    ppermute x167 -> x25, starting transfers between devices: 202 us -> 19.5 us  [exchange(): return lax.ppermute(value, axis, [(i, i ^ bit) for i in range(size)])]
    ppermute x167 -> x25, waiting for transfers between devices: 257 us -> 87.4 us  [exchange(): return lax.ppermute(value, axis, [(i, i ^ bit) for i in range(size)])]
    all_to_all x0 -> x20, waiting for transfers between devices: none -> 126 us  [swapped(): return lax.all_to_all(value, 'ctx', 0, 0, axis_index_groups=groups)]
    all_to_all x0 -> x20, starting transfers between devices: none -> 86.7 us  [swapped(): return lax.all_to_all(value, 'ctx', 0, 0, axis_index_groups=groups)]
    all_to_all x0 -> x3, blocking collectives: none -> 52.1 us  [swapped(): return lax.all_to_all(value, 'ctx', 0, 0, axis_index_groups=groups)]
    all_gather x1 -> x0, blocking collectives: 50.1 us -> none  [head_body(): norms = lax.all_gather(norm_stack, 'fsdp', axis=1, tiled=True)]
    pallas_call x21, Pallas kernels: 212 us -> 164 us  [run_kernel(): pl.pallas_call(kernel, name=name, in_specs=[spec(s) for s in spaces], out...]
    convert_element_type x15 -> x12, other arithmetic: 2.66 us -> 23.6 us  [added(): return (left.astype(F32) + right.astype(F32)).astype(BF16)]
  transfers between devices with their start and end apart: 167 -> 45, of which waited for: 53 -> 22; matrix products, arithmetic and copies ran while one was open for 1% -> 7% of each run, Pallas kernels for 24% -> 24%
where the time goes in v2:
time: 596 us; the launch traced here: 586 us
  waiting for transfers between devices  213 us (36%)
  Pallas kernels  164 us (28%)
  starting transfers between devices  106 us (18%)
  blocking collectives  52.1 us (9%)
  other arithmetic  28.4 us (5%)
  local copies, waits for them, and re-layouts  21.3 us (4%)
    pallas_call x21, Pallas kernels, run_kernel(): pl.pallas_call(kernel, name=name, in_specs=[spec(s) for s in spaces], out...  164 us
    all_to_all x20, waiting for transfers between devices, swapped(): return lax.all_to_all(value, 'ctx', 0, 0, axis_index_groups=groups)  126 us
    ppermute x25, waiting for transfers between devices, exchange(): return lax.ppermute(value, axis, [(i, i ^ bit) for i in range(size)])  87.4 us
    all_to_all x20, starting transfers between devices, swapped(): return lax.all_to_all(value, 'ctx', 0, 0, axis_index_groups=groups)  86.7 us
    all_to_all x3, blocking collectives, swapped(): return lax.all_to_all(value, 'ctx', 0, 0, axis_index_groups=groups)  52.1 us
    convert_element_type x12, other arithmetic, added(): return (left.astype(F32) + right.astype(F32)).astype(BF16)  23.6 us
    ppermute x25, starting transfers between devices, exchange(): return lax.ppermute(value, axis, [(i, i ^ bit) for i in range(size)])  19.5 us
  transfers between devices with their start and end apart: 45, of which 22 were waited for; matrix products, arithmetic and copies ran while one was open for 7% of the time, Pallas kernels for 24%

profile of v2, /device:TPU:0, one launch (start us, length us, event | category | flops | bytes accessed | tf_op | source)
XLA Modules:
  0.0 586.2 jit_solution(990007066896575646)
XLA Ops:
  6.6 18.7 %collective-permute-done.refs_5_.refs_4_ = bf16[208,768]{1,0:T(8,128)(2,1)S(1)} collective-permute-done((bf16[208,768]{1,0:T(8,128)(2,1)S(1)}, bf16[208,768]{1,0:T(8,128)(2,1)S(1)}, u32[]{:S(2)}, u32[]{:S(2)}) %collective-permute-start) | collective-permute-done | bytes 319520 | tf_op jit(solution)/shard_map/ppermute | solution.py:880
  54.6 10.6 %all-to-all-done.ins = bf16[8,192,256]{2,1,0:T(8,128)(2,1)} async-done(((bf16[8,192,256]{2,1,0:T(8,128)(2,1)}), bf16[8,192,256]{2,1,0:T(8,128)(2,1)}, u32[]{:S(2)}, u32[]{:S(2)}) %all-to-all-start) | async-done | bytes 786464 | tf_op jit(solution)/shard_map/all_to_all | solution.py:888
  73.1 16.2 %all-to-all-done.4.ins = bf16[8,192,256]{2,1,0:T(8,128)(2,1)} async-done(((bf16[8,192,256]{2,1,0:T(8,128)(2,1)}), bf16[8,192,256]{2,1,0:T(8,128)(2,1)}, u32[]{:S(2)}, u32[]{:S(2)}) %all-to-all-start.4) | async-done | bytes 786464 | tf_op jit(solution)/shard_map/all_to_all | solution.py:888
  93.6 12.3 %collective-permute-done.6.refs_4_.w1 = bf16[1728,768]{1,0:T(8,128)(2,1)} collective-permute-done((bf16[1728,768]{1,0:T(8,128)(2,1)S(1)}, bf16[1728,768]{1,0:T(8,128)(2,1)}, u32[]{:S(2)}, u32[]{:S(2)}) %collective-permute-start.6) | collective-permute-done | bytes 2654240 | tf_op jit(solution)/shard_map/ppermute | solution.py:880
  106.5 9.0 %attend.3 = (bf16[8,64,256]{2,1,0:T(8,128)(2,1)}, f32[8,64,256]{2,1,0:T(8,128)}, f32[8,1,256]{2,1,0:T(1,128)}) custom-call(s32[8]{0:T(128)} %fusion.16.ids, bf16[8,192,256]{2,1,0:T(8,128)(2,1)} %all-to-all-done.ins), custom_call_target="tpu_custom_call" | custom-call | flops 2415919104 | bytes 1581088 | tf_op jit(solution)/shard_map/attend/pallas_call | solution.py:408
  121.2 9.0 %attend.4 = (bf16[8,64,256]{2,1,0:T(8,128)(2,1)}, f32[8,64,256]{2,1,0:T(8,128)}, f32[8,1,256]{2,1,0:T(1,128)}) custom-call(s32[8]{0:T(128)} %fusion.16.ids, bf16[8,192,256]{2,1,0:T(8,128)(2,1)} %all-to-all-done.2.ins), custom_call_target="tpu_custom_call" | custom-call | flops 2415919104 | bytes 1581088 | tf_op jit(solution)/shard_map/attend/pallas_call | solution.py:408
  130.2 9.1 %attend.5 = (bf16[8,64,256]{2,1,0:T(8,128)(2,1)}, f32[8,64,256]{2,1,0:T(8,128)}, f32[8,1,256]{2,1,0:T(1,128)}) custom-call(s32[8]{0:T(128)} %fusion.16.ids, bf16[8,192,256]{2,1,0:T(8,128)(2,1)} %all-to-all-done.4.ins), custom_call_target="tpu_custom_call" | custom-call | flops 2415919104 | bytes 1581088 | tf_op jit(solution)/shard_map/attend/pallas_call | solution.py:408
  139.3 15.1 %all_to_all.115.refs_2_ = bf16[8,64,256]{2,1,0:T(8,128)(2,1)} all-to-all(bf16[8,64,256]{2,1,0:T(8,128)(2,1)} %get-tuple-element.76), channel_id=1, replica_groups=mesh['ctx'=8,'fsdp'=4] {'ctx'}, dimensions={0} | all-to-all | bytes 524288 | tf_op jit(solution)/shard_map/all_to_all | solution.py:888
  154.4 12.2 %all_to_all.116.refs_1_ = bf16[8,64,256]{2,1,0:T(8,128)(2,1)} all-to-all(bf16[8,64,256]{2,1,0:T(8,128)(2,1)S(1)} %copy-done.27), channel_id=1, replica_groups=mesh['ctx'=8,'fsdp'=4] {'ctx'}, dimensions={0} | all-to-all | bytes 524288 | tf_op jit(solution)/shard_map/all_to_all | solution.py:888
  166.6 19.1 %mlp.1 = (bf16[512,3072]{1,0:T(8,128)(2,1)}, bf16[512,3072]{1,0:T(8,128)(2,1)}, bf16[512,768]{1,0:T(8,128)(2,1)}, f32[512,768]{1,0:T(8,128)}, f32[512,768]{1,0:T...) custom-call(s32[2]{0:T(128)} %pad_add_fusion.refs_0_.scalars, ...), custom_call_target="tpu_custom_call" | custom-call | flops 7247757312 | bytes 25608220 | tf_op jit(solution)/shard_map/mlp/pallas_call | solution.py:408
  189.3 6.3 %down_grad.1 = (bf16[2,2,4,96,768]{4,3,2,1,0:T(8,128)(2,1)}, bf16[2,2,4,96,768]{4,3,2,1,0:T(8,128)(2,1)}) custom-call(s32[2]{0:T(128)} %pad_add_fusion.refs_0_.scalars, f32[5]{0:T(128)} %mix.7, bf16[512,3072]{1,0:T(8,128)(2,1)} %get-tuple-element.78.hidden, bf16[512,768]{1,0:T(8,128)(2,1)} %bitcast.83), custom_call_target="tpu_custom_call" | custom-call | flops 2415919104 | bytes 8650780 | tf_op jit(solution)/shard_map/down_grad/pallas_call | solution.py:408
  195.6 8.5 %up_out_grad.1 = (bf16[2,2,4,120,768]{4,3,2,1,0:T(8,128)(2,1)}, bf16[2,2,4,120,768]{4,3,2,1,0:T(8,128)(2,1)}) custom-call(s32[2]{0:T(128)} %pad_add_fusion.refs_0_.scalars, bf16[512,768]{1,0:T(8,128)(2,1)} %get-tuple-element.83.n2, bf16[512,3072]{1,0:T(8,128)(2,1)} %get-tuple-element.84.dhidden, bf16[2,12,64,256]{3,2,1,0:T(8,128)(2,1)} %get-tuple-element.85.ot, ...), custom_call_target="tpu_custom_call" | custom-call | flops 3019898880 | bytes 11403272 | tf_op jit(solution)/shard_map/up_out_grad/pallas_call | solution.py:408
  204.8 16.6 %attend_back.3 = bf16[8,192,256]{2,1,0:T(8,128)(2,1)} custom-call(s32[8]{0:T(128)} %fusion.16.ids, bf16[8,192,256]{2,1,0:T(8,128)(2,1)} %all-to-all-done.ins, bf16[8,64,256]{2,1,0:T(8,128)(2,1)} %copy-done.26, f32[8,64,256]{2,1,0:T(8,128)} %get-tuple-element.91.ot, f32[8,1,256]{2,1,0:T(1,128)} %get-tuple-element.70.lse), custom_call_target="tpu_custom_call" | custom-call | flops 6039797760 | bytes 2367520 | tf_op jit(solution)/shard_map/attend_back/pallas_call | solution.py:408
  221.4 6.1 %all-to-all-start.9 = ((bf16[8,192,256]{2,1,0:T(8,128)(2,1)}), bf16[8,192,256]{2,1,0:T(8,128)(2,1)S(1)}, u32[]{:S(2)}, u32[]{:S(2)}) async-start(bf16[8,192,256]{2,1,0:T(8,128)(2,1)} %attend_back.3), calls=%async_computation.9 | async-start | bytes 1572864 | tf_op jit(solution)/shard_map/all_to_all | solution.py:888
  227.7 20.6 %all-to-all-done.9.grads = bf16[8,192,256]{2,1,0:T(8,128)(2,1)S(1)} async-done(((bf16[8,192,256]{2,1,0:T(8,128)(2,1)}), bf16[8,192,256]{2,1,0:T(8,128)(2,1)S(1)}, u32[]{:S(2)}, u32[]{:S(2)}) %all-to-all-start.9) | async-done | bytes 786464 | tf_op jit(solution)/shard_map/all_to_all | solution.py:888
  280.9 10.3 %collective-permute-done.10 = bf16[2,4,96,768]{3,2,1,0:T(8,128)(2,1)} collective-permute-done((bf16[2,4,96,768]{3,2,1,0:T(8,128)(2,1)}, bf16[2,4,96,768]{3,2,1,0:T(8,128)(2,1)}, u32[]{:S(2)}, u32[]{:S(2)}) %collective-permute-start.10) | collective-permute-done | bytes 1179680 | tf_op jit(solution)/shard_map/ppermute | solution.py:880
  301.9 16.8 %all-to-all-done.8.grads = bf16[8,64,256]{2,1,0:T(8,128)(2,1)S(1)} async-done(((bf16[8,64,256]{2,1,0:T(8,128)(2,1)}), bf16[8,64,256]{2,1,0:T(8,128)(2,1)S(1)}, u32[]{:S(2)}, u32[]{:S(2)}) %all-to-all-start.8) | async-done | bytes 262176 | tf_op jit(solution)/shard_map/all_to_all | solution.py:888
  324.2 9.4 %collective-permute-done.11 = bf16[4,96,768]{2,1,0:T(8,128)(2,1)} collective-permute-done((bf16[4,96,768]{2,1,0:T(8,128)(2,1)}, bf16[4,96,768]{2,1,0:T(8,128)(2,1)}, u32[]{:S(2)}, u32[]{:S(2)}) %collective-permute-start.11) | collective-permute-done | bytes 589856 | tf_op jit(solution)/shard_map/ppermute | solution.py:880
  343.5 16.7 %attend_back.4 = bf16[8,192,256]{2,1,0:T(8,128)(2,1)} custom-call(s32[8]{0:T(128)} %fusion.16.ids, bf16[8,192,256]{2,1,0:T(8,128)(2,1)} %all-to-all-done.2.ins, bf16[8,64,256]{2,1,0:T(8,128)(2,1)} %all-to-all-done.7.grads, f32[8,64,256]{2,1,0:T(8,128)} %get-tuple-element.94.ot, f32[8,1,256]{2,1,0:T(1,128)} %get-tuple-element.74.lse), custom_call_target="tpu_custom_call" | custom-call | flops 6039797760 | bytes 2367520 | tf_op jit(solution)/shard_map/attend_back/pallas_call | solution.py:408
  367.7 16.7 %all-to-all-done.10.grads = bf16[8,192,256]{2,1,0:T(8,128)(2,1)S(1)} async-done(((bf16[8,192,256]{2,1,0:T(8,128)(2,1)}), bf16[8,192,256]{2,1,0:T(8,128)(2,1)S(1)}, u32[]{:S(2)}, u32[]{:S(2)}) %all-to-all-start.10) | async-done | bytes 786464 | tf_op jit(solution)/shard_map/all_to_all | solution.py:888
  390.9 16.6 %attend_back.5 = bf16[8,192,256]{2,1,0:T(8,128)(2,1)} custom-call(s32[8]{0:T(128)} %fusion.16.ids, bf16[8,192,256]{2,1,0:T(8,128)(2,1)} %all-to-all-done.4.ins, bf16[8,64,256]{2,1,0:T(8,128)(2,1)} %copy-done.24, f32[8,64,256]{2,1,0:T(8,128)} %get-tuple-element.97.ot, f32[8,1,256]{2,1,0:T(1,128)} %get-tuple-element.98.lse), custom_call_target="tpu_custom_call" | custom-call | flops 6039797760 | bytes 2367520 | tf_op jit(solution)/shard_map/attend_back/pallas_call | solution.py:408
  407.5 24.8 %all_to_all.117.grads = bf16[8,192,256]{2,1,0:T(8,128)(2,1)} all-to-all(bf16[8,192,256]{2,1,0:T(8,128)(2,1)} %attend_back.5), channel_id=1, replica_groups=mesh['ctx'=8,'fsdp'=4] {'ctx'}, dimensions={0} | all-to-all | bytes 1572864 | tf_op jit(solution)/shard_map/all_to_all | solution.py:888
  440.1 9.8 %result.1 = (bf16[512,768]{1,0:T(8,128)(2,1)}, f32[8,768]{1,0:T(8,128)}) custom-call(s32[2]{0:T(128)} %pad_add_fusion.refs_0_.scalars, f32[5]{0:T(128)} %mix.7, bf16[512,3072]{1,0:T(8,128)(2,1)} %get-tuple-element.78.hidden, f32[512,768]{1,0:T(8,128)} %get-tuple-element.79.mid, f32[512,768]{1,0:T(8,128)} %get-tuple-element.80.prev, ...), custom_call_target="tpu_custom_call" | custom-call | flops 2415919104 | bytes 18505756 | tf_op jit(solution)/shard_map/result/pallas_call | solution.py:408
  453.8 8.3 %input_grad.1 = (bf16[512,768]{1,0:T(8,128)(2,1)}, f32[8,768]{1,0:T(8,128)}) custom-call(s32[2]{0:T(128)} %pad_add_fusion.refs_0_.scalars, bf16[512,768]{1,0:T(8,128)(2,1)} %bitcast.91, f32[8,768]{1,0:T(8,128)} %get-tuple-element.67.norms, f32[512,768]{1,0:T(8,128)} %get-tuple-element.101.dmid, bf16[2,3,4,64,256]{4,3,2,1,0:T(8,128)(2,1)} %get-tuple-element.102.refs_0_, ...), custom_call_target="tpu_custom_call" | custom-call | flops 1811939328 | bytes 11550728 | tf_op jit(solution)/shard_map/input_grad/pallas_call | solution.py:408
  466.5 8.1 %collective-permute-done.24 = f32[9,768]{1,0:T(8,128)S(1)} collective-permute-done((f32[9,768]{1,0:T(8,128)S(1)}, f32[9,768]{1,0:T(8,128)S(1)}, u32[]{:S(2)}, u32[]{:S(2)}) %collective-permute-start.24) | collective-permute-done | bytes 27680 | tf_op jit(solution)/shard_map/ppermute | solution.py:880
  483.3 9.3 %all-to-all-done.22 = f32[8,9,768]{2,1,0:T(8,128)S(1)} async-done(((f32[8,9,768]{2,1,0:T(8,128)}), f32[8,9,768]{2,1,0:T(8,128)S(1)}, u32[]{:S(2)}, u32[]{:S(2)}) %all-to-all-start.22) | async-done | bytes 221216 | tf_op jit(solution)/shard_map/all_to_all | solution.py:888
  496.3 9.3 %all-to-all-done.14 = bf16[8,24,768]{2,1,0:T(8,128)(2,1)S(1)} async-done(((bf16[8,24,768]{2,1,0:T(8,128)(2,1)}), bf16[8,24,768]{2,1,0:T(8,128)(2,1)S(1)}, u32[]{:S(2)}, u32[]{:S(2)}) %all-to-all-start.14) | async-done | bytes 294944 | tf_op jit(solution)/shard_map/all_to_all | solution.py:888
  517.7 9.4 %all-to-all-done.19.near = bf16[4,120,768]{2,1,0:T(8,128)(2,1)S(1)} async-done(((bf16[4,120,768]{2,1,0:T(8,128)(2,1)}), bf16[4,120,768]{2,1,0:T(8,128)(2,1)S(1)}, u32[]{:S(2)}, u32[]{:S(2)}) %all-to-all-start.19) | async-done | bytes 737312 | tf_op jit(solution)/shard_map/all_to_all | solution.py:888
  531.5 8.4 %all-to-all-done.16 = bf16[8,24,768]{2,1,0:T(8,128)(2,1)S(1)} async-done(((bf16[8,24,768]{2,1,0:T(8,128)(2,1)}), bf16[8,24,768]{2,1,0:T(8,128)(2,1)S(1)}, u32[]{:S(2)}, u32[]{:S(2)}) %all-to-all-start.16) | async-done | bytes 294944 | tf_op jit(solution)/shard_map/all_to_all | solution.py:888
  546.3 6.3 %all-to-all-done.15.refs_1_ = bf16[8,24,768]{2,1,0:T(8,128)(2,1)S(1)} async-done(((bf16[8,24,768]{2,1,0:T(8,128)(2,1)}), bf16[8,24,768]{2,1,0:T(8,128)(2,1)S(1)}, u32[]{:S(2)}, u32[]{:S(2)}) %all-to-all-start.15) | async-done | bytes 294944 | tf_op jit(solution)/shard_map/all_to_all | solution.py:888
  556.8 8.0 %collective-permute-done.22.far = bf16[4,96,768]{2,1,0:T(8,128)(2,1)} collective-permute-done((bf16[4,96,768]{2,1,0:T(8,128)(2,1)S(1)}, bf16[4,96,768]{2,1,0:T(8,128)(2,1)}, u32[]{:S(2)}, u32[]{:S(2)}) %collective-permute-start.22) | collective-permute-done | bytes 589856 | tf_op jit(solution)/shard_map/ppermute | solution.py:880
  569.0 9.5 %collective-permute-done.21.far = bf16[4,120,768]{2,1,0:T(8,128)(2,1)S(1)} collective-permute-done((bf16[4,120,768]{2,1,0:T(8,128)(2,1)S(1)}, bf16[4,120,768]{2,1,0:T(8,128)(2,1)S(1)}, u32[]{:S(2)}, u32[]{:S(2)}) %collective-permute-start.21) | collective-permute-done | bytes 737312 | tf_op jit(solution)/shard_map/ppermute | solution.py:880
  (202 shorter events, 197.7 us)
Async XLA Ops:
  2.1 23.9 %collective-permute-start.3 = (bf16[384,768]{1,0:T(8,128)(2,1)S(1)}, bf16[384,768]{1,0:T(8,128)(2,1)}, u32[]{:S(2)}, u32[]{:S(2)}) collective-permute-start(bf16[384,768]{1,0:T(8,128)(2,1)S(1)} %maximum_maximum_fusion.refs_4_.refs_7_.refs_11_), channel_id=1, source_target_pairs={{0,2},{1,3},{2,0},{3,1},{4,6},{5,7},{6,4},{7,5},{8,10},{9,11},{10,... | collective-permute-start | bytes 1769480 | tf_op jit(solution)/shard_map/ppermute | solution.py:880
  6.1 19.2 %collective-permute-start = (bf16[208,768]{1,0:T(8,128)(2,1)S(1)}, bf16[208,768]{1,0:T(8,128)(2,1)S(1)}, u32[]{:S(2)}, u32[]{:S(2)}) collective-permute-start(bf16[208,768]{1,0:T(8,128)(2,1)S(1)} %pad_maximum_fusion.1.refs_4_.refs_3_), channel_id=1, source_target_pairs={{0,2},{1,3},{2,0},{3,1},{4,6},{5,7},{6,4},{7,5},{8,10},{9,11},{10,... | collective-permute-start | bytes 958472 | tf_op jit(solution)/shard_map/ppermute | solution.py:880
  6.2 27.7 %collective-permute-start.1 = (bf16[208,768]{1,0:T(8,128)(2,1)S(1)}, bf16[208,768]{1,0:T(8,128)(2,1)S(1)}, u32[]{:S(2)}, u32[]{:S(2)}) collective-permute-start(bf16[208,768]{1,0:T(8,128)(2,1)S(1)} %pad_maximum_fusion.1.refs_4_.refs_3_), channel_id=1, source_target_pairs={{0,1},{1,0},{2,3},{3,2},{4,5},{5,4},{6,7},{7,6},{8,9},{9,8},{10,11... | collective-permute-start | bytes 958472 | tf_op jit(solution)/shard_map/ppermute | solution.py:880
  26.0 20.5 %collective-permute-start.5 = (bf16[384,768]{1,0:T(8,128)(2,1)}, bf16[384,768]{1,0:T(8,128)(2,1)}, u32[]{:S(2)}, u32[]{:S(2)}) collective-permute-start(bf16[384,768]{1,0:T(8,128)(2,1)} %collective-permute-done.3.refs_5_.refs_8_.refs_12_), channel_id=1, source_target_pairs={{0,1},{1,0},{2,3},{3,2},{4,5},{5,4},{6,7},{7,6},{8,9},{9,8},{10,11... | collective-permute-start | bytes 1769480 | tf_op jit(solution)/shard_map/ppermute | solution.py:880
  38.6 26.6 %all-to-all-start = ((bf16[8,192,256]{2,1,0:T(8,128)(2,1)}), bf16[8,192,256]{2,1,0:T(8,128)(2,1)}, u32[]{:S(2)}, u32[]{:S(2)}) async-start(bf16[8,192,256]{2,1,0:T(8,128)(2,1)} %get-tuple-element.68), calls=%async_computation | async-start | bytes 1572864 | tf_op jit(solution)/shard_map/all_to_all | solution.py:888
  46.5 59.4 %collective-permute-start.6 = (bf16[1728,768]{1,0:T(8,128)(2,1)S(1)}, bf16[1728,768]{1,0:T(8,128)(2,1)}, u32[]{:S(2)}, u32[]{:S(2)}) collective-permute-start(bf16[1728,768]{1,0:T(8,128)(2,1)S(1)} %pad_maximum_fusion.refs_3_.w0), channel_id=1, source_target_pairs={{0,2},{1,3},{2,0},{3,1},{4,6},{5,7},{6,4},{7,5},{8,10},{9,11},{10,... | collective-permute-start | bytes 7962632 | tf_op jit(solution)/shard_map/ppermute | solution.py:880
  65.2 24.1 %all-to-all-start.4 = ((bf16[8,192,256]{2,1,0:T(8,128)(2,1)}), bf16[8,192,256]{2,1,0:T(8,128)(2,1)}, u32[]{:S(2)}, u32[]{:S(2)}) async-start(bf16[8,192,256]{2,1,0:T(8,128)(2,1)} %qkv.5), calls=%async_computation.4 | async-start | bytes 1572864 | tf_op jit(solution)/shard_map/all_to_all | solution.py:888
  89.3 26.2 %all-to-all-start.2 = ((bf16[8,192,256]{2,1,0:T(8,128)(2,1)}), bf16[8,192,256]{2,1,0:T(8,128)(2,1)}, u32[]{:S(2)}, u32[]{:S(2)}) async-start(bf16[8,192,256]{2,1,0:T(8,128)(2,1)} %qkv.4), calls=%async_computation.2 | async-start | bytes 1572864 | tf_op jit(solution)/shard_map/all_to_all | solution.py:888
  93.5 73.1 %collective-permute-start.7 = (bf16[1728,768]{1,0:T(8,128)(2,1)S(1)}, bf16[1728,768]{1,0:T(8,128)(2,1)}, u32[]{:S(2)}, u32[]{:S(2)}) collective-permute-start(bf16[1728,768]{1,0:T(8,128)(2,1)S(1)} %pad_maximum_fusion.refs_3_.w0), channel_id=1, source_target_pairs={{0,1},{1,0},{2,3},{3,2},{4,5},{5,4},{6,7},{7,6},{8,9},{9,8},{10,11... | collective-permute-start | bytes 7962632 | tf_op jit(solution)/shard_map/ppermute | solution.py:880
  105.9 60.7 %collective-permute-start.8 = (bf16[1728,768]{1,0:T(8,128)(2,1)}, bf16[1728,768]{1,0:T(8,128)(2,1)}, u32[]{:S(2)}, u32[]{:S(2)}) collective-permute-start(bf16[1728,768]{1,0:T(8,128)(2,1)} %collective-permute-done.6.refs_4_.w1), channel_id=1, source_target_pairs={{0,1},{1,0},{2,3},{3,2},{4,5},{5,4},{6,7},{7,6},{8,9},{9,8},{10,11... | collective-permute-start | bytes 7962632 | tf_op jit(solution)/shard_map/ppermute | solution.py:880
  115.5 23.8 %all-to-all-start.1 = ((bf16[8,64,256]{2,1,0:T(8,128)(2,1)}), bf16[8,64,256]{2,1,0:T(8,128)(2,1)S(1)}, u32[]{:S(2)}, u32[]{:S(2)}) async-start(bf16[8,64,256]{2,1,0:T(8,128)(2,1)} %get-tuple-element.69), calls=%async_computation.1 | async-start | bytes 524288 | tf_op jit(solution)/shard_map/all_to_all | solution.py:888
  185.7 18.4 %all-to-all-start.6 = ((bf16[8,64,256]{2,1,0:T(8,128)(2,1)}), bf16[8,64,256]{2,1,0:T(8,128)(2,1)S(1)}, u32[]{:S(2)}, u32[]{:S(2)}) async-start(bf16[8,64,256]{2,1,0:T(8,128)(2,1)} %get-tuple-element.90), calls=%async_computation.6 | async-start | bytes 524288 | tf_op jit(solution)/shard_map/all_to_all | solution.py:888
  204.1 53.9 %collective-permute-start.9 = (bf16[2,2,4,96,768]{4,3,2,1,0:T(8,128)(2,1)}, bf16[2,2,4,96,768]{4,3,2,1,0:T(8,128)(2,1)}, u32[]{:S(2)}, u32[]{:S(2)}) collective-permute-start(bf16[2,2,4,96,768]{4,3,2,1,0:T(8,128)(2,1)} %get-tuple-element.82), channel_id=1, source_target_pairs={{0,1},{1,0},{2,3},{3,2},{4,5},{5,4},{6,7},{7,6},{8,9},{9,8},{10,11... | collective-permute-start | bytes 7077896 | tf_op jit(solution)/shard_map/ppermute | solution.py:880
  221.4 26.9 %all-to-all-start.9 = ((bf16[8,192,256]{2,1,0:T(8,128)(2,1)}), bf16[8,192,256]{2,1,0:T(8,128)(2,1)S(1)}, u32[]{:S(2)}, u32[]{:S(2)}) async-start(bf16[8,192,256]{2,1,0:T(8,128)(2,1)} %attend_back.3), calls=%async_computation.9 | async-start | bytes 1572864 | tf_op jit(solution)/shard_map/all_to_all | solution.py:888
  227.5 41.0 %collective-permute-start.12 = (bf16[2,2,4,120,768]{4,3,2,1,0:T(8,128)(2,1)}, bf16[2,2,4,120,768]{4,3,2,1,0:T(8,128)(2,1)}, u32[]{:S(2)}, u32[]{:S(2)}) collective-permute-start(bf16[2,2,4,120,768]{4,3,2,1,0:T(8,128)(2,1)} %get-tuple-element.88), channel_id=1, source_target_pairs={{0,1},{1,0},{2,3},{3,2},{4,5},{5,4},{6,7},{7,6},{8,9},{9,8},{10,11... | collective-permute-start | bytes 8847368 | tf_op jit(solution)/shard_map/ppermute | solution.py:880
  260.5 30.6 %collective-permute-start.10 = (bf16[2,4,96,768]{3,2,1,0:T(8,128)(2,1)}, bf16[2,4,96,768]{3,2,1,0:T(8,128)(2,1)}, u32[]{:S(2)}, u32[]{:S(2)}) collective-permute-start(bf16[2,4,96,768]{3,2,1,0:T(8,128)(2,1)} %fusion.4), channel_id=1, source_target_pairs={{0,2},{1,3},{2,0},{3,1},{4,6},{5,7},{6,4},{7,5},{8,10},{9,11},{10,... | collective-permute-start | bytes 3538952 | tf_op jit(solution)/shard_map/ppermute | solution.py:880
  274.1 20.2 %all-to-all-start.12 = ((bf16[8,24,768]{2,1,0:T(8,128)(2,1)}), bf16[8,24,768]{2,1,0:T(8,128)(2,1)S(1)}, u32[]{:S(2)}, u32[]{:S(2)}) async-start(bf16[8,24,768]{2,1,0:T(8,128)(2,1)} %fusion.8), calls=%async_computation.12 | async-start | bytes 589824 | tf_op jit(solution)/shard_map/all_to_all | solution.py:888
  278.9 61.8 %collective-permute-start.13 = (bf16[2,4,120,768]{3,2,1,0:T(8,128)(2,1)}, bf16[2,4,120,768]{3,2,1,0:T(8,128)(2,1)}, u32[]{:S(2)}, u32[]{:S(2)}) collective-permute-start(bf16[2,4,120,768]{3,2,1,0:T(8,128)(2,1)} %slice_bitcast_fusion), channel_id=1, source_target_pairs={{0,4},{4,0},{8,12},{12,8},{16,20},{20,16},{24,28},{28,24},{1,5},{5... | collective-permute-start | bytes 4423688 | tf_op jit(solution)/shard_map/ppermute | solution.py:880
  294.3 24.4 %all-to-all-start.8 = ((bf16[8,64,256]{2,1,0:T(8,128)(2,1)}), bf16[8,64,256]{2,1,0:T(8,128)(2,1)S(1)}, u32[]{:S(2)}, u32[]{:S(2)}) async-start(bf16[8,64,256]{2,1,0:T(8,128)(2,1)} %get-tuple-element.96), calls=%async_computation.8 | async-start | bytes 524288 | tf_op jit(solution)/shard_map/all_to_all | solution.py:888
  299.8 33.8 %collective-permute-start.11 = (bf16[4,96,768]{2,1,0:T(8,128)(2,1)}, bf16[4,96,768]{2,1,0:T(8,128)(2,1)}, u32[]{:S(2)}, u32[]{:S(2)}) collective-permute-start(bf16[4,96,768]{2,1,0:T(8,128)(2,1)} %slice_bitcast_fusion.4), channel_id=1, source_target_pairs={{0,4},{4,0},{8,12},{12,8},{16,20},{20,16},{24,28},{28,24},{1,5},{5... | collective-permute-start | bytes 1769480 | tf_op jit(solution)/shard_map/ppermute | solution.py:880
  336.5 23.6 %all-to-all-start.20 = ((bf16[4,96,768]{2,1,0:T(8,128)(2,1)}), bf16[4,96,768]{2,1,0:T(8,128)(2,1)S(1)}, u32[]{:S(2)}, u32[]{:S(2)}) async-start(bf16[4,96,768]{2,1,0:T(8,128)(2,1)} %fusion.5), calls=%async_computation.20 | async-start | bytes 1179648 | tf_op jit(solution)/shard_map/all_to_all | solution.py:888
  360.2 24.2 %all-to-all-start.10 = ((bf16[8,192,256]{2,1,0:T(8,128)(2,1)}), bf16[8,192,256]{2,1,0:T(8,128)(2,1)S(1)}, u32[]{:S(2)}, u32[]{:S(2)}) async-start(bf16[8,192,256]{2,1,0:T(8,128)(2,1)} %attend_back.4), calls=%async_computation.10 | async-start | bytes 1572864 | tf_op jit(solution)/shard_map/all_to_all | solution.py:888
  366.2 22.6 %collective-permute-start.14 = (bf16[4,120,768]{2,1,0:T(8,128)(2,1)}, bf16[4,120,768]{2,1,0:T(8,128)(2,1)}, u32[]{:S(2)}, u32[]{:S(2)}) collective-permute-start(bf16[4,120,768]{2,1,0:T(8,128)(2,1)} %slice_bitcast_fusion.2), channel_id=1, source_target_pairs={{0,2},{1,3},{2,0},{3,1},{4,6},{5,7},{6,4},{7,5},{8,10},{9,11},{10,... | collective-permute-start | bytes 2211848 | tf_op jit(solution)/shard_map/ppermute | solution.py:880
  385.3 22.2 %all-to-all-start.21 = ((bf16[4,96,768]{2,1,0:T(8,128)(2,1)}), bf16[4,96,768]{2,1,0:T(8,128)(2,1)S(1)}, u32[]{:S(2)}, u32[]{:S(2)}) async-start(bf16[4,96,768]{2,1,0:T(8,128)(2,1)} %broadcast_in_dim.19), calls=%async_computation.21 | async-start | bytes 1179648 | tf_op jit(solution)/shard_map/all_to_all | solution.py:888
  432.3 42.3 %all-to-all-start.18 = ((bf16[4,120,768]{2,1,0:T(8,128)(2,1)}), bf16[4,120,768]{2,1,0:T(8,128)(2,1)S(1)}, u32[]{:S(2)}, u32[]{:S(2)}) async-start(bf16[4,120,768]{2,1,0:T(8,128)(2,1)} %fusion.2), calls=%async_computation.18 | async-start | bytes 1474560 | tf_op jit(solution)/shard_map/all_to_all | solution.py:888
  439.3 24.1 %collective-permute-start.17 = (bf16[2,8,24,768]{3,2,1,0:T(8,128)(2,1)}, bf16[2,8,24,768]{3,2,1,0:T(8,128)(2,1)S(1)}, u32[]{:S(2)}, u32[]{:S(2)}) collective-permute-start(bf16[2,8,24,768]{3,2,1,0:T(8,128)(2,1)} %get-tuple-element.110), channel_id=1, source_target_pairs={{0,1},{1,0},{2,3},{3,2},{4,5},{5,4},{6,7},{7,6},{8,9},{9,8},{10,11... | collective-permute-start | bytes 1769480 | tf_op jit(solution)/shard_map/ppermute | solution.py:880
  464.3 17.0 %collective-permute-start.18 = (bf16[8,24,768]{2,1,0:T(8,128)(2,1)}, bf16[8,24,768]{2,1,0:T(8,128)(2,1)}, u32[]{:S(2)}, u32[]{:S(2)}) collective-permute-start(bf16[8,24,768]{2,1,0:T(8,128)(2,1)} %fusion.12), channel_id=1, source_target_pairs={{0,2},{1,3},{2,0},{3,1},{4,6},{5,7},{6,4},{7,5},{8,10},{9,11},{10,... | collective-permute-start | bytes 884744 | tf_op jit(solution)/shard_map/ppermute | solution.py:880
  475.4 17.2 %all-to-all-start.22 = ((f32[8,9,768]{2,1,0:T(8,128)}), f32[8,9,768]{2,1,0:T(8,128)S(1)}, u32[]{:S(2)}, u32[]{:S(2)}) async-start(f32[8,9,768]{2,1,0:T(8,128)} %broadcast_in_dim.20), calls=%async_computation.22 | async-start | bytes 786432 | tf_op jit(solution)/shard_map/all_to_all | solution.py:888
  506.5 20.7 %all-to-all-start.19 = ((bf16[4,120,768]{2,1,0:T(8,128)(2,1)}), bf16[4,120,768]{2,1,0:T(8,128)(2,1)S(1)}, u32[]{:S(2)}, u32[]{:S(2)}) async-start(bf16[4,120,768]{2,1,0:T(8,128)(2,1)} %broadcast_in_dim.18), calls=%async_computation.19 | async-start | bytes 1474560 | tf_op jit(solution)/shard_map/all_to_all | solution.py:888
  544.1 20.7 %collective-permute-start.22 = (bf16[4,96,768]{2,1,0:T(8,128)(2,1)S(1)}, bf16[4,96,768]{2,1,0:T(8,128)(2,1)}, u32[]{:S(2)}, u32[]{:S(2)}) collective-permute-start(bf16[4,96,768]{2,1,0:T(8,128)(2,1)S(1)} %all-to-all-done.21.near), channel_id=1, source_target_pairs={{0,4},{4,0},{8,12},{12,8},{16,20},{20,16},{24,28},{28,24},{1,5},{5... | collective-permute-start | bytes 1769480 | tf_op jit(solution)/shard_map/ppermute | solution.py:880
  546.0 32.5 %collective-permute-start.21 = (bf16[4,120,768]{2,1,0:T(8,128)(2,1)S(1)}, bf16[4,120,768]{2,1,0:T(8,128)(2,1)S(1)}, u32[]{:S(2)}, u32[]{:S(2)}) collective-permute-start(bf16[4,120,768]{2,1,0:T(8,128)(2,1)S(1)} %all-to-all-done.19.near), channel_id=1, source_target_pairs={{0,4},{4,0},{8,12},{12,8},{16,20},{20,16},{24,28},{28,24},{1,5},{5... | collective-permute-start | bytes 2211848 | tf_op jit(solution)/shard_map/ppermute | solution.py:880
  553.4 29.2 %all-to-all-start.17 = ((bf16[8,24,768]{2,1,0:T(8,128)(2,1)}), bf16[8,24,768]{2,1,0:T(8,128)(2,1)S(1)}, u32[]{:S(2)}, u32[]{:S(2)}) async-start(bf16[8,24,768]{2,1,0:T(8,128)(2,1)} %broadcast_in_dim.17), calls=%async_computation.17 | async-start | bytes 589824 | tf_op jit(solution)/shard_map/all_to_all | solution.py:888
  (47 other events, 771.1 us)

commit v3 on v2

--- a/solution.py
+++ b/solution.py
@@ -544,7 +544,7 @@
 
 
 def attend_back_kernel(
-    count, scale, ids, ins, grads, ot, lse, outs, qt, qq, kt, kk, vv, gt, gg, delta, scores, gains, *sums
+    count, scale, stage, ids, ins, grads, ot, lse, outs, qt, qq, kt, kk, vv, gt, gg, delta, scores, gains, *sums
 ):
     streams = count // 2
     dqs, dks, dvs = sums[:streams], sums[streams : 2 * streams], sums[2 * streams :]
@@ -560,7 +560,7 @@
         qq[slot] = q.T
         kk[slot] = k.T
         vv[slot] = block[2 * size :].T
-        g = grads[d]
+        g = grads[d, stage * size : (stage + 1) * size, :]
         gt[slot] = g
         gg[slot] = g.T
         delta[slot] = jnp.sum(g.astype(F32) * ot[slot], axis=0, keepdims=True)
@@ -616,13 +616,14 @@
 
 
 def mlp_kernel(count, stages, hps, batches, scalars, mix, x, grad, norms, *refs):
-    heads = refs[:stages]
-    pieces = refs[stages : stages + 4]
-    refs = refs[stages + 4 :]
+    heads = refs[0]
+    pieces = refs[1:5]
+    refs = refs[5:]
     hidden, dhidden, n2_out, mid_out, dmid_out, dmid_low, ot, norm_grads = refs[:8]
-    head_grads = refs[8 : 8 + stages]
-    out_scr, up_scr, down_scr, dn2, got, sems = refs[8 + stages :]
+    head_grads = refs[8]
+    out_scr, up_scr, down_scr, dn2, got, sems = refs[9:]
     width = x.shape[1]
+    size = ot.shape[2]
     share = width // 4
     groups = up_scr.shape[1] // width
     deep = down_scr.shape[0] // 4
@@ -637,7 +638,9 @@
     )
     for stage in range(stages):
         for slot in range(count):
-            ot[slot // hps, stage * hps + slot % hps] = heads[stage][slot]
+            ot[slot // hps, stage * hps + slot % hps] = heads[
+                slot, stage * size : (stage + 1) * size, :
+            ]
     for copy in copies_out:
         copy.wait()
     tokens = x.shape[0] // batches
@@ -699,7 +702,9 @@
     norm_grads[1:2, :] = bias_sum
     for stage in range(stages):
         for slot in range(count):
-            head_grads[stage][slot] = got[slot // hps, stage * hps + slot % hps]
+            head_grads[slot, stage * size : (stage + 1) * size, :] = got[
+                slot // hps, stage * hps + slot % hps
+            ]
 
 
 def result_kernel(window, scalars, mix, hidden, mid, prev, grad, w0, w1, w2, w3, out, out_mix, acc):
@@ -718,12 +723,11 @@
     target = outs[order // 2]
     rows = value.shape[0] // count
     low = value.astype(BF16)
-    bit = lax.rem(me, jnp.int32(2))
     for sub in range(count):
-        side = lax.bitwise_xor(bit, jnp.int32(sub % 2))
-        target[order % 2, side, sub // 2, first : first + rows, :] = low[
-            sub * rows : (sub + 1) * rows, :
-        ]
+        slot = lax.bitwise_xor(me, jnp.int32(sub))
+        target[order % 2, lax.rem(slot, jnp.int32(2)), lax.div(slot, jnp.int32(2)), first : first + rows, :] = (
+            low[sub * rows : (sub + 1) * rows, :]
+        )
 
 
 def down_grad_kernel(count, scalars, mix, hidden, grad, keep, send):
@@ -776,21 +780,21 @@
         )
 
 
-def in_grad_kernel(count, hps, scalars, cosine, sine, n1t, grads, dt, keep, send, left):
-    batches = dt.shape[0]
-    size = dt.shape[3]
+def grads_kernel(count, window, scalars, mix, hidden, mid, prev, grad, w0, w1, w2, w3, n2, dhidden, ot, dmid, *refs):
+    down, up, (out, out_mix), (acc, left, whole) = refs[:2], refs[2:4], refs[4:6], refs[6:]
+    down_grad_kernel(count, scalars, mix, hidden, grad, *down)
+    up_out_grad_kernel(count, scalars, n2, dhidden, ot, dmid, *up, left, whole)
+    result_kernel(window, scalars, mix, hidden, mid, prev, grad, w0, w1, w2, w3, out, out_mix, acc)
+
+
+def in_grad_kernel(count, hps, natural, scalars, cosine, sine, n1t, *refs):
+    stages = (len(refs) - 3) // 2
+    dts = refs[stages : 2 * stages]
+    keep, send, left = refs[2 * stages :]
+    batches = dts[0].shape[0]
+    size = dts[0].shape[3]
     half = size // 2
-    tokens = dt.shape[4]
-    for slot in range(count):
-        batch, head = slot // hps, slot % hps
-        c = cosine[batch]
-        s = sine[batch]
-        for part in range(2):
-            top = grads[slot, part * size : part * size + half, :].astype(F32)
-            low = grads[slot, part * size + half : (part + 1) * size, :].astype(F32)
-            dt[batch, part, head, 0:half, :] = (top * c + low * s).astype(BF16)
-            dt[batch, part, head, half:size, :] = (low * c - top * s).astype(BF16)
-        dt[batch, 2, head] = grads[slot, 2 * size :, :]
+    tokens = dts[0].shape[4]
     width = n1t.shape[0]
     rows = width // 4
     thin = rows // count
@@ -798,18 +802,44 @@
         here = pl.ds(pl.multiple_of(block_index(scalars, order) * rows, rows), rows)
         left[order * rows : (order + 1) * rows, :] = n1t[here, :]
     cols = 3 * hps * size
-    value = None
-    for batch in range(batches):
-        term = mm(
-            left[:, batch * tokens : (batch + 1) * tokens], dt[batch].reshape(cols, tokens), 1, 1
-        )
-        value = term if value is None else value + term
-    low = value.astype(BF16)
-    for order in range(4):
-        target = (keep, send)[order // 2]
-        for sub in range(count):
-            start = order * rows + sub * thin
-            target[order % 2, sub] = low[start : start + thin, :]
+    for stage in range(stages):
+        grads = refs[stage]
+        dt = dts[stage]
+        for slot in range(count):
+            batch, head = slot // hps, slot % hps
+            c = cosine[batch]
+            s = sine[batch]
+            for part in range(2):
+                top = grads[slot, part * size : part * size + half, :].astype(F32)
+                low = grads[slot, part * size + half : (part + 1) * size, :].astype(F32)
+                dt[batch, part, head, 0:half, :] = (top * c + low * s).astype(BF16)
+                dt[batch, part, head, half:size, :] = (low * c - top * s).astype(BF16)
+            dt[batch, 2, head] = grads[slot, 2 * size :, :]
+        value = None
+        for batch in range(batches):
+            term = mm(
+                left[:, batch * tokens : (batch + 1) * tokens],
+                dt[batch].reshape(cols, tokens),
+                1,
+                1,
+            )
+            value = term if value is None else value + term
+        low = value.astype(BF16)
+        for order in range(4):
+            if natural:
+                target = (keep, send)[order // 2]
+                for sub in range(count):
+                    start = order * rows + sub * thin
+                    target[order % 2, sub] = low[start : start + thin, :]
+            else:
+                put_pieces(
+                    scalars[0],
+                    low[order * rows : (order + 1) * rows, :],
+                    (keep, send),
+                    order,
+                    count,
+                    stage * thin,
+                )
 
 
 def input_grad_kernel(stages, windows, scalars, x, norms, dmid, *refs):
@@ -857,22 +887,33 @@
     norm_grads[1:2, :] = bias_sum
 
 
-def place_split_kernel(moves, scalars, near, far, *outs):
-    bit = lax.rem(scalars[0], jnp.int32(2))
+def turned(index, count):
+    result = 0
+    while count > 1:
+        result = 2 * result + index % 2
+        index //= 2
+        count //= 2
+    return result
+
+
+def place_kernel(moves, scalars, near, far, *outs):
+    count = near.shape[0]
     for side, source in enumerate((near, far)):
-        for sub in range(source.shape[0]):
-            slot = 2 * sub + lax.bitwise_xor(bit, jnp.int32(side))
-            for out, first, rows, to, wide in moves:
-                outs[out][slot, :, to : to + wide] = source[sub, first : first + rows, :].astype(F32)
-
-
-def place_in_kernel(width, wide, *refs):
-    *pieces, out = refs
-    for s, piece in enumerate(pieces):
-        for sub in range(piece.shape[0]):
-            for part in range(3):
-                to = part * width + s * wide
-                out[sub, :, to : to + wide] = piece[sub, :, part * wide : (part + 1) * wide].astype(F32)
+        for sub in range(count):
+            slot = lax.bitwise_xor(scalars[0], jnp.int32(2 * turned(sub, count) + side))
+            for out, first, rows, begin, wide, to in moves:
+                outs[out][slot, :, to : to + wide] = source[
+                    sub, first : first + rows, begin : begin + wide
+                ].astype(F32)
+
+
+def place_in_kernel(moves, width, wide, thin, scalars, near, far, last, out):
+    place_kernel(moves, scalars, near, far, out)
+    final = len(moves) // 3
+    for sub in range(last.shape[0]):
+        for part in range(3):
+            to = part * width + final * wide
+            out[sub, :, to : to + wide] = last[sub, :, part * wide : (part + 1) * wide].astype(F32)
 
 
 def exchange(value, axis, bit):
@@ -896,34 +937,45 @@
     return swapped(jnp.broadcast_to(own[None], (count, *own.shape)), groups)
 
 
+def total(terms):
+    value = terms[0].astype(F32)
+    for term in terms[1:]:
+        value = value + term.astype(F32)
+    return value.astype(BF16)
+
+
+def reduce_blocks(keep, send, order):
+    count = lax.axis_size("ctx")
+    labels = ["x", 1]
+    bit = count // 2
+    while bit > 1:
+        labels.append(bit)
+        bit //= 2
+    dims = (2,) * len(labels) + keep.shape[3:]
+    terms = [keep.reshape(dims), exchange(send, "fsdp", 1).reshape(dims)]
+    sent = []
+    for label in order:
+        axis = labels.index(label)
+        sent.append(total([lax.index_in_dim(t, 1, axis, keepdims=False) for t in terms]))
+        got = exchange(sent[-1], *(("fsdp", 2) if label == "x" else ("ctx", label)))
+        terms = [lax.index_in_dim(t, 0, axis, keepdims=False) for t in terms] + [got]
+        labels.pop(axis)
+    return total(terms), sent
+
+
+def gather_blocks(own):
+    held = own[None]
+    bit = lax.axis_size("ctx") // 2
+    while bit > 1:
+        held = jnp.concatenate([held, exchange(held, "ctx", bit)])
+        bit //= 2
+    return held, exchange(held, "ctx", 1)
+
+
 def halved(keep, send):
     got = exchange(send, "fsdp", 1)
     passed = added(keep[1], got[1])
-    own = added(keep[0], got[0])
-    return added(own, exchange(passed, "fsdp", 2))
-
-
-def other_bits():
-    count = lax.axis_size("ctx")
-    return [list(range(first, count, 2)) for first in range(2)]
-
-
-def sum_far(own):
-    groups = other_bits()
-    part = summed(swapped(own, groups))
-    near = spread(part, lax.axis_size("ctx") // 2, groups)
-    return part, near, exchange(near, "ctx", 1)
-
-
-def chip_first(keep, send):
-    own = halved(keep, send)
-    return own, added(own[0], exchange(own[1], "ctx", 1))
-
-
-def chip_last(keep, send):
-    both = added(keep, exchange(send, "fsdp", 1))
-    both = added(both[:, 0], exchange(both[:, 1], "ctx", 1))
-    return both, added(both[0], exchange(both[1], "fsdp", 2))
+    return total([keep[0], got[0], exchange(passed, "fsdp", 2)])
 
 
 def reduce_whole(keep, send):
@@ -988,7 +1040,7 @@
         for s in range(stages)
     ]
     first_in = gathered(jnp.concatenate([chunks[0], jnp.pad(norm_rows, ((0, 0), (0, cols - width)))]))
-    rest_in = gathered(jnp.concatenate(chunks[1:]))
+    rest_in = gathered(after(jnp.concatenate(chunks[1:]), first_in[1]))
     groups = inner // width
     up_rows = jnp.moveaxis(up_proj.reshape(share, groups, width), 1, 0).reshape(-1, width)
     packed = jnp.concatenate([up_rows, down_proj, output_proj])
@@ -1017,8 +1069,9 @@
 
     pair_shape = shape_of((count, 3 * size, tokens), BF16)
     x = after(x, mix_early)
-    weights = gathered(after(packed, rest_in[3]))
-    held = []
+    packed = after(packed, rest_in[1])
+    weights = [packed, exchange(packed, "fsdp", 2), exchange(packed, "fsdp", 1)]
+    made = []
     n1t = norms = None
     windows = [(0, share)] + [(share * s, share) for s in range(stages - 1)]
     for s in range(stages):
@@ -1039,15 +1092,18 @@
         )
         if first:
             n1t, norms = result[1:]
-        held.append(swapped(result[0]))
+        made.append(result[0])
 
     tiles = count * (count + 1) // 2
     one = tokens * tokens * size * 2
     streams_in = count // 2
     head_shape = shape_of((count, size, tokens), BF16)
+    held = []
     attended = []
     saved = []
     for s in range(stages):
+        while len(held) < min(s + 2, stages):
+            held.append(swapped(after(made[len(held)], *([saved[-1][1]] if saved else []))))
         result = run_kernel(
             functools.partial(attend_kernel, count, scale),
             "attend",
@@ -1065,13 +1121,14 @@
             4 * 2 * one * tiles,
         )
         saved.append(result[1:])
-        attended.append(swapped(result[0]))
-
+        attended.append(result[0])
+
+    weights.append(exchange(after(weights[1], saved[-2][1]), "fsdp", 1))
     result = run_kernel(
         functools.partial(mlp_kernel, count, stages, hps, batches),
         "mlp",
-        [scalars, mixing, x, grad, norms] + attended + weights,
-        [SMEM, SMEM, VMEM, VMEM, VMEM] + [VMEM] * stages + [ANY] * 4,
+        [scalars, mixing, x, grad, norms, swapped(jnp.concatenate(attended, axis=1))] + weights,
+        [SMEM, SMEM, VMEM, VMEM, VMEM, VMEM] + [ANY] * 4,
         [
             shape_of((rows, inner), BF16),
             shape_of((rows, inner), BF16),
@@ -1081,8 +1138,8 @@
             shape_of((rows, width), BF16),
             shape_of((batches, heads, size, tokens), BF16),
             shape_of((8, width), F32),
-        ]
-        + [head_shape] * stages,
+            shape_of((count, stages * size, tokens), BF16),
+        ],
         [
             pltpu.VMEM((width, width), BF16),
             pltpu.VMEM((width, inner), BF16),
@@ -1094,43 +1151,59 @@
         6 * rows * width * inner,
     )
     hidden, dhidden, n2, mid, dmid, dmid_low, ot, norm2_grads = result[:8]
-    sent_grads = [swapped(value) for value in result[8:]]
+    head_grads = swapped(result[8])
 
     sub = inner // 4 // count
     thin = share // count
-    down_sums = run_kernel(
-        functools.partial(down_grad_kernel, count),
-        "down_grad",
-        [scalars, mixing, hidden, grad],
-        [SMEM, SMEM, VMEM, VMEM],
-        [shape_of((2, 2, count // 2, sub, width), BF16)] * 2,
-        [],
-        2 * rows * width * inner,
-    )
-    up_sums = run_kernel(
-        functools.partial(up_out_grad_kernel, count),
-        "up_out_grad",
-        [scalars, n2, dhidden, ot, dmid_low],
-        [SMEM] + [VMEM] * 4,
-        [shape_of((2, 2, count // 2, thin * (groups + 1), width), BF16)] * 2,
-        [pltpu.VMEM((width, rows), BF16), pltpu.VMEM((width, rows), BF16)],
-        2 * rows * width * (inner + width),
-    )
-    down_chip, down_own = chip_first(*down_sums)
-    up_both, up_own = chip_last(*up_sums)
-    down_part, *down_parts = sum_far(down_own)
-    up_part, *up_parts = sum_far(up_own)
-    gates = [(down_sums[0], up_sums[0]), (down_chip, up_both), (down_own, up_own)]
+    result = run_kernel(
+        functools.partial(grads_kernel, count, (groups * share, inner // 4)),
+        "grads",
+        [scalars, mixing, hidden, mid, prev, grad] + weights + [n2, dhidden, ot, dmid_low],
+        [SMEM, SMEM] + [VMEM] * 12,
+        [shape_of((2, 2, count // 2, sub, width), BF16)] * 2
+        + [shape_of((2, 2, count // 2, thin * (groups + 1), width), BF16)] * 2
+        + [shape_of((rows, width), BF16), shape_of((8, width), F32)],
+        [
+            pltpu.VMEM((rows, width), F32),
+            pltpu.VMEM((width, rows), BF16),
+            pltpu.VMEM((width, rows), BF16),
+        ],
+        2 * rows * width * (3 * inner + width),
+    )
+    down_sums, up_sums, (next_input, mix_last) = result[:2], result[2:4], result[4:]
+
+    def in_grads(arrived, natural):
+        few = len(arrived)
+        lead = (2, count, thin) if natural else (2, 2, count // 2, few * thin)
+        result = run_kernel(
+            functools.partial(in_grad_kernel, count, hps, natural),
+            "in_grad",
+            [scalars, cosine, sine, n1t] + arrived,
+            [SMEM] + [VMEM] * (3 + few),
+            [shape_of((batches, 3, hps, size, tokens), BF16)] * few
+            + [shape_of((*lead, cols), BF16)] * 2,
+            [pltpu.VMEM((width, rows), BF16)],
+            2 * few * rows * width * cols,
+        )
+        return list(result[:few]), result[few:]
+
+    far_bits = [1 << k for k in range(1, count.bit_length() - 1)]
+    down_own, down_sent = reduce_blocks(*down_sums, ["x", 1] + far_bits)
+    up_own, up_sent = reduce_blocks(*up_sums, [1, "x"] + far_bits)
+    down_parts = gather_blocks(down_own)
+    up_parts = gather_blocks(up_own)
 
     dts = []
-    in_parts = []
+    back = [mix_last]
+    moved = []
+    ready = {0: (down_sent[0], up_sent[0]), stages - 1: ()}
     for s in range(stages):
-        turn = gates[s] if s < len(gates) else gates[-1]
-        turn = turn + ((back,) if s else ())
-        (back,) = run_kernel(
-            functools.partial(attend_back_kernel, count, scale),
+        if s == stages - 1:
+            ready[s] += (moved[0],)
+        (value,) = run_kernel(
+            functools.partial(attend_back_kernel, count, scale, s),
             "attend_back",
-            [ids, after(held[s], *turn), sent_grads[s]] + list(saved[s]),
+            [ids, after(held[s], back[-1], *ready.get(s, ())), head_grads] + list(saved[s]),
             [SMEM] + [VMEM] * 4,
             [pair_shape],
             [
@@ -1149,28 +1222,14 @@
             + [pltpu.VMEM((count, tokens, size), F32)] * (2 * streams_in),
             4 * 5 * one * tiles,
         )
-        dt, keep, send = run_kernel(
-            functools.partial(in_grad_kernel, count, hps),
-            "in_grad",
-            [scalars, cosine, sine, n1t, swapped(back)],
-            [SMEM] + [VMEM] * 4,
-            [shape_of((batches, 3, hps, size, tokens), BF16)]
-            + [shape_of((2, count, thin, cols), BF16)] * 2,
-            [pltpu.VMEM((width, rows), BF16)],
-            2 * rows * width * cols,
-        )
-        dts.append(dt)
-        in_parts.append(reduce_whole(keep, send))
-
-    next_input, mix_last = run_kernel(
-        functools.partial(result_kernel, (groups * share, inner // 4)),
-        "result",
-        [scalars, mixing, hidden, mid, prev, after(grad, back)] + weights,
-        [SMEM, SMEM] + [VMEM] * 8,
-        [shape_of((rows, width), BF16), shape_of((8, width), F32)],
-        [pltpu.VMEM((rows, width), F32)],
-        2 * rows * width * inner,
-    )
+        back.append(value)
+        moved.append(swapped(value))
+    early_dts, early_sums = in_grads([after(moved[0], back[-1])] + moved[1:-1], False)
+    last_dts, last_sums = in_grads(moved[-1:], True)
+    dts = early_dts + last_dts
+    early_own, early_sent = reduce_blocks(*early_sums, ["x", 1] + far_bits)
+    early_parts = gather_blocks(early_own)
+    last_parts = reduce_whole(*last_sums)
 
     grad_input, norm1_grads = run_kernel(
         functools.partial(input_grad_kernel, stages, windows),
@@ -1187,12 +1246,13 @@
     )
     small = small + exchange(small, "fsdp", 1)
     small = small + exchange(small, "fsdp", 2)
-    small = jnp.sum(spread(small, count), axis=0)
+    for bit in [1] + far_bits:
+        small = small + exchange(small, "ctx", bit)
     norm_total = lax.dynamic_slice_in_dim(small[:4], place * share, share, 1)
     mix_total = jnp.sum(small[4:], axis=1)
 
     (grad_down,) = run_kernel(
-        functools.partial(place_split_kernel, ((0, 0, sub, 0, width),)),
+        functools.partial(place_kernel, ((0, 0, sub, 0, width, 0),)),
         "place_down",
         [scalars, *down_parts],
         [SMEM] + [VMEM] * 2,
@@ -1200,9 +1260,9 @@
         [],
         0,
     )
-    moves = tuple((0, g * thin, thin, g * width, width) for g in range(groups))
+    moves = tuple((0, g * thin, thin, 0, width, g * width) for g in range(groups))
     grad_up, grad_out = run_kernel(
-        functools.partial(place_split_kernel, moves + ((1, groups * thin, thin, 0, width),)),
+        functools.partial(place_kernel, moves + ((1, groups * thin, thin, 0, width, 0),)),
         "place_up",
         [scalars, *up_parts],
         [SMEM] + [VMEM] * 2,
@@ -1210,11 +1270,17 @@
         [],
         0,
     )
+    wide = hps * size
+    moves = tuple(
+        (0, g * thin, thin, part * wide, wide, part * width + g * wide)
+        for g in range(stages - 1)
+        for part in range(3)
+    )
     (grad_in,) = run_kernel(
-        functools.partial(place_in_kernel, width, hps * size),
+        functools.partial(place_in_kernel, moves, width, wide, thin),
         "place_in",
-        in_parts,
-        [VMEM] * stages,
+        [scalars, *early_parts, last_parts],
+        [SMEM] + [VMEM] * 3,
         [shape_of((count, thin, 3 * width), F32)],
         [],
         0,

time: 596 us -> 455 us (0.76)
  waiting for transfers between devices: 213 us -> 149 us
  blocking collectives: 52.1 us -> 0 us
  starting transfers between devices: 106 us -> 75.1 us
  local copies, waits for them, and re-layouts: 21.3 us -> 29.9 us
  Pallas kernels: 164 us -> 157 us
    all_to_all x20 -> x10, waiting for transfers between devices: 126 us -> 50.2 us  [swapped(): return lax.all_to_all(value, 'ctx', 0, 0, axis_index_groups=groups)]
    all_to_all x3 -> x0, blocking collectives: 52.1 us -> none  [swapped(): return lax.all_to_all(value, 'ctx', 0, 0, axis_index_groups=groups)]
    all_to_all x20 -> x10, starting transfers between devices: 86.7 us -> 43.8 us  [swapped(): return lax.all_to_all(value, 'ctx', 0, 0, axis_index_groups=groups)]
    convert_element_type x12 -> x1, other arithmetic: 23.6 us -> 0.07 us  [added(): return (left.astype(F32) + right.astype(F32)).astype(BF16)]
    convert_element_type x0 -> x10, other arithmetic: none -> 16.9 us  [total(): return value.astype(BF16)]
    ppermute x25 -> x40, starting transfers between devices: 19.5 us -> 31.3 us  [exchange(): return lax.ppermute(value, axis, [(i, i ^ bit) for i in range(size)])]
    ppermute x25 -> x40, waiting for transfers between devices: 87.4 us -> 98.7 us  [exchange(): return lax.ppermute(value, axis, [(i, i ^ bit) for i in range(size)])]
    pallas_call x21 -> x18, Pallas kernels: 164 us -> 157 us  [run_kernel(): pl.pallas_call(kernel, name=name, in_specs=[spec(s) for s in spaces], out...]
  transfers between devices with their start and end apart: 45 -> 50, of which waited for: 22 -> 26; matrix products, arithmetic and copies ran while one was open for 7% -> 12% of each run, Pallas kernels for 24% -> 26%
where the time goes in v3:
time: 455 us; the launch traced here: 446 us
  Pallas kernels  157 us (35%)
  waiting for transfers between devices  149 us (33%)
  starting transfers between devices  75.1 us (17%)
  other arithmetic  33.5 us (7%)
  local copies, waits for them, and re-layouts  29.9 us (7%)
    pallas_call x18, Pallas kernels, run_kernel(): pl.pallas_call(kernel, name=name, in_specs=[spec(s) for s in spaces], out...  157 us
    ppermute x40, waiting for transfers between devices, exchange(): return lax.ppermute(value, axis, [(i, i ^ bit) for i in range(size)])  98.7 us
    all_to_all x10, waiting for transfers between devices, swapped(): return lax.all_to_all(value, 'ctx', 0, 0, axis_index_groups=groups)  50.2 us
    all_to_all x10, starting transfers between devices, swapped(): return lax.all_to_all(value, 'ctx', 0, 0, axis_index_groups=groups)  43.8 us
    ppermute x40, starting transfers between devices, exchange(): return lax.ppermute(value, axis, [(i, i ^ bit) for i in range(size)])  31.3 us
    convert_element_type x10, other arithmetic, total(): return value.astype(BF16)  16.9 us
  transfers between devices with their start and end apart: 50, of which 26 were waited for; matrix products, arithmetic and copies ran while one was open for 12% of the time, Pallas kernels for 26%

profile of v3, /device:TPU:0, one launch (start us, length us, event | category | flops | bytes accessed | tf_op | source)
XLA Modules:
  0.0 445.7 jit_solution(16641310384834604290)
XLA Ops:
  6.3 5.3 %early.1 = (bf16[4,512,768]{2,1,0:T(8,128)(2,1)}, f32[512,768]{1,0:T(8,128)}, f32[8,768]{1,0:T(8,128)}) custom-call(f32[5]{0:T(128)} %mix.5, bf16[4,512,768]{2,1,0:T(8,128)(2,1)} %bitcast.150, bf16[512,768]{1,0:T(8,128)(2,1)} %bitcast.173), custom_call_target="tpu_custom_call" | custom-call | flops 9437184 | bytes 8675348 | tf_op jit(solution)/shard_map/early/pallas_call | solution.py:408
  18.4 4.0 qkv.3
  22.4 5.8 %all-to-all-start = ((bf16[8,192,256]{2,1,0:T(8,128)(2,1)}), bf16[8,192,256]{2,1,0:T(8,128)(2,1)S(1)}, u32[]{:S(2)}, u32[]{:S(2)}) async-start(bf16[8,192,256]{2,1,0:T(8,128)(2,1)} %get-tuple-element.67), calls=%async_computation | async-start | bytes 1572864 | tf_op jit(solution)/shard_map/all_to_all | solution.py:929
  40.6 8.1 %all-to-all-done.ins = bf16[8,192,256]{2,1,0:T(8,128)(2,1)S(1)} async-done(((bf16[8,192,256]{2,1,0:T(8,128)(2,1)}), bf16[8,192,256]{2,1,0:T(8,128)(2,1)S(1)}, u32[]{:S(2)}, u32[]{:S(2)}) %all-to-all-start) | async-done | bytes 786464 | tf_op jit(solution)/shard_map/all_to_all | solution.py:929
  56.6 9.0 %attend.3 = (bf16[8,64,256]{2,1,0:T(8,128)(2,1)}, f32[8,64,256]{2,1,0:T(8,128)}, f32[8,1,256]{2,1,0:T(1,128)}) custom-call(s32[8]{0:T(128)} %fusion.23.ids, bf16[8,192,256]{2,1,0:T(8,128)(2,1)} %copy-done.21), custom_call_target="tpu_custom_call" | custom-call | flops 2415919104 | bytes 1581088 | tf_op jit(solution)/shard_map/attend/pallas_call | solution.py:408
  65.6 7.2 %all-to-all-done.1.ins = bf16[8,192,256]{2,1,0:T(8,128)(2,1)S(1)} async-done(((bf16[8,192,256]{2,1,0:T(8,128)(2,1)}), bf16[8,192,256]{2,1,0:T(8,128)(2,1)S(1)}, u32[]{:S(2)}, u32[]{:S(2)}) %all-to-all-start.1) | async-done | bytes 786464 | tf_op jit(solution)/shard_map/all_to_all | solution.py:929
  76.4 9.0 %attend.4 = (bf16[8,64,256]{2,1,0:T(8,128)(2,1)}, f32[8,64,256]{2,1,0:T(8,128)}, f32[8,1,256]{2,1,0:T(1,128)}) custom-call(s32[8]{0:T(128)} %fusion.23.ids, bf16[8,192,256]{2,1,0:T(8,128)(2,1)} %copy-done.22), custom_call_target="tpu_custom_call" | custom-call | flops 2415919104 | bytes 1581088 | tf_op jit(solution)/shard_map/attend/pallas_call | solution.py:408
  85.4 5.5 %collective-permute-done.6.refs_2_.w1 = bf16[1728,768]{1,0:T(8,128)(2,1)} collective-permute-done((bf16[1728,768]{1,0:T(8,128)(2,1)}, bf16[1728,768]{1,0:T(8,128)(2,1)}, u32[]{:S(2)}, u32[]{:S(2)}) %collective-permute-start.6) | collective-permute-done | bytes 2654240 | tf_op jit(solution)/shard_map/ppermute | solution.py:921
  90.9 5.7 %all-to-all-done.2.ins = bf16[8,192,256]{2,1,0:T(8,128)(2,1)S(1)} async-done(((bf16[8,192,256]{2,1,0:T(8,128)(2,1)}), bf16[8,192,256]{2,1,0:T(8,128)(2,1)S(1)}, u32[]{:S(2)}, u32[]{:S(2)}) %all-to-all-start.2) | async-done | bytes 786464 | tf_op jit(solution)/shard_map/all_to_all | solution.py:929
  97.6 9.0 %attend.5 = (bf16[8,64,256]{2,1,0:T(8,128)(2,1)}, f32[8,64,256]{2,1,0:T(8,128)}, f32[8,1,256]{2,1,0:T(1,128)}) custom-call(s32[8]{0:T(128)} %fusion.23.ids, bf16[8,192,256]{2,1,0:T(8,128)(2,1)} %copy-done.23), custom_call_target="tpu_custom_call" | custom-call | flops 2415919104 | bytes 1581088 | tf_op jit(solution)/shard_map/attend/pallas_call | solution.py:408
  112.2 20.3 %all-to-all-done.3.refs_0_ = bf16[8,192,256]{2,1,0:T(8,128)(2,1)S(1)} async-done(((bf16[8,192,256]{2,1,0:T(8,128)(2,1)}), bf16[8,192,256]{2,1,0:T(8,128)(2,1)S(1)}, u32[]{:S(2)}, u32[]{:S(2)}) %all-to-all-start.3) | async-done | bytes 786464 | tf_op jit(solution)/shard_map/all_to_all | solution.py:929
  133.4 19.1 %mlp.1 = (bf16[512,3072]{1,0:T(8,128)(2,1)}, bf16[512,3072]{1,0:T(8,128)(2,1)}, bf16[512,768]{1,0:T(8,128)(2,1)}, f32[512,768]{1,0:T(8,128)}, f32[512,768]{1,0:T...) custom-call(s32[2]{0:T(128)} %pad_add_fusion.refs_0_.scalars, ...), custom_call_target="tpu_custom_call" | custom-call | flops 7247757312 | bytes 25608220 | tf_op jit(solution)/shard_map/mlp/pallas_call | solution.py:408
  152.5 18.6 %grads.1 = (bf16[2,2,4,96,768]{4,3,2,1,0:T(8,128)(2,1)}, bf16[2,2,4,96,768]{4,3,2,1,0:T(8,128)(2,1)}, bf16[2,2,4,120,768]{4,3,2,1,0:T(8,128)(2,1)}, bf16[2,2,4,1...) custom-call(s32[2]{0:T(128)} %pad_add_fusion.refs_0_.scalars, f32[5]{0:T(128)} %mix.5, ...), custom_call_target="tpu_custom_call" | custom-call | flops 7851737088 | bytes 34627612 | tf_op jit(solution)/shard_map/grads/pallas_call | solution.py:408
  171.6 4.4 all-to-all-start.4
  176.0 4.0 collective-permute-done.9
  187.9 8.8 %all-to-all-done.4.grads = bf16[8,192,256]{2,1,0:T(8,128)(2,1)} async-done(((bf16[8,192,256]{2,1,0:T(8,128)(2,1)}), bf16[8,192,256]{2,1,0:T(8,128)(2,1)}, u32[]{:S(2)}, u32[]{:S(2)}) %all-to-all-start.4) | async-done | bytes 786464 | tf_op jit(solution)/shard_map/all_to_all | solution.py:929
  196.7 16.7 %attend_back.3 = bf16[8,192,256]{2,1,0:T(8,128)(2,1)} custom-call(s32[8]{0:T(128)} %fusion.23.ids, bf16[8,192,256]{2,1,0:T(8,128)(2,1)} %copy-done.21, bf16[8,192,256]{2,1,0:T(8,128)(2,1)} %all-to-all-done.4.grads, f32[8,64,256]{2,1,0:T(8,128)} %get-tuple-element.96.ot, f32[8,1,256]{2,1,0:T(1,128)} %get-tuple-element.69.lse), custom_call_target="tpu_custom_call" | custom-call | flops 6039797760 | bytes 2891808 | tf_op jit(solution)/shard_map/attend_back/pallas_call | solution.py:408
  213.4 4.2 all-to-all-start.5
  226.1 16.7 %attend_back.4 = bf16[8,192,256]{2,1,0:T(8,128)(2,1)} custom-call(s32[8]{0:T(128)} %fusion.23.ids, bf16[8,192,256]{2,1,0:T(8,128)(2,1)} %copy-done.22, bf16[8,192,256]{2,1,0:T(8,128)(2,1)} %all-to-all-done.4.grads, f32[8,64,256]{2,1,0:T(8,128)} %get-tuple-element.98.ot, f32[8,1,256]{2,1,0:T(1,128)} %get-tuple-element.74.lse), custom_call_target="tpu_custom_call" | custom-call | flops 6039797760 | bytes 2891808 | tf_op jit(solution)/shard_map/attend_back/pallas_call | solution.py:408
  242.8 6.2 %all-to-all-start.6 = ((bf16[8,192,256]{2,1,0:T(8,128)(2,1)}), bf16[8,192,256]{2,1,0:T(8,128)(2,1)}, u32[]{:S(2)}, u32[]{:S(2)}) async-start(bf16[8,192,256]{2,1,0:T(8,128)(2,1)} %attend_back.4), calls=%async_computation.6 | async-start | bytes 1572864 | tf_op jit(solution)/shard_map/all_to_all | solution.py:929
  250.2 29.8 %collective-permute-done.29 = bf16[2,2,96,768]{3,2,1,0:T(8,128)(2,1)} collective-permute-done((bf16[2,2,96,768]{3,2,1,0:T(8,128)(2,1)}, bf16[2,2,96,768]{3,2,1,0:T(8,128)(2,1)}, u32[]{:S(2)}, u32[]{:S(2)}) %collective-permute-start.29) | collective-permute-done | bytes 589856 | tf_op jit(solution)/shard_map/ppermute | solution.py:921
  293.3 16.7 %attend_back.5 = bf16[8,192,256]{2,1,0:T(8,128)(2,1)} custom-call(s32[8]{0:T(128)} %fusion.23.ids, bf16[8,192,256]{2,1,0:T(8,128)(2,1)} %copy-done.23, bf16[8,192,256]{2,1,0:T(8,128)(2,1)} %all-to-all-done.4.grads, f32[8,64,256]{2,1,0:T(8,128)} %get-tuple-element.100.ot, f32[8,1,256]{2,1,0:T(1,128)} %get-tuple-element.101.lse), custom_call_target="tpu_custom_call" | custom-call | flops 6039797760 | bytes 2891808 | tf_op jit(solution)/shard_map/attend_back/pallas_call | solution.py:408
  310.0 5.0 %in_grad.2 = (bf16[2,3,4,64,256]{4,3,2,1,0:T(8,128)(2,1)}, bf16[2,3,4,64,256]{4,3,2,1,0:T(8,128)(2,1)}, bf16[2,2,4,48,768]{4,3,2,1,0:T(8,128)(2,1)}, bf16[2,2,4,48,768]{4,3,2,1,0:T(8,128)(2,1)}) custom-call(s32[2]{0:T(128)} %pad_add_fusion.refs_0_.scalars, f32[2,32,256]{2,1,0:T(8,128)} %get-tuple-element.132.refs_2_.cosine, ...), custom_call_target="tpu_custom_call" | custom-call | flops 1207959552 | bytes 6422536 | tf_op jit(solution)/shard_map/in_grad/pallas_call | solution.py:408
  319.8 6.9 %collective-permute-done.32 = bf16[1,96,768]{2,1,0:T(8,128)(2,1)S(1)} collective-permute-done((bf16[1,96,768]{2,1,0:T(8,128)(2,1)S(1)}, bf16[1,96,768]{2,1,0:T(8,128)(2,1)S(1)}, u32[]{:S(2)}, u32[]{:S(2)}) %collective-permute-start.32) | collective-permute-done | bytes 147488 | tf_op jit(solution)/shard_map/ppermute | solution.py:921
  327.7 4.3 all-to-all-start.7
  346.4 9.5 %collective-permute-done.23 = bf16[2,120,768]{2,1,0:T(8,128)(2,1)S(1)} collective-permute-done((bf16[2,120,768]{2,1,0:T(8,128)(2,1)S(1)}, bf16[2,120,768]{2,1,0:T(8,128)(2,1)S(1)}, u32[]{:S(2)}, u32[]{:S(2)}) %collective-permute-start.23) | collective-permute-done | bytes 368672 | tf_op jit(solution)/shard_map/ppermute | solution.py:921
  363.1 8.3 %input_grad.1 = (bf16[512,768]{1,0:T(8,128)(2,1)}, f32[8,768]{1,0:T(8,128)}) custom-call(s32[2]{0:T(128)} %pad_add_fusion.refs_0_.scalars, bf16[512,768]{1,0:T(8,128)(2,1)} %bitcast.172, f32[8,768]{1,0:T(8,128)} %get-tuple-element.66.norms, f32[512,768]{1,0:T(8,128)} %get-tuple-element.88.dmid, bf16[2,3,4,64,256]{4,3,2,1,0:T(8,128)(2,1)} %get-tuple-element.103.refs_0_, ...), custom_call_target="tpu_custom_call" | custom-call | flops 1811939328 | bytes 11550728 | tf_op jit(solution)/shard_map/input_grad/pallas_call | solution.py:408
  377.4 5.3 %collective-permute-done.13 = bf16[2,2,48,768]{3,2,1,0:T(8,128)(2,1)S(1)} collective-permute-done((bf16[2,2,48,768]{3,2,1,0:T(8,128)(2,1)S(1)}, bf16[2,2,48,768]{3,2,1,0:T(8,128)(2,1)S(1)}, u32[]{:S(2)}, u32[]{:S(2)}) %collective-permute-start.13) | collective-permute-done | bytes 294944 | tf_op jit(solution)/shard_map/ppermute | solution.py:921
  403.0 5.6 %collective-permute-done.16 = bf16[1,48,768]{2,1,0:T(8,128)(2,1)S(1)} collective-permute-done((bf16[1,48,768]{2,1,0:T(8,128)(2,1)S(1)}, bf16[1,48,768]{2,1,0:T(8,128)(2,1)S(1)}, u32[]{:S(2)}, u32[]{:S(2)}) %collective-permute-start.16) | collective-permute-done | bytes 73760 | tf_op jit(solution)/shard_map/ppermute | solution.py:921
  409.5 4.4 all-to-all-start.9
  421.1 5.4 %collective-permute-done.37 = f32[9,768]{1,0:T(8,128)S(1)} collective-permute-done((f32[9,768]{1,0:T(8,128)S(1)}, f32[9,768]{1,0:T(8,128)S(1)}, u32[]{:S(2)}, u32[]{:S(2)}) %collective-permute-start.37) | collective-permute-done | bytes 27680 | tf_op jit(solution)/shard_map/ppermute | solution.py:921
  426.6 4.2 collective-permute-done.38
  (250 shorter events, 150.6 us)
Async XLA Ops:
  3.0 14.5 %collective-permute-start.1 = (bf16[208,768]{1,0:T(8,128)(2,1)S(1)}, bf16[208,768]{1,0:T(8,128)(2,1)S(1)}, u32[]{:S(2)}, u32[]{:S(2)}) collective-permute-start(bf16[208,768]{1,0:T(8,128)(2,1)S(1)} %pad_maximum_fusion.5.refs_4_.refs_3_), channel_id=1, source_target_pairs={{0,1},{1,0},{2,3},{3,2},{4,5},{5,4},{6,7},{7,6},{8,9},{9,8},{10,11... | collective-permute-start | bytes 958472 | tf_op jit(solution)/shard_map/ppermute | solution.py:921
  15.8 15.7 %collective-permute-start.3 = (bf16[384,768]{1,0:T(8,128)(2,1)S(1)}, bf16[384,768]{1,0:T(8,128)(2,1)S(1)}, u32[]{:S(2)}, u32[]{:S(2)}) collective-permute-start(bf16[384,768]{1,0:T(8,128)(2,1)S(1)} %maximum_maximum_fusion.refs_4_.refs_7_.refs_11_), channel_id=1, source_target_pairs={{0,2},{1,3},{2,0},{3,1},{4,6},{5,7},{6,4},{7,5},{8,10},{9,11},{10,... | collective-permute-start | bytes 1769480 | tf_op jit(solution)/shard_map/ppermute | solution.py:921
  22.4 26.4 %all-to-all-start = ((bf16[8,192,256]{2,1,0:T(8,128)(2,1)}), bf16[8,192,256]{2,1,0:T(8,128)(2,1)S(1)}, u32[]{:S(2)}, u32[]{:S(2)}) async-start(bf16[8,192,256]{2,1,0:T(8,128)(2,1)} %get-tuple-element.67), calls=%async_computation | async-start | bytes 1572864 | tf_op jit(solution)/shard_map/all_to_all | solution.py:929
  31.5 59.4 %collective-permute-start.6 = (bf16[1728,768]{1,0:T(8,128)(2,1)}, bf16[1728,768]{1,0:T(8,128)(2,1)}, u32[]{:S(2)}, u32[]{:S(2)}) collective-permute-start(bf16[1728,768]{1,0:T(8,128)(2,1)} %pad_maximum_fusion.refs_1_.w0), channel_id=1, source_target_pairs={{0,2},{1,3},{2,0},{3,1},{4,6},{5,7},{6,4},{7,5},{8,10},{9,11},{10,... | collective-permute-start | bytes 7962632 | tf_op jit(solution)/shard_map/ppermute | solution.py:921
  48.7 24.0 %all-to-all-start.1 = ((bf16[8,192,256]{2,1,0:T(8,128)(2,1)}), bf16[8,192,256]{2,1,0:T(8,128)(2,1)S(1)}, u32[]{:S(2)}, u32[]{:S(2)}) async-start(bf16[8,192,256]{2,1,0:T(8,128)(2,1)} %qkv.4), calls=%async_computation.1 | async-start | bytes 1572864 | tf_op jit(solution)/shard_map/all_to_all | solution.py:929
  72.7 23.9 %all-to-all-start.2 = ((bf16[8,192,256]{2,1,0:T(8,128)(2,1)}), bf16[8,192,256]{2,1,0:T(8,128)(2,1)S(1)}, u32[]{:S(2)}, u32[]{:S(2)}) async-start(bf16[8,192,256]{2,1,0:T(8,128)(2,1)} %qkv.5), calls=%async_computation.2 | async-start | bytes 1572864 | tf_op jit(solution)/shard_map/all_to_all | solution.py:929
  76.3 35.9 %collective-permute-start.7 = (bf16[1728,768]{1,0:T(8,128)(2,1)}, bf16[1728,768]{1,0:T(8,128)(2,1)}, u32[]{:S(2)}, u32[]{:S(2)}) collective-permute-start(bf16[1728,768]{1,0:T(8,128)(2,1)} %pad_maximum_fusion.refs_1_.w0), channel_id=1, source_target_pairs={{0,1},{1,0},{2,3},{3,2},{4,5},{5,4},{6,7},{7,6},{8,9},{9,8},{10,11... | collective-permute-start | bytes 7962632 | tf_op jit(solution)/shard_map/ppermute | solution.py:921
  90.9 41.6 %collective-permute-start.8 = (bf16[1728,768]{1,0:T(8,128)(2,1)}, bf16[1728,768]{1,0:T(8,128)(2,1)}, u32[]{:S(2)}, u32[]{:S(2)}) collective-permute-start(bf16[1728,768]{1,0:T(8,128)(2,1)} %collective-permute-done.6.refs_2_.w1), channel_id=1, source_target_pairs={{0,1},{1,0},{2,3},{3,2},{4,5},{5,4},{6,7},{7,6},{8,9},{9,8},{10,11... | collective-permute-start | bytes 7962632 | tf_op jit(solution)/shard_map/ppermute | solution.py:921
  108.4 24.1 %all-to-all-start.3 = ((bf16[8,192,256]{2,1,0:T(8,128)(2,1)}), bf16[8,192,256]{2,1,0:T(8,128)(2,1)S(1)}, u32[]{:S(2)}, u32[]{:S(2)}) async-start(bf16[8,192,256]{2,1,0:T(8,128)(2,1)} %pad_maximum_fusion.1), calls=%async_computation.3 | async-start | bytes 1572864 | tf_op jit(solution)/shard_map/all_to_all | solution.py:929
  171.1 13.0 %collective-permute-start.10 = (bf16[2,2,4,120,768]{4,3,2,1,0:T(8,128)(2,1)}, bf16[2,2,4,120,768]{4,3,2,1,0:T(8,128)(2,1)}, u32[]{:S(2)}, u32[]{:S(2)}) collective-permute-start(bf16[2,2,4,120,768]{4,3,2,1,0:T(8,128)(2,1)} %get-tuple-element.93), channel_id=1, source_target_pairs={{0,1},{1,0},{2,3},{3,2},{4,5},{5,4},{6,7},{7,6},{8,9},{9,8},{10,11... | collective-permute-start | bytes 8847368 | tf_op jit(solution)/shard_map/ppermute | solution.py:921
  171.6 25.1 %all-to-all-start.4 = ((bf16[8,192,256]{2,1,0:T(8,128)(2,1)}), bf16[8,192,256]{2,1,0:T(8,128)(2,1)}, u32[]{:S(2)}, u32[]{:S(2)}) async-start(bf16[8,192,256]{2,1,0:T(8,128)(2,1)} %get-tuple-element.95), calls=%async_computation.4 | async-start | bytes 1572864 | tf_op jit(solution)/shard_map/all_to_all | solution.py:929
  183.5 40.5 %collective-permute-start.28 = (bf16[2,2,2,96,768]{4,3,2,1,0:T(8,128)(2,1)}, bf16[2,2,2,96,768]{4,3,2,1,0:T(8,128)(2,1)}, u32[]{:S(2)}, u32[]{:S(2)}) collective-permute-start(bf16[2,2,2,96,768]{4,3,2,1,0:T(8,128)(2,1)} %bitcast.13), channel_id=1, source_target_pairs={{0,2},{1,3},{2,0},{3,1},{4,6},{5,7},{6,4},{7,5},{8,10},{9,11},{10,... | collective-permute-start | bytes 3538952 | tf_op jit(solution)/shard_map/ppermute | solution.py:921
  213.4 29.5 %all-to-all-start.5 = ((bf16[8,192,256]{2,1,0:T(8,128)(2,1)}), bf16[8,192,256]{2,1,0:T(8,128)(2,1)}, u32[]{:S(2)}, u32[]{:S(2)}) async-start(bf16[8,192,256]{2,1,0:T(8,128)(2,1)} %attend_back.3), calls=%async_computation.5 | async-start | bytes 1572864 | tf_op jit(solution)/shard_map/all_to_all | solution.py:929
  222.0 94.7 %collective-permute-start.21 = (bf16[2,2,2,120,768]{4,3,2,1,0:T(8,128)(2,1)}, bf16[2,2,2,120,768]{4,3,2,1,0:T(8,128)(2,1)}, u32[]{:S(2)}, u32[]{:S(2)}) collective-permute-start(bf16[2,2,2,120,768]{4,3,2,1,0:T(8,128)(2,1)} %fusion), channel_id=1, source_target_pairs={{0,4},{4,0},{8,12},{12,8},{16,20},{20,16},{24,28},{28,24},{1,5},{5... | collective-permute-start | bytes 4423688 | tf_op jit(solution)/shard_map/ppermute | solution.py:921
  226.0 54.0 %collective-permute-start.29 = (bf16[2,2,96,768]{3,2,1,0:T(8,128)(2,1)}, bf16[2,2,96,768]{3,2,1,0:T(8,128)(2,1)}, u32[]{:S(2)}, u32[]{:S(2)}) collective-permute-start(bf16[2,2,96,768]{3,2,1,0:T(8,128)(2,1)} %fusion.3), channel_id=1, source_target_pairs={{0,4},{4,0},{8,12},{12,8},{16,20},{20,16},{24,28},{28,24},{1,5},{5... | collective-permute-start | bytes 1769480 | tf_op jit(solution)/shard_map/ppermute | solution.py:921
  242.8 67.2 %all-to-all-start.6 = ((bf16[8,192,256]{2,1,0:T(8,128)(2,1)}), bf16[8,192,256]{2,1,0:T(8,128)(2,1)}, u32[]{:S(2)}, u32[]{:S(2)}) async-start(bf16[8,192,256]{2,1,0:T(8,128)(2,1)} %attend_back.4), calls=%async_computation.6 | async-start | bytes 1572864 | tf_op jit(solution)/shard_map/all_to_all | solution.py:929
  290.7 24.4 %collective-permute-start.31 = (bf16[96,768]{1,0:T(8,128)(2,1)}, bf16[96,768]{1,0:T(8,128)(2,1)}, u32[]{:S(2)}, u32[]{:S(2)}) collective-permute-start(bf16[96,768]{1,0:T(8,128)(2,1)} %fusion.12), channel_id=1, source_target_pairs={{0,16},{4,20},{8,24},{12,28},{16,0},{20,4},{24,8},{28,12},{1,17},{... | collective-permute-start | bytes 442376 | tf_op jit(solution)/shard_map/ppermute | solution.py:921
  315.0 26.0 %collective-permute-start.11 = (bf16[2,2,4,48,768]{4,3,2,1,0:T(8,128)(2,1)}, bf16[2,2,4,48,768]{4,3,2,1,0:T(8,128)(2,1)}, u32[]{:S(2)}, u32[]{:S(2)}) collective-permute-start(bf16[2,2,4,48,768]{4,3,2,1,0:T(8,128)(2,1)} %get-tuple-element.109), channel_id=1, source_target_pairs={{0,1},{1,0},{2,3},{3,2},{4,5},{5,4},{6,7},{7,6},{8,9},{9,8},{10,11... | collective-permute-start | bytes 3538952 | tf_op jit(solution)/shard_map/ppermute | solution.py:921
  319.2 19.0 %collective-permute-start.22 = (bf16[2,2,120,768]{3,2,1,0:T(8,128)(2,1)}, bf16[2,2,120,768]{3,2,1,0:T(8,128)(2,1)}, u32[]{:S(2)}, u32[]{:S(2)}) collective-permute-start(bf16[2,2,120,768]{3,2,1,0:T(8,128)(2,1)} %fusion.1), channel_id=1, source_target_pairs={{0,2},{1,3},{2,0},{3,1},{4,6},{5,7},{6,4},{7,5},{8,10},{9,11},{10,... | collective-permute-start | bytes 2211848 | tf_op jit(solution)/shard_map/ppermute | solution.py:921
  327.7 32.2 %all-to-all-start.7 = ((bf16[8,192,256]{2,1,0:T(8,128)(2,1)}), bf16[8,192,256]{2,1,0:T(8,128)(2,1)}, u32[]{:S(2)}, u32[]{:S(2)}) async-start(bf16[8,192,256]{2,1,0:T(8,128)(2,1)} %attend_back.5), calls=%async_computation.7 | async-start | bytes 1572864 | tf_op jit(solution)/shard_map/all_to_all | solution.py:929
  337.4 93.5 %collective-permute-start.34 = (bf16[4,96,768]{2,1,0:T(8,128)(2,1)S(1)}, bf16[4,96,768]{2,1,0:T(8,128)(2,1)}, u32[]{:S(2)}, u32[]{:S(2)}) collective-permute-start(bf16[4,96,768]{2,1,0:T(8,128)(2,1)S(1)} %pad_maximum_fusion.3.near), channel_id=1, source_target_pairs={{0,4},{4,0},{8,12},{12,8},{16,20},{20,16},{24,28},{28,24},{1,5},{5... | collective-permute-start | bytes 1769480 | tf_op jit(solution)/shard_map/ppermute | solution.py:921
  339.3 16.5 %collective-permute-start.23 = (bf16[2,120,768]{2,1,0:T(8,128)(2,1)S(1)}, bf16[2,120,768]{2,1,0:T(8,128)(2,1)S(1)}, u32[]{:S(2)}, u32[]{:S(2)}) collective-permute-start(bf16[2,120,768]{2,1,0:T(8,128)(2,1)S(1)} %fusion.6), channel_id=1, source_target_pairs={{0,8},{4,12},{8,0},{12,4},{16,24},{20,28},{24,16},{28,20},{1,9},{5... | collective-permute-start | bytes 1105928 | tf_op jit(solution)/shard_map/ppermute | solution.py:921
  343.1 29.0 %collective-permute-start.12 = (bf16[2,2,2,48,768]{4,3,2,1,0:T(8,128)(2,1)}, bf16[2,2,2,48,768]{4,3,2,1,0:T(8,128)(2,1)}, u32[]{:S(2)}, u32[]{:S(2)}) collective-permute-start(bf16[2,2,2,48,768]{4,3,2,1,0:T(8,128)(2,1)} %bitcast.21), channel_id=1, source_target_pairs={{0,2},{1,3},{2,0},{3,1},{4,6},{5,7},{6,4},{7,5},{8,10},{9,11},{10,... | collective-permute-start | bytes 1769480 | tf_op jit(solution)/shard_map/ppermute | solution.py:921
  358.4 16.4 %collective-permute-start.24 = (bf16[120,768]{1,0:T(8,128)(2,1)}, bf16[120,768]{1,0:T(8,128)(2,1)}, u32[]{:S(2)}, u32[]{:S(2)}) collective-permute-start(bf16[120,768]{1,0:T(8,128)(2,1)} %fusion.7), channel_id=1, source_target_pairs={{0,16},{4,20},{8,24},{12,28},{16,0},{20,4},{24,8},{28,12},{1,17},{... | collective-permute-start | bytes 552968 | tf_op jit(solution)/shard_map/ppermute | solution.py:921
  363.1 20.5 %collective-permute-start.19 = (bf16[2,8,24,768]{3,2,1,0:T(8,128)(2,1)}, bf16[2,8,24,768]{3,2,1,0:T(8,128)(2,1)S(1)}, u32[]{:S(2)}, u32[]{:S(2)}) collective-permute-start(bf16[2,8,24,768]{3,2,1,0:T(8,128)(2,1)} %get-tuple-element.111), channel_id=1, source_target_pairs={{0,1},{1,0},{2,3},{3,2},{4,5},{5,4},{6,7},{7,6},{8,9},{9,8},{10,11... | collective-permute-start | bytes 1769480 | tf_op jit(solution)/shard_map/ppermute | solution.py:921
  387.7 15.2 %collective-permute-start.26 = (bf16[2,120,768]{2,1,0:T(8,128)(2,1)S(1)}, bf16[2,120,768]{2,1,0:T(8,128)(2,1)S(1)}, u32[]{:S(2)}, u32[]{:S(2)}) collective-permute-start(bf16[2,120,768]{2,1,0:T(8,128)(2,1)S(1)} %pad_maximum_fusion.4), channel_id=1, source_target_pairs={{0,8},{4,12},{8,0},{12,4},{16,24},{20,28},{24,16},{28,20},{1,9},{5... | collective-permute-start | bytes 1105928 | tf_op jit(solution)/shard_map/ppermute | solution.py:921
  392.9 15.8 %all-to-all-start.8 = ((bf16[8,24,768]{2,1,0:T(8,128)(2,1)}), bf16[8,24,768]{2,1,0:T(8,128)(2,1)S(1)}, u32[]{:S(2)}, u32[]{:S(2)}) async-start(bf16[8,24,768]{2,1,0:T(8,128)(2,1)} %fusion.5), calls=%async_computation.8 | async-start | bytes 589824 | tf_op jit(solution)/shard_map/all_to_all | solution.py:929
  396.4 17.5 %collective-permute-start.35 = (f32[9,768]{1,0:T(8,128)S(1)}, f32[9,768]{1,0:T(8,128)}, u32[]{:S(2)}, u32[]{:S(2)}) collective-permute-start(f32[9,768]{1,0:T(8,128)S(1)} %pad_maximum_fusion.9), channel_id=1, source_target_pairs={{0,1},{1,0},{2,3},{3,2},{4,5},{5,4},{6,7},{7,6},{8,9},{9,8},{10,11... | collective-permute-start | bytes 82952 | tf_op jit(solution)/shard_map/ppermute | solution.py:921
  402.9 34.4 %collective-permute-start.27 = (bf16[4,120,768]{2,1,0:T(8,128)(2,1)S(1)}, bf16[4,120,768]{2,1,0:T(8,128)(2,1)S(1)}, u32[]{:S(2)}, u32[]{:S(2)}) collective-permute-start(bf16[4,120,768]{2,1,0:T(8,128)(2,1)S(1)} %pad_maximum_fusion.2.near), channel_id=1, source_target_pairs={{0,4},{4,0},{8,12},{12,8},{16,20},{20,16},{24,28},{28,24},{1,5},{5... | collective-permute-start | bytes 2211848 | tf_op jit(solution)/shard_map/ppermute | solution.py:921
  408.6 12.4 %collective-permute-start.17 = (bf16[2,48,768]{2,1,0:T(8,128)(2,1)S(1)}, bf16[2,48,768]{2,1,0:T(8,128)(2,1)S(1)}, u32[]{:S(2)}, u32[]{:S(2)}) collective-permute-start(bf16[2,48,768]{2,1,0:T(8,128)(2,1)S(1)} %pad_maximum_fusion.8), channel_id=1, source_target_pairs={{0,8},{4,12},{8,0},{12,4},{16,24},{20,28},{24,16},{28,20},{1,9},{5... | collective-permute-start | bytes 442376 | tf_op jit(solution)/shard_map/ppermute | solution.py:921
  409.5 31.8 %all-to-all-start.9 = ((bf16[8,24,768]{2,1,0:T(8,128)(2,1)}), bf16[8,24,768]{2,1,0:T(8,128)(2,1)S(1)}, u32[]{:S(2)}, u32[]{:S(2)}) async-start(bf16[8,24,768]{2,1,0:T(8,128)(2,1)} %broadcast_in_dim.23), calls=%async_computation.9 | async-start | bytes 589824 | tf_op jit(solution)/shard_map/all_to_all | solution.py:929
  421.0 20.3 %collective-permute-start.18 = (bf16[4,48,768]{2,1,0:T(8,128)(2,1)S(1)}, bf16[4,48,768]{2,1,0:T(8,128)(2,1)S(1)}, u32[]{:S(2)}, u32[]{:S(2)}) collective-permute-start(bf16[4,48,768]{2,1,0:T(8,128)(2,1)S(1)} %pad_maximum_fusion.6.near), channel_id=1, source_target_pairs={{0,4},{4,0},{8,12},{12,8},{16,20},{20,16},{24,28},{28,24},{1,5},{5... | collective-permute-start | bytes 884744 | tf_op jit(solution)/shard_map/ppermute | solution.py:921
  (67 other events, 530.4 us)
